TPU v7x, 128 devices: a whole 4x4x4 slice. The times are simulated.
128 devices in a mesh: dom: 8 (over z, core), wide: 16 (over x, y).
Axes of the slice: x: 4, y: 4, z: 4, core: 2. Of those that a mesh axis runs over, the one named last changes fastest.
Arguments:
- embeddings: float32 [16384, 1024], P(('dom', 'wide')), may hold values from -1 to 3
- domain_ids: int32 [16384, 1], P(('dom', 'wide')), may hold values from 0 to 7; in each aligned block of 128 rows (0 to 127, 128 to 255, ...) at most 32 rows name the same one
- order: int32 [128, 128], P(('dom', 'wide')), may hold values from 0 to 127, each once within a row
Outputs:
- whitened_rows: float32 [16384, 1024], P(('dom', 'wide'))
Inputs may be any that keep to these rules, and one draw needn't show every extreme that they name: `domain_ids`: among the rows of one device at most 32 name one domain; every domain is named by some row. Each row of order is a permutation.
All inputs are finite; a program needn't handle non-finite values.
Results may differ from a plain program's by a relative error of at most 0.0003.
Values sent between devices are 32-bit elements; how exact they have to be, the bound alone decides.
No kernel may reach another device: no remote copies, remote signals or barrier semaphores. Data moves between devices by JAX's collectives and lax.ppermute only.
A program may use at most 64 MiB of HBM per device.

v0:
```python
import functools

import jax
import jax.numpy as jnp
from jax import lax
from jax.experimental import pallas as pl
from jax.experimental.pallas import tpu as pltpu
from jax.sharding import PartitionSpec as P


RIDGE = 0.1
SHIFT = 1.0
EMPTY = 1e30
B = 128
AXES = ("dom", "wide")


def coords(n):
    d, w = divmod(n, 16)
    return [w // 4, w % 4, d // 2, d % 2]


def number(c):
    x, y, z, core = c
    return (z * 2 + core) * 16 + x * 4 + y


CARRIED = ((4, 2, 1, 7), (3, 5, 6, 0))


def toward(n, turn):
    c = coords(n)
    mask = CARRIED[c[3]][turn]
    for axis, bit in ((0, 4), (1, 2), (2, 1)):
        if mask & bit:
            c[axis] = 3 - c[axis]
    return number(c)


def partner(n, axis):
    c = coords(n)
    c[axis] ^= 1
    return number(c)


def permute(x, to):
    return lax.ppermute(x, AXES, [(n, to(n)) for n in range(128)])


def iota(shape, axis):
    return lax.broadcasted_iota(jnp.int32, shape, axis)


def split(x):
    high = x.astype(jnp.bfloat16)
    rest = x - high.astype(jnp.float32)
    middle = rest.astype(jnp.bfloat16)
    low = (rest - middle.astype(jnp.float32)).astype(jnp.bfloat16)
    return high, middle, low


def left(x):
    h, m, l = split(x)
    return jnp.concatenate([l, m, h, m, h, h], axis=1)


def right(x):
    h, m, l = split(x)
    return jnp.concatenate([h, m, l, h, m, h], axis=1)


def product(a, b):
    return lax.dot_general(a, b, (((1,), (1,)), ((), ())), preferred_element_type=jnp.float32)


def plain(a, b):
    return lax.dot_general(a, b, (((1,), (0,)), ((), ())), preferred_element_type=jnp.float32)


def pick(place, x):
    h, m, l = split(x)
    p = place.astype(jnp.bfloat16)
    return plain(jnp.concatenate([p, p, p], axis=1), jnp.concatenate([l, m, h], axis=0))


def pack_kernel(where_ref, small_ref, ids2_ref, x_ref, x2_ref, *refs):
    out_refs, sel_ref = refs[:4], refs[4]
    rows = x_ref.shape[0]
    core, home = where_ref[0], where_ref[1]
    earlier = jnp.where(iota((rows, rows), 0) < iota((rows, rows), 1), 1.0, 0.0).astype(jnp.bfloat16)

    def group_and_rank(ids):
        turned = ids ^ home
        group = jnp.zeros_like(turned)
        for place, mask in enumerate(CARRIED[0] + CARRIED[1]):
            group = jnp.where(turned == mask, place, group)
        group = group ^ (4 * core)
        group = jnp.broadcast_to(group.astype(jnp.float32), (8, rows))
        onehot = jnp.where(group == iota((8, rows), 0).astype(jnp.float32), 1.0, 0.0)
        counted = plain(onehot.astype(jnp.bfloat16), earlier)
        return group[0:1, :], jnp.sum(counted * onehot, axis=0, keepdims=True)

    group, rank = group_and_rank(small_ref[0:1, :])
    group2, rank2 = group_and_rank(ids2_ref[...])
    slot = jnp.concatenate([group * 64.0 + rank, group2 * 64.0 + 32.0 + rank2], axis=1)
    place = jnp.where(slot == iota((256, 2 * rows), 0).astype(jnp.float32), 1.0, 0.0)
    used = jnp.sum(place, axis=1, keepdims=True)
    packed = jnp.where(used > 0.5, pick(place, jnp.concatenate([x_ref[...], x2_ref[...]], axis=0)), EMPTY)
    for g in range(4):
        out_refs[g][...] = packed[g * 64 : (g + 1) * 64]
    home_slot = jnp.broadcast_to(group * 32.0 + rank, (rows, rows))
    want = jnp.broadcast_to(small_ref[1:2, :].astype(jnp.float32), (rows, rows)).T
    picked = jnp.where(want == iota((rows, rows), 1).astype(jnp.float32), home_slot, 0.0)
    sel_ref[...] = jnp.broadcast_to(jnp.sum(picked, axis=1, keepdims=True), (rows, rows))


CHUNKS = ((0, 2), (2, 8))
PLACE_IN = [{p: n for n, p in enumerate((i, k) for k in range(*cols) for i in range(k, 8))} for cols in CHUNKS]
STAT = len(PLACE_IN[0]) * B
HALVES = ((STAT + 16) // 2, len(PLACE_IN[1]) * B // 2)
CUTS = ((0, 648, 968), (0, 896, 1344))


def gram_kernel(chunk, core_ref, *refs):
    rows_refs, (mine_ref, other_ref), (xs, xl, flat) = refs[:4], refs[4:6], refs[6:]
    for g in range(4):
        x = rows_refs[g][...]
        live = x[:, 0:1] < 1e29
        xs[g * 64 : (g + 1) * 64, :] = jnp.where(live, x - SHIFT, 0.0)
    first, end = CHUNKS[chunk]
    if chunk == 0:
        total = jnp.sum(xs[...], axis=0, keepdims=True)
        flat[STAT : STAT + 8, :] = jnp.concatenate([total[:, j * B : (j + 1) * B] for j in range(8)], axis=0)
        live = [jnp.where(ref[:, 0:B] < 1e29, 1.0, 0.0) for ref in rows_refs]
        count = jnp.sum(jnp.concatenate(live, axis=0), axis=0, keepdims=True)
        flat[STAT + 8 : STAT + 16, :] = jnp.broadcast_to(count, (8, B))
    xl[first * B :, :] = left(xs[:, first * B :].T)
    for k in range(first, end, 2):
        h, m, l = split(xs[:, k * B : (k + 2) * B])
        two = plain(xl[k * B :, :], jnp.concatenate([h, m, l, h, m, h], axis=0))
        for c in range(2):
            n = PLACE_IN[chunk][k + c, k + c] * B
            flat[n : n + (8 - k - c) * B, :] = two[c * B :, c * B : (c + 1) * B]
    half = HALVES[chunk]
    for ref, which in ((mine_ref, core_ref[0]), (other_ref, 1 - core_ref[0])):
        ref[...] = flat[pl.ds(pl.multiple_of(which * half, 8), half), :]


def row_of(x, j):
    return jnp.broadcast_to(x[j : j + 1, :], x.shape)


def col_of(x, j):
    return jnp.broadcast_to(x[:, j : j + 1], x.shape)


def inverse_factor(block, one, out_ref, between):
    sub = iota((8, B), 0)
    lane = iota((8, B), 1)
    groups = B // 8
    s = [block(g) for g in range(groups)]
    t = [jnp.where(lane == sub + 8 * g, 1.0, 0.0) for g in range(groups)]

    def eliminate(e0, e1, c, ahead, rows):
        v = jnp.zeros((8, B), jnp.float32)
        invs = []
        for j in range(8):
            top = {k: row_of(c[k], j) for k in range(j, 8)}
            inv = 1.0 / top[j]
            invs.append(inv)
            here = sub == j
            b0, b1 = row_of(e0, j), row_of(e1, j)
            m = jnp.where(here, 0.0, c[j] * inv)
            for k in range(j + 1, 8):
                c[k] = c[k] - m * top[k]
            v = jnp.where(here, b1 * lax.rsqrt(top[j]), v)
            e0 = e0 - m * b0
            e1 = e1 - m * b1
            if rows is not None:
                f0, f1, d = rows
                n = d[j] * inv
                f0, f1 = f0 - n * b0, f1 - n * b1
                for k in range(j + 1, 8):
                    d[k] = d[k] - n * top[k]
                for k in range(8):
                    r = row_of(ahead[k], j)
                    ahead[k] = ahead[k] - m * r
                    d[8 + k] = d[8 + k] - n * r
                rows = f0, f1, d
        scale = invs[7]
        for j in range(7):
            scale = jnp.where(sub == j, invs[j], scale)
        return v, e0 * scale, e1 * scale, rows

    def spread(x, first, count):
        return [col_of(x, first + j) * one for j in range(count)]

    def update(h, base, w0, w1):
        cols = [col_of(s[h], base + r) for r in range(8)]
        for r in range(8):
            s[h] = s[h] - cols[r] * w0[r]
            t[h] = t[h] - cols[r] * w1[r]

    for g in range(0, groups, 2):
        base = 8 * g
        near = range(g + 2, min(g + 4, groups))
        far = range(g + 4, groups)
        c = spread(s[g], base, 16)
        d = spread(s[g + 1], base, 16)
        v, p0, p1, (f0, f1, d) = eliminate(s[g], t[g], c[:8], c[8:], (s[g + 1], t[g + 1], d))
        out_ref[base : base + 8, :] = v
        if near:
            w0 = [row_of(p0, r) for r in range(8)]
            w1 = [row_of(p1, r) for r in range(8)]
        if far:
            below = jnp.concatenate([s[h] for h in far], axis=0)
            below = jnp.where(iota(below.shape, 1) >= base, below, 0.0)
            below = jnp.where(iota(below.shape, 1) < base + 16, below, 0.0)
        for h in near:
            update(h, base, w0, w1)
        between[g]()
        v, q0, q1, _ = eliminate(f0, f1, d[8:], None, None)
        out_ref[base + 8 : base + 16, :] = v
        if near:
            w0 = [row_of(q0, r) for r in range(8)]
            w1 = [row_of(q1, r) for r in range(8)]
            for h in near:
                update(h, base + 8, w0, w1)
        if far:
            fix = [col_of(p0, base + 8 + r) for r in range(8)]
            for r in range(8):
                p0 = p0 - fix[r] * w0[r]
                p1 = p1 - fix[r] * w1[r]
            parts = [jnp.concatenate([p0, p1], axis=1), jnp.concatenate([q0, q1], axis=1)]
            zero = jnp.zeros((8, 2 * B), jnp.float32)
            w = jnp.concatenate([parts[i - g] if g <= i < g + 2 else zero for i in range(groups)], axis=0)
            h, m, l = split(w)
            change = lax.dot_general(
                left(below), jnp.concatenate([h, m, l, h, m, h], axis=0), (((1,), (0,)), ((), ())), preferred_element_type=jnp.float32
            )
            for i, n in enumerate(far):
                s[n] = s[n] - change[8 * i : 8 * i + 8, :B]
                t[n] = t[n] - change[8 * i : 8 * i + 8, B:]
        between[g + 1]()


def gather_chunk(chunk, core, refs, flat):
    for which, ref in enumerate(refs):
        start = (which // 2 ^ core) * HALVES[chunk] + CUTS[chunk][which % 2]
        flat[pl.ds(pl.multiple_of(start, 8), ref.shape[0]), :] = ref[...]


def make_covariance(chunk, flat, mean, scale):
    mean_t = jnp.concatenate([mean, jnp.zeros((B - 8, B), jnp.float32)], axis=0).T
    eye = jnp.where(iota((B, B), 0) == iota((B, B), 1), RIDGE, 0.0)
    scale = jnp.broadcast_to(scale[0:1, :], (B, B))
    for (i, k), n in PLACE_IN[chunk].items():
        block = flat[n * B : (n + 1) * B, :] * scale
        block = block - jnp.broadcast_to(mean_t[:, i : i + 1], (B, B)) * mean[k : k + 1, :]
        flat[n * B : (n + 1) * B, :] = block + eye if i == k else block


def center_rows(rows_refs, mean, k):
    out = []
    for ref in rows_refs:
        live = ref[:, 0:1] < 1e29
        out.append(jnp.where(live, ref[:, k * B : (k + 1) * B] - SHIFT - mean[k : k + 1, :], 0.0))
    return jnp.concatenate(out, axis=0)


def leaf(block, ones, inv, work):
    slots = [[] for _ in range(16)]
    for i, piece in enumerate(work):
        slots[i * 16 // len(work)].append(piece)

    def run(pieces):
        for piece in pieces:
            piece()

    inverse_factor(lambda g: block[8 * g : 8 * g + 8, :], ones[...], inv, [functools.partial(run, p) for p in slots])


def in_a_region(scalar):
    return pl.when(scalar >= 0)


def first_kernel(core_ref, *refs):
    parts_refs, rows_refs, (stat_ref, col0_ref, col1_ref, inv_ref, z_ref, x_ref) = refs[:4], refs[4:8], refs[8:14]
    flat, ones, inv, inv_r, diagonal, first_r, x0, z_l = refs[14:]
    core = core_ref[0]
    gather_chunk(0, core, parts_refs, flat)
    scale = 1.0 / flat[STAT + 8 : STAT + 16, :]
    mean = flat[STAT : STAT + 8, :] * scale
    stat_ref[0:8, :] = mean
    stat_ref[8:16, :] = scale
    make_covariance(0, flat, mean, scale)
    ones[...] = jnp.ones((8, B), jnp.float32)

    @in_a_region(core)
    def _():
        def center(k, ref):
            ref[...] = center_rows(rows_refs, stat_ref[...], k)

        leaf(flat[0:B], ones, inv, [lambda: center(0, x0), lambda: center(1, x_ref)])
        inv_r[...] = right(inv[...])
        below = product(left(flat[B : 2 * B, :]), inv_r[...])
        first_r[...] = right(below)
        diagonal[...] = flat[8 * B : 9 * B, :] - product(left(below), first_r[...])

    @in_a_region(core)
    def _():
        def solve(j):
            p = product(left(flat[(2 + j) * B : (5 + j) * B, :]), inv_r[...])
            col0_ref[j * B : (j + 3) * B, :] = p

        def apply(j):
            change = product(left(col0_ref[j * B : (j + 3) * B, :]), first_r[...])
            col1_ref[j * B : (j + 3) * B, :] = flat[(9 + j) * B : (12 + j) * B, :] - change

        def whiten():
            z = product(left(x0[...]), inv_r[...])
            z_ref[...] = z
            z_l[...] = left(z)

        def down():
            x_ref[...] = x_ref[...] - product(z_l[...], first_r[...])

        work = [lambda: solve(0), lambda: solve(3), whiten, lambda: apply(0), lambda: apply(3), down]
        leaf(diagonal[...], ones, inv_ref, work)


def second_kernel(core_ref, *refs):
    parts_refs, (stat_ref, col0_ref, col1_ref, inv1_ref, z0_ref, x1_ref), rows_refs, out_refs = refs[:4], refs[4:10], refs[10:14], refs[14:18]
    flat, ones, inv, inv_r, diagonal, panel, x, z_l, rows_l, rows_r, white = refs[18:]
    core = core_ref[0]
    at = PLACE_IN[1]
    mean = stat_ref[0:8, :]
    gather_chunk(1, core, parts_refs, flat)
    make_covariance(1, flat, mean, stat_ref[8:16, :])
    ones[...] = jnp.ones((8, B), jnp.float32)
    inv_r[...] = right(inv1_ref[...])
    second = product(left(col1_ref[0:B, :]), inv_r[...])
    panel[2 * B : 3 * B, :] = second
    both_l = jnp.concatenate([left(col0_ref[0:B, :]), left(second)], axis=1)
    both_r = jnp.concatenate([right(col0_ref[0:B, :]), right(second)], axis=1)
    diagonal[...] = flat[0:B, :] - product(both_l, both_r)

    def start_of(k):
        row = jnp.int32(0)
        for j in range(3, 8):
            row = jnp.where(k == j, at[j, j] * B, row)
        return pl.multiple_of(row, B)

    def step(k, low):
        both = low == 2
        width = 12 * B if both else 6 * B

        def solve(lo, hi):
            if both:
                column = col1_ref[(1 + lo) * B : (1 + hi) * B, :]
                panel[(3 + lo) * B : (3 + hi) * B, :] = product(left(column), inv_r[...])
            else:
                size = (hi - lo) * B
                column = flat[pl.ds(start_of(k - 1) + (2 + lo) * B, size), :]
                panel[pl.ds(pl.multiple_of((k + 1 + lo) * B, B), size), :] = product(left(column), inv_r[...])

        def whiten():
            z = product(left(x1_ref[...] if both else x[k - 1]), inv_r[...])
            white[k - 1] = z
            if both:
                white[0] = z0_ref[...]
                z_l[:, : 6 * B] = left(z0_ref[...])
            z_l[:, width - 6 * B : width] = left(z)

        def center(j):
            x[j] = center_rows(rows_refs, stat_ref[...], j)

        def parts(lo, hi):
            if both:
                old = col0_ref[(lo - 2) * B : (hi - 2) * B, :]
                rows_l[lo * B : hi * B, : 6 * B] = left(old)
                rows_r[lo * B : hi * B, : 6 * B] = right(old)
            new = panel[lo * B : hi * B, :]
            rows_l[lo * B : hi * B, width - 6 * B : width] = left(new)
            rows_r[lo * B : hi * B, width - 6 * B : width] = right(new)

        def down(j):
            hi = min(j + 2, 8)
            change = product(z_l[:, :width], rows_r[j * B : hi * B, :width])
            for i in range(j, hi):
                x[i] = x[i] - change[:, (i - j) * B : (i - j + 1) * B]

        def update(j, lo, hi):
            top = min(j + 2, 8)
            change = product(rows_l[lo * B : hi * B, :width], rows_r[j * B : top * B, :width])
            for c in range(j, top):
                first = max(lo, c)
                n, size = at[first, c] * B, (hi - first) * B
                flat[n : n + size, :] = flat[n : n + size, :] - change[(first - lo) * B :, (c - j) * B : (c - j + 1) * B]

        def spans(lo, hi):
            return [(i, min(i + 3, hi)) for i in range(lo, hi, 3)]

        work = [functools.partial(solve, *span) for span in spans(0, 7 - low)]
        work += [whiten]
        work += [functools.partial(parts, *span) for span in spans(low, 8)]
        if both:
            work += [functools.partial(center, j) for j in range(2, 8)]
        columns = range(low, 8, 2)
        work += [functools.partial(update, j, *span) for j in columns for span in spans(j, 8)]
        work += [functools.partial(down, j) for j in columns]
        leaf(diagonal[...], ones, inv, work)
        inv_r[...] = right(inv[...])
        below = product(left(flat[pl.ds(start_of(k) + B, B), :]), inv_r[...])
        panel[pl.ds(pl.multiple_of((k + 1) * B, B), B), :] = below
        diagonal[...] = flat[pl.ds(start_of(jnp.minimum(k + 1, 7)), B), :] - product(left(below), right(below))

    in_a_region(core)(lambda: step(2, 2))
    pl.loop(3, 8)(lambda k: step(k, 3))
    white[7] = product(left(x[7]), inv_r[...])
    for k in range(8):
        for g in range(4):
            out_refs[g][:, k * B : (k + 1) * B] = white[k, g * 64 : (g + 1) * 64, :]


def unpack_kernel(sel_ref, *refs):
    own_refs, other_refs, out_ref = refs[:4], refs[4:8], refs[8]
    sel = sel_ref[...]
    lane = iota((B, 256), 1).astype(jnp.float32)
    place = jnp.where(jnp.concatenate([sel, sel], axis=1) == lane, 1.0, 0.0)
    out_ref[...] = pick(place, jnp.concatenate([r[:32, :] for r in own_refs] + [r[32:, :] for r in other_refs], axis=0))


VMEM = pl.BlockSpec(memory_space=pltpu.VMEM)
SMEM = pl.BlockSpec(memory_space=pltpu.SMEM)


def f32(*shape):
    return jax.ShapeDtypeStruct(shape, jnp.float32)


def call(kernel, outs, args, scratch=(), mib=24, scalars=1, flops=1000000):
    return pl.pallas_call(
        kernel,
        out_shape=outs,
        in_specs=[SMEM] * scalars + [VMEM] * (len(args) - scalars),
        out_specs=jax.tree.map(lambda _: VMEM, outs),
        scratch_shapes=scratch,
        cost_estimate=pl.CostEstimate(flops=flops, bytes_accessed=4000000, transcendentals=0),
        compiler_params=pltpu.CompilerParams(vmem_limit_bytes=mib << 20),
    )(*args)


def whiten(embeddings, domain_ids, order):
    d, w = lax.axis_index("dom"), lax.axis_index("wide")
    core = (d % 2).reshape(1).astype(jnp.int32)
    home = ((w // 8) * 4 + (w % 4) // 2 * 2 + d // 4).reshape(1).astype(jnp.int32)

    def swap(x):
        return permute(x, lambda n: partner(n, 3))

    def exchange(arrays):
        return [permute(x, lambda n, turn=turn: toward(n, turn)) for turn, x in enumerate(arrays)]

    ids = domain_ids.reshape(1, B)
    where = jnp.concatenate([core, home])
    *packed, sel = call(
        pack_kernel,
        [f32(64, 1024)] * 4 + [f32(B, B)],
        (where, jnp.concatenate([ids, order]), swap(ids), embeddings, swap(embeddings)),
        mib=12,
    )
    rows = exchange(packed)

    def scratch(*shapes, dtype=jnp.float32):
        return [pltpu.VMEM(shape, dtype) for shape in shapes]

    def wide(*shapes):
        return scratch(*shapes, dtype=jnp.bfloat16)

    def gram(chunk):
        half = HALVES[chunk]
        return call(
            functools.partial(gram_kernel, chunk),
            [f32(half, B)] * 2,
            (core, *rows),
            scratch((256, 1024)) + wide((1024, 1536)) + scratch((2 * half, B)),
        )

    def across(x, turn, i):
        return permute(x, lambda n: partner(n, (turn + (2 if i else coords(n)[3])) % 3))

    grams = [gram(chunk) for chunk in range(2)]
    sums = []
    for chunk, (mine, other) in enumerate(grams):
        other = swap(other)
        sums.append([mine[lo:hi] + other[lo:hi] for lo, hi in zip(CUTS[chunk], CUTS[chunk][1:])])

    def doubled(x, turn, i):
        partners = across(x, turn, i)
        return x + partners

    for turn in range(3):
        sums = [[doubled(x, turn, i) for i, x in enumerate(parts)] for parts in sums]
    sums = [parts + [swap(x) for x in parts] for parts in sums]
    tile, tall = (B, B), (6 * B, B)
    state = call(
        first_kernel,
        [f32(16, B), f32(*tall), f32(*tall), f32(*tile), f32(256, B), f32(256, B)],
        (core, *sums[0], *rows),
        scratch((STAT + 16, B), (8, B), tile) + wide((B, 6 * B)) + scratch(tile) + wide((B, 6 * B)) + scratch((256, B)) + wide((256, 6 * B)),
        flops=6000000000,
    )
    white = call(
        second_kernel,
        [f32(64, 1024)] * 4,
        (core, *sums[1], *state, *rows),
        scratch((2 * HALVES[1] + 8 * B, B), (8, B), tile)
        + wide((B, 6 * B))
        + scratch(tile, (14 * B, B), (8, 256, B))
        + wide((256, 12 * B), (8 * B, 12 * B), (8 * B, 12 * B))
        + scratch((8, 256, B)),
        flops=20000000000,
    )
    white = exchange(white)
    return call(unpack_kernel, f32(B, 1024), (sel, *white, *[swap(x) for x in white]), mib=12, scalars=0)


def solution(mesh):
    placed = (P(AXES, None), P(AXES, None), P(AXES, None))
    return jax.shard_map(whiten, mesh=mesh, in_specs=placed, out_specs=P(AXES, None), check_vma=False)
```

profile of v0, /device:TPU:1, one launch (start us, length us, event | category | flops | bytes accessed | tf_op | source)
XLA Modules:
  0.0 135.6 jit_solution(8491693384126102368)
XLA Ops:
  0.0 1.4 %collective-permute-start.1 = (f32[128,1024]{1,0:T(8,128)}, f32[128,1024]{1,0:T(8,128)S(1)}, u32[]{:S(2)}, u32[]{:S(2)}) collective-permute-start(f32[128,1024]{1,0:T(8,128)} %x_ref.1), channel_id=1, source_target_pairs={{0,16},{1,17},{2,18},{3,19},{4,20},{5,21},{6,22},{7,23},{8,24},{9,... | collective-permute-start | bytes 1572872 | tf_op jit(solution)/shard_map/ppermute | solution.py:47
  4.2 1.3 shard_map.37
  5.4 6.4 %collective-permute-start.2 = (f32[64,1024]{1,0:T(8,128)S(1)}, f32[64,1024]{1,0:T(8,128)S(1)}, u32[]{:S(2)}, u32[]{:S(2)}) collective-permute-start(f32[64,1024]{1,0:T(8,128)S(1)} %get-tuple-element.25), channel_id=1, source_target_pairs={{0,12},{1,13},{2,14},{3,15},{4,8},{5,9},{6,10},{7,11},{8,4},{9,5},... | collective-permute-start | bytes 786440 | tf_op jit(solution)/shard_map/ppermute | solution.py:47
  13.0 1.4 %collective-permute-start.4 = (f32[64,1024]{1,0:T(8,128)S(1)}, f32[64,1024]{1,0:T(8,128)S(1)}, u32[]{:S(2)}, u32[]{:S(2)}) collective-permute-start(f32[64,1024]{1,0:T(8,128)S(1)} %get-tuple-element.27), channel_id=1, source_target_pairs={{0,96},{1,97},{2,98},{3,99},{4,100},{5,101},{6,102},{7,103},{8,104... | collective-permute-start | bytes 786440 | tf_op jit(solution)/shard_map/ppermute | solution.py:47
  15.0 2.8 %collective-permute-done.2.refs_0_.refs_4_.refs_10_ = f32[64,1024]{1,0:T(8,128)S(1)} collective-permute-done((f32[64,1024]{1,0:T(8,128)S(1)}, f32[64,1024]{1,0:T(8,128)S(1)}, u32[]{:S(2)}, u32[]{:S(2)}) %collective-permute-start.2) | collective-permute-done | bytes 262176 | tf_op jit(solution)/shard_map/ppermute | solution.py:47
  17.8 2.6 %collective-permute-done.3.refs_1_.refs_5_.refs_11_ = f32[64,1024]{1,0:T(8,128)S(1)} collective-permute-done((f32[64,1024]{1,0:T(8,128)S(1)}, f32[64,1024]{1,0:T(8,128)S(1)}, u32[]{:S(2)}, u32[]{:S(2)}) %collective-permute-start.3) | collective-permute-done | bytes 262176 | tf_op jit(solution)/shard_map/ppermute | solution.py:47
  21.5 1.8 %shard_map.38 = (f32[1344,128]{1,0:T(8,128)S(1)}, f32[1344,128]{1,0:T(8,128)S(1)}) custom-call(s32[1]{0:T(128)} %bitcast.core_ref, f32[64,1024]{1,0:T(8,128)S(1)} %collective-permute-done.2.refs_0_.refs_4_.refs_10_, f32[64,1024]{1,0:T(8,128)S(1)} %collective-permute-done.3.refs_1_.refs_5_.refs_11_, ...), custom_call_target="tpu_custom_call" | custom-call | flops 1000000 | bytes 4000000 | tf_op jit(solution)/shard_map/pallas_call | solution.py:443
  23.3 8.1 %collective-permute-start.6 = (f32[1344,128]{1,0:T(8,128)S(1)}, f32[1344,128]{1,0:T(8,128)S(1)}, u32[]{:S(2)}, u32[]{:S(2)}) collective-permute-start(f32[1344,128]{1,0:T(8,128)S(1)} %get-tuple-element.30), channel_id=1, source_target_pairs={{0,16},{1,17},{2,18},{3,19},{4,20},{5,21},{6,22},{7,23},{8,24},{9,... | collective-permute-start | bytes 2064392 | tf_op jit(solution)/shard_map/ppermute | solution.py:47
  34.9 9.6 %collective-permute-done.16 = f32[648,128]{1,0:T(8,128)S(1)} collective-permute-done((f32[648,128]{1,0:T(8,128)S(1)}, f32[648,128]{1,0:T(8,128)S(1)}, u32[]{:S(2)}, u32[]{:S(2)}) %collective-permute-start.16) | collective-permute-done | bytes 331808 | tf_op jit(solution)/shard_map/ppermute | solution.py:47
  44.7 1.5 %collective-permute-start.8 = (f32[896,128]{1,0:T(8,128)S(1)}, f32[896,128]{1,0:T(8,128)S(1)}, u32[]{:S(2)}, u32[]{:S(2)}) collective-permute-start(f32[896,128]{1,0:T(8,128)S(1)} %add.69), channel_id=1, source_target_pairs={{0,1},{1,0},{2,3},{3,2},{4,5},{5,4},{6,7},{7,6},{8,9},{9,8},{10,11... | collective-permute-start | bytes 1376264 | tf_op jit(solution)/shard_map/ppermute | solution.py:47
  46.3 4.5 %collective-permute-done.17 = f32[648,128]{1,0:T(8,128)S(1)} collective-permute-done((f32[648,128]{1,0:T(8,128)S(1)}, f32[648,128]{1,0:T(8,128)S(1)}, u32[]{:S(2)}, u32[]{:S(2)}) %collective-permute-start.17) | collective-permute-done | bytes 331808 | tf_op jit(solution)/shard_map/ppermute | solution.py:47
  51.1 16.3 %collective-permute-done.19 = f32[320,128]{1,0:T(8,128)S(1)} collective-permute-done((f32[320,128]{1,0:T(8,128)S(1)}, f32[320,128]{1,0:T(8,128)S(1)}, u32[]{:S(2)}, u32[]{:S(2)}) %collective-permute-start.19) | collective-permute-done | bytes 163872 | tf_op jit(solution)/shard_map/ppermute | solution.py:47
  67.6 1.5 %collective-permute-start.11 = (f32[448,128]{1,0:T(8,128)S(1)}, f32[448,128]{1,0:T(8,128)S(1)}, u32[]{:S(2)}, u32[]{:S(2)}) collective-permute-start(f32[448,128]{1,0:T(8,128)S(1)} %add.73), channel_id=1, source_target_pairs={{0,4},{1,5},{2,6},{3,7},{4,0},{5,1},{6,2},{7,3},{8,12},{9,13},{10,... | collective-permute-start | bytes 688136 | tf_op jit(solution)/shard_map/ppermute | solution.py:47
  69.8 3.8 %collective-permute-done.20 = f32[320,128]{1,0:T(8,128)S(1)} collective-permute-done((f32[320,128]{1,0:T(8,128)S(1)}, f32[320,128]{1,0:T(8,128)S(1)}, u32[]{:S(2)}, u32[]{:S(2)}) %collective-permute-start.20) | collective-permute-done | bytes 163872 | tf_op jit(solution)/shard_map/ppermute | solution.py:47
  73.6 4.8 %collective-permute-done.11 = f32[448,128]{1,0:T(8,128)S(1)} collective-permute-done((f32[448,128]{1,0:T(8,128)S(1)}, f32[448,128]{1,0:T(8,128)S(1)}, u32[]{:S(2)}, u32[]{:S(2)}) %collective-permute-start.11) | collective-permute-done | bytes 229408 | tf_op jit(solution)/shard_map/ppermute | solution.py:47
  78.6 1.7 %collective-permute-start.23 = (f32[320,128]{1,0:T(8,128)S(1)}, f32[320,128]{1,0:T(8,128)S(1)}, u32[]{:S(2)}, u32[]{:S(2)}) collective-permute-start(f32[320,128]{1,0:T(8,128)S(1)} %add.83.refs_1_), channel_id=1, source_target_pairs={{0,16},{1,17},{2,18},{3,19},{4,20},{5,21},{6,22},{7,23},{8,24},{9,... | collective-permute-start | bytes 491528 | tf_op jit(solution)/shard_map/ppermute | solution.py:47
  80.4 4.5 %collective-permute-done.12 = f32[448,128]{1,0:T(8,128)S(1)} collective-permute-done((f32[448,128]{1,0:T(8,128)S(1)}, f32[448,128]{1,0:T(8,128)S(1)}, u32[]{:S(2)}, u32[]{:S(2)}) %collective-permute-start.12) | collective-permute-done | bytes 229408 | tf_op jit(solution)/shard_map/ppermute | solution.py:47
  84.9 1.8 %collective-permute-start.14 = (f32[448,128]{1,0:T(8,128)S(1)}, f32[448,128]{1,0:T(8,128)S(1)}, u32[]{:S(2)}, u32[]{:S(2)}) collective-permute-start(f32[448,128]{1,0:T(8,128)S(1)} %add.75.refs_1_), channel_id=1, source_target_pairs={{0,16},{1,17},{2,18},{3,19},{4,20},{5,21},{6,22},{7,23},{8,24},{9,... | collective-permute-start | bytes 688136 | tf_op jit(solution)/shard_map/ppermute | solution.py:47
  86.9 6.4 %shard_map.40 = (f32[16,128]{1,0:T(8,128)S(1)}, f32[768,128]{1,0:T(8,128)S(1)}, f32[768,128]{1,0:T(8,128)S(1)}, f32[128,128]{1,0:T(8,128)S(1)}, f32[256,128]{1,0:T(8,128)S(1)}, /*index=5*/f32[256,128]{1,0:T(8,128)S(1)}) custom-call(s32[1]{0:T(128)} %bitcast.core_ref, f32[648,128]{1,0:T(8,128)S(1)} %add.79.refs_0_, f32[320,128]{1,0:T(8,128)S(1)} %add.83.refs_1_, ...), custom_call_target="tpu_custom_call" | custom-call | flops 6000000000 | bytes 4000000 | tf_op jit(solution)/shard_map/pallas_call | solution.py:443
  93.3 21.7 %shard_map.41 = (f32[64,1024]{1,0:T(8,128)S(1)}, f32[64,1024]{1,0:T(8,128)S(1)}, f32[64,1024]{1,0:T(8,128)S(1)}, f32[64,1024]{1,0:T(8,128)S(1)}) custom-call(s32[1]{0:T(128)} %bitcast.core_ref, f32[896,128]{1,0:T(8,128)S(1)} %add.71.refs_0_, f32[448,128]{1,0:T(8,128)S(1)} %add.75.refs_1_, f32[896,128]{1,0:T(8,128)S(1)} %collective-permute-done.13.refs_2_, ...), custom_call_target="tpu_custom_call" | custom-call | flops 20000000000 | bytes 4000000 | tf_op jit(solution)/shard_map/pallas_call | solution.py:443
  115.1 4.2 %collective-permute-start.25 = (f32[64,1024]{1,0:T(8,128)S(1)}, f32[64,1024]{1,0:T(8,128)S(1)}, u32[]{:S(2)}, u32[]{:S(2)}) collective-permute-start(f32[64,1024]{1,0:T(8,128)S(1)} %get-tuple-element.40), channel_id=1, source_target_pairs={{0,3},{1,2},{2,1},{3,0},{4,7},{5,6},{6,5},{7,4},{8,11},{9,10},{10,... | collective-permute-start | bytes 786440 | tf_op jit(solution)/shard_map/ppermute | solution.py:47
  119.3 3.0 %collective-permute-start.26 = (f32[64,1024]{1,0:T(8,128)S(1)}, f32[64,1024]{1,0:T(8,128)S(1)}, u32[]{:S(2)}, u32[]{:S(2)}) collective-permute-start(f32[64,1024]{1,0:T(8,128)S(1)} %get-tuple-element.41), channel_id=1, source_target_pairs={{0,96},{1,97},{2,98},{3,99},{4,100},{5,101},{6,102},{7,103},{8,104... | collective-permute-start | bytes 786440 | tf_op jit(solution)/shard_map/ppermute | solution.py:47
  122.9 5.7 %collective-permute-done.24.refs_0_ = f32[64,1024]{1,0:T(8,128)S(1)} collective-permute-done((f32[64,1024]{1,0:T(8,128)S(1)}, f32[64,1024]{1,0:T(8,128)S(1)}, u32[]{:S(2)}, u32[]{:S(2)}) %collective-permute-start.24) | collective-permute-done | bytes 262176 | tf_op jit(solution)/shard_map/ppermute | solution.py:47
  129.2 3.6 %collective-permute-start.30 = (f32[64,1024]{1,0:T(8,128)S(1)}, f32[64,1024]{1,0:T(8,128)S(1)}, u32[]{:S(2)}, u32[]{:S(2)}) collective-permute-start(f32[64,1024]{1,0:T(8,128)S(1)} %collective-permute-done.26.refs_2_), channel_id=1, source_target_pairs={{0,16},{1,17},{2,18},{3,19},{4,20},{5,21},{6,22},{7,23},{8,24},{9,... | collective-permute-start | bytes 786440 | tf_op jit(solution)/shard_map/ppermute | solution.py:47
  (70 shorter events, 14.9 us)
Async XLA Ops:
  5.4 12.4 %collective-permute-start.2 = (f32[64,1024]{1,0:T(8,128)S(1)}, f32[64,1024]{1,0:T(8,128)S(1)}, u32[]{:S(2)}, u32[]{:S(2)}) collective-permute-start(f32[64,1024]{1,0:T(8,128)S(1)} %get-tuple-element.25), channel_id=1, source_target_pairs={{0,12},{1,13},{2,14},{3,15},{4,8},{5,9},{6,10},{7,11},{8,4},{9,5},... | collective-permute-start | bytes 786440 | tf_op jit(solution)/shard_map/ppermute | solution.py:47
  11.8 8.6 %collective-permute-start.3 = (f32[64,1024]{1,0:T(8,128)S(1)}, f32[64,1024]{1,0:T(8,128)S(1)}, u32[]{:S(2)}, u32[]{:S(2)}) collective-permute-start(f32[64,1024]{1,0:T(8,128)S(1)} %get-tuple-element.26), channel_id=1, source_target_pairs={{0,3},{1,2},{2,1},{3,0},{4,7},{5,6},{6,5},{7,4},{8,11},{9,10},{10,... | collective-permute-start | bytes 786440 | tf_op jit(solution)/shard_map/ppermute | solution.py:47
  13.0 8.5 %collective-permute-start.4 = (f32[64,1024]{1,0:T(8,128)S(1)}, f32[64,1024]{1,0:T(8,128)S(1)}, u32[]{:S(2)}, u32[]{:S(2)}) collective-permute-start(f32[64,1024]{1,0:T(8,128)S(1)} %get-tuple-element.27), channel_id=1, source_target_pairs={{0,96},{1,97},{2,98},{3,99},{4,100},{5,101},{6,102},{7,103},{8,104... | collective-permute-start | bytes 786440 | tf_op jit(solution)/shard_map/ppermute | solution.py:47
  14.3 7.2 %collective-permute-start.5 = (f32[64,1024]{1,0:T(8,128)S(1)}, f32[64,1024]{1,0:T(8,128)S(1)}, u32[]{:S(2)}, u32[]{:S(2)}) collective-permute-start(f32[64,1024]{1,0:T(8,128)S(1)} %get-tuple-element.28), channel_id=1, source_target_pairs={{0,111},{1,110},{2,109},{3,108},{4,107},{5,106},{6,105},{7,104},{8... | collective-permute-start | bytes 786440 | tf_op jit(solution)/shard_map/ppermute | solution.py:47
  23.3 9.8 %collective-permute-start.6 = (f32[1344,128]{1,0:T(8,128)S(1)}, f32[1344,128]{1,0:T(8,128)S(1)}, u32[]{:S(2)}, u32[]{:S(2)}) collective-permute-start(f32[1344,128]{1,0:T(8,128)S(1)} %get-tuple-element.30), channel_id=1, source_target_pairs={{0,16},{1,17},{2,18},{3,19},{4,20},{5,21},{6,22},{7,23},{8,24},{9,... | collective-permute-start | bytes 2064392 | tf_op jit(solution)/shard_map/ppermute | solution.py:47
  33.2 11.4 %collective-permute-start.7 = (f32[896,128]{1,0:T(8,128)S(1)}, f32[896,128]{1,0:T(8,128)S(1)}, u32[]{:S(2)}, u32[]{:S(2)}) collective-permute-start(f32[896,128]{1,0:T(8,128)S(1)} %slice_add_fusion), channel_id=1, source_target_pairs={{0,4},{1,5},{2,6},{3,7},{4,0},{5,1},{6,2},{7,3},{8,12},{9,13},{10,... | collective-permute-start | bytes 1376264 | tf_op jit(solution)/shard_map/ppermute | solution.py:47
  34.6 9.9 %collective-permute-start.16 = (f32[648,128]{1,0:T(8,128)S(1)}, f32[648,128]{1,0:T(8,128)S(1)}, u32[]{:S(2)}, u32[]{:S(2)}) collective-permute-start(f32[648,128]{1,0:T(8,128)S(1)} %slice_add_fusion.1), channel_id=1, source_target_pairs={{0,4},{1,5},{2,6},{3,7},{4,0},{5,1},{6,2},{7,3},{8,12},{9,13},{10,... | collective-permute-start | bytes 995336 | tf_op jit(solution)/shard_map/ppermute | solution.py:47
  44.5 6.3 %collective-permute-start.17 = (f32[648,128]{1,0:T(8,128)S(1)}, f32[648,128]{1,0:T(8,128)S(1)}, u32[]{:S(2)}, u32[]{:S(2)}) collective-permute-start(f32[648,128]{1,0:T(8,128)S(1)} %add.77), channel_id=1, source_target_pairs={{0,1},{1,0},{2,3},{3,2},{4,5},{5,4},{6,7},{7,6},{8,9},{9,8},{10,11... | collective-permute-start | bytes 995336 | tf_op jit(solution)/shard_map/ppermute | solution.py:47
  44.7 24.5 %collective-permute-start.8 = (f32[896,128]{1,0:T(8,128)S(1)}, f32[896,128]{1,0:T(8,128)S(1)}, u32[]{:S(2)}, u32[]{:S(2)}) collective-permute-start(f32[896,128]{1,0:T(8,128)S(1)} %add.69), channel_id=1, source_target_pairs={{0,1},{1,0},{2,3},{3,2},{4,5},{5,4},{6,7},{7,6},{8,9},{9,8},{10,11... | collective-permute-start | bytes 1376264 | tf_op jit(solution)/shard_map/ppermute | solution.py:47
  46.2 21.3 %collective-permute-start.10 = (f32[448,128]{1,0:T(8,128)S(1)}, f32[448,128]{1,0:T(8,128)S(1)}, u32[]{:S(2)}, u32[]{:S(2)}) collective-permute-start(f32[448,128]{1,0:T(8,128)S(1)} %slice_add_fusion.2), channel_id=1, source_target_pairs={{0,32},{1,33},{2,34},{3,35},{4,36},{5,37},{6,38},{7,39},{8,40},{9,... | collective-permute-start | bytes 688136 | tf_op jit(solution)/shard_map/ppermute | solution.py:47
  50.9 18.4 %collective-permute-start.18 = (f32[648,128]{1,0:T(8,128)S(1)}, f32[648,128]{1,0:T(8,128)S(1)}, u32[]{:S(2)}, u32[]{:S(2)}) collective-permute-start(f32[648,128]{1,0:T(8,128)S(1)} %add.78), channel_id=1, source_target_pairs={{0,32},{1,33},{2,34},{3,35},{4,36},{5,37},{6,38},{7,39},{8,40},{9,... | collective-permute-start | bytes 995336 | tf_op jit(solution)/shard_map/ppermute | solution.py:47
  51.0 16.4 %collective-permute-start.19 = (f32[320,128]{1,0:T(8,128)S(1)}, f32[320,128]{1,0:T(8,128)S(1)}, u32[]{:S(2)}, u32[]{:S(2)}) collective-permute-start(f32[320,128]{1,0:T(8,128)S(1)} %slice_add_fusion.3), channel_id=1, source_target_pairs={{0,32},{1,33},{2,34},{3,35},{4,36},{5,37},{6,38},{7,39},{8,40},{9,... | collective-permute-start | bytes 491528 | tf_op jit(solution)/shard_map/ppermute | solution.py:47
  67.5 6.0 %collective-permute-start.20 = (f32[320,128]{1,0:T(8,128)S(1)}, f32[320,128]{1,0:T(8,128)S(1)}, u32[]{:S(2)}, u32[]{:S(2)}) collective-permute-start(f32[320,128]{1,0:T(8,128)S(1)} %add.81), channel_id=1, source_target_pairs={{0,4},{1,5},{2,6},{3,7},{4,0},{5,1},{6,2},{7,3},{8,12},{9,13},{10,... | collective-permute-start | bytes 491528 | tf_op jit(solution)/shard_map/ppermute | solution.py:47
  67.6 10.8 %collective-permute-start.11 = (f32[448,128]{1,0:T(8,128)S(1)}, f32[448,128]{1,0:T(8,128)S(1)}, u32[]{:S(2)}, u32[]{:S(2)}) collective-permute-start(f32[448,128]{1,0:T(8,128)S(1)} %add.73), channel_id=1, source_target_pairs={{0,4},{1,5},{2,6},{3,7},{4,0},{5,1},{6,2},{7,3},{8,12},{9,13},{10,... | collective-permute-start | bytes 688136 | tf_op jit(solution)/shard_map/ppermute | solution.py:47
  69.2 17.5 %collective-permute-start.9 = (f32[896,128]{1,0:T(8,128)S(1)}, f32[896,128]{1,0:T(8,128)S(1)}, u32[]{:S(2)}, u32[]{:S(2)}) collective-permute-start(f32[896,128]{1,0:T(8,128)S(1)} %add.70), channel_id=1, source_target_pairs={{0,32},{1,33},{2,34},{3,35},{4,36},{5,37},{6,38},{7,39},{8,40},{9,... | collective-permute-start | bytes 1376264 | tf_op jit(solution)/shard_map/ppermute | solution.py:47
  69.4 17.5 %collective-permute-start.22 = (f32[648,128]{1,0:T(8,128)S(1)}, f32[648,128]{1,0:T(8,128)S(1)}, u32[]{:S(2)}, u32[]{:S(2)}) collective-permute-start(f32[648,128]{1,0:T(8,128)S(1)} %add.79.refs_0_), channel_id=1, source_target_pairs={{0,16},{1,17},{2,18},{3,19},{4,20},{5,21},{6,22},{7,23},{8,24},{9,... | collective-permute-start | bytes 995336 | tf_op jit(solution)/shard_map/ppermute | solution.py:47
  78.5 6.3 %collective-permute-start.12 = (f32[448,128]{1,0:T(8,128)S(1)}, f32[448,128]{1,0:T(8,128)S(1)}, u32[]{:S(2)}, u32[]{:S(2)}) collective-permute-start(f32[448,128]{1,0:T(8,128)S(1)} %add.74), channel_id=1, source_target_pairs={{0,1},{1,0},{2,3},{3,2},{4,5},{5,4},{6,7},{7,6},{8,9},{9,8},{10,11... | collective-permute-start | bytes 688136 | tf_op jit(solution)/shard_map/ppermute | solution.py:47
  78.6 8.2 %collective-permute-start.23 = (f32[320,128]{1,0:T(8,128)S(1)}, f32[320,128]{1,0:T(8,128)S(1)}, u32[]{:S(2)}, u32[]{:S(2)}) collective-permute-start(f32[320,128]{1,0:T(8,128)S(1)} %add.83.refs_1_), channel_id=1, source_target_pairs={{0,16},{1,17},{2,18},{3,19},{4,20},{5,21},{6,22},{7,23},{8,24},{9,... | collective-permute-start | bytes 491528 | tf_op jit(solution)/shard_map/ppermute | solution.py:47
  84.9 8.4 %collective-permute-start.14 = (f32[448,128]{1,0:T(8,128)S(1)}, f32[448,128]{1,0:T(8,128)S(1)}, u32[]{:S(2)}, u32[]{:S(2)}) collective-permute-start(f32[448,128]{1,0:T(8,128)S(1)} %add.75.refs_1_), channel_id=1, source_target_pairs={{0,16},{1,17},{2,18},{3,19},{4,20},{5,21},{6,22},{7,23},{8,24},{9,... | collective-permute-start | bytes 688136 | tf_op jit(solution)/shard_map/ppermute | solution.py:47
  86.7 6.6 %collective-permute-start.13 = (f32[896,128]{1,0:T(8,128)S(1)}, f32[896,128]{1,0:T(8,128)S(1)}, u32[]{:S(2)}, u32[]{:S(2)}) collective-permute-start(f32[896,128]{1,0:T(8,128)S(1)} %add.71.refs_0_), channel_id=1, source_target_pairs={{0,16},{1,17},{2,18},{3,19},{4,20},{5,21},{6,22},{7,23},{8,24},{9,... | collective-permute-start | bytes 1376264 | tf_op jit(solution)/shard_map/ppermute | solution.py:47
  115.0 13.6 %collective-permute-start.24 = (f32[64,1024]{1,0:T(8,128)S(1)}, f32[64,1024]{1,0:T(8,128)S(1)}, u32[]{:S(2)}, u32[]{:S(2)}) collective-permute-start(f32[64,1024]{1,0:T(8,128)S(1)} %get-tuple-element.39), channel_id=1, source_target_pairs={{0,12},{1,13},{2,14},{3,15},{4,8},{5,9},{6,10},{7,11},{8,4},{9,5},... | collective-permute-start | bytes 786440 | tf_op jit(solution)/shard_map/ppermute | solution.py:47
  115.1 13.5 %collective-permute-start.25 = (f32[64,1024]{1,0:T(8,128)S(1)}, f32[64,1024]{1,0:T(8,128)S(1)}, u32[]{:S(2)}, u32[]{:S(2)}) collective-permute-start(f32[64,1024]{1,0:T(8,128)S(1)} %get-tuple-element.40), channel_id=1, source_target_pairs={{0,3},{1,2},{2,1},{3,0},{4,7},{5,6},{6,5},{7,4},{8,11},{9,10},{10,... | collective-permute-start | bytes 786440 | tf_op jit(solution)/shard_map/ppermute | solution.py:47
  119.3 9.9 %collective-permute-start.26 = (f32[64,1024]{1,0:T(8,128)S(1)}, f32[64,1024]{1,0:T(8,128)S(1)}, u32[]{:S(2)}, u32[]{:S(2)}) collective-permute-start(f32[64,1024]{1,0:T(8,128)S(1)} %get-tuple-element.41), channel_id=1, source_target_pairs={{0,96},{1,97},{2,98},{3,99},{4,100},{5,101},{6,102},{7,103},{8,104... | collective-permute-start | bytes 786440 | tf_op jit(solution)/shard_map/ppermute | solution.py:47
  122.3 10.5 %collective-permute-start.27 = (f32[64,1024]{1,0:T(8,128)S(1)}, f32[64,1024]{1,0:T(8,128)S(1)}, u32[]{:S(2)}, u32[]{:S(2)}) collective-permute-start(f32[64,1024]{1,0:T(8,128)S(1)} %get-tuple-element.42), channel_id=1, source_target_pairs={{0,111},{1,110},{2,109},{3,108},{4,107},{5,106},{6,105},{7,104},{8... | collective-permute-start | bytes 786440 | tf_op jit(solution)/shard_map/ppermute | solution.py:47
  (11 other events, 29.6 us)
where the time goes:
time: 136 us
  waiting for transfers between devices  59.3 us (44%)
  starting transfers between devices  40 us (29%)
  Pallas kernels  33.6 us (25%)
  local copies, waits for them, and re-layouts  1.7 us (1%)
    ppermute x32, waiting for transfers between devices, permute(): return lax.ppermute(x, AXES, [(n, to(n)) for n in range(128)])  59.3 us
    ppermute x32, starting transfers between devices, permute(): return lax.ppermute(x, AXES, [(n, to(n)) for n in range(128)])  40 us
    pallas_call x6, Pallas kernels, call(): pl.pallas_call(kernel, out_shape=outs, in_specs=[SMEM] * scalars + [VMEM]...  33.6 us
  transfers between devices with their start and end apart: 32, of which 15 were waited for; matrix products, arithmetic and copies ran while one was open for 1% of the time, Pallas kernels for 6%

commit v1 on v0

--- a/solution.py
+++ b/solution.py
@@ -25,7 +25,7 @@
     return (z * 2 + core) * 16 + x * 4 + y
 
 
-CARRIED = ((4, 2, 1, 7), (3, 5, 6, 0))
+CARRIED = ((7, 0, 4, 2), (3, 5, 6, 1))
 
 
 def toward(n, turn):
@@ -161,36 +161,55 @@
     s = [block(g) for g in range(groups)]
     t = [jnp.where(lane == sub + 8 * g, 1.0, 0.0) for g in range(groups)]
 
-    def eliminate(e0, e1, c, ahead, rows):
+    even = sub % 2 == 0
+
+    def eliminate(e0, e1, c, rows):
         v = jnp.zeros((8, B), jnp.float32)
-        invs = []
-        for j in range(8):
+        straight = crossed = jnp.zeros((8, B), jnp.float32)
+        for j in range(0, 8, 2):
             top = {k: row_of(c[k], j) for k in range(j, 8)}
-            inv = 1.0 / top[j]
-            invs.append(inv)
-            here = sub == j
-            b0, b1 = row_of(e0, j), row_of(e1, j)
-            m = jnp.where(here, 0.0, c[j] * inv)
-            for k in range(j + 1, 8):
-                c[k] = c[k] - m * top[k]
-            v = jnp.where(here, b1 * lax.rsqrt(top[j]), v)
-            e0 = e0 - m * b0
-            e1 = e1 - m * b1
+            low = {k: row_of(c[k], j + 1) for k in range(j + 1, 8)}
+            p, q, r = top[j], top[j + 1], low[j + 1]
+            inv = 1.0 / (p * r - q * q)
+            pair = (sub == j) | (sub == j + 1)
+
+            def multipliers(x, y):
+                return (r * x - q * y) * inv, (p * y - q * x) * inv
+
+            def sides(x):
+                return row_of(x, j), row_of(x, j + 1)
+
+            x, y = jnp.where(pair, 0.0, c[j]), jnp.where(pair, 0.0, c[j + 1])
+            for k in range(j + 2, min(j + 4, 8)):
+                both = x * (r * top[k] - q * low[k]) + y * (p * low[k] - q * top[k])
+                c[k] = c[k] - both * inv
+            m, n = multipliers(x, y)
+            for k in range(j + 4, 8):
+                c[k] = c[k] - m * top[k] - n * low[k]
+            (b0, d0), (b1, d1) = sides(e0), sides(e1)
+            e0 = e0 - m * b0 - n * d0
+            e1 = e1 - m * b1 - n * d1
+            over = q * (1.0 / p)
+            v = jnp.where(sub == j, b1 * lax.rsqrt(p), v)
+            v = jnp.where(sub == j + 1, (d1 - over * b1) * lax.rsqrt(r - over * q), v)
+            straight = jnp.where(pair, jnp.where(even, r, p) * inv, straight)
+            crossed = jnp.where(pair, q * inv, crossed)
             if rows is not None:
                 f0, f1, d = rows
-                n = d[j] * inv
-                f0, f1 = f0 - n * b0, f1 - n * b1
-                for k in range(j + 1, 8):
-                    d[k] = d[k] - n * top[k]
+                m, n = multipliers(d[j], d[j + 1])
+                f0 = f0 - m * b0 - n * d0
+                f1 = f1 - m * b1 - n * d1
+                for k in range(j + 2, 8):
+                    d[k] = d[k] - m * top[k] - n * low[k]
                 for k in range(8):
-                    r = row_of(ahead[k], j)
-                    ahead[k] = ahead[k] - m * r
-                    d[8 + k] = d[8 + k] - n * r
+                    d[8 + k] = d[8 + k] - m * row_of(d[j], k) - n * row_of(d[j + 1], k)
                 rows = f0, f1, d
-        scale = invs[7]
-        for j in range(7):
-            scale = jnp.where(sub == j, invs[j], scale)
-        return v, e0 * scale, e1 * scale, rows
+
+        def scaled(e):
+            other = jnp.where(even, pltpu.roll(e, 7, 0), pltpu.roll(e, 1, 0))
+            return e * straight - other * crossed
+
+        return v, scaled(e0), scaled(e1), rows
 
     def spread(x, first, count):
         return [col_of(x, first + j) * one for j in range(count)]
@@ -205,9 +224,9 @@
         base = 8 * g
         near = range(g + 2, min(g + 4, groups))
         far = range(g + 4, groups)
-        c = spread(s[g], base, 16)
+        c = spread(s[g], base, 8)
         d = spread(s[g + 1], base, 16)
-        v, p0, p1, (f0, f1, d) = eliminate(s[g], t[g], c[:8], c[8:], (s[g + 1], t[g + 1], d))
+        v, p0, p1, (f0, f1, d) = eliminate(s[g], t[g], c, (s[g + 1], t[g + 1], d))
         out_ref[base : base + 8, :] = v
         if near:
             w0 = [row_of(p0, r) for r in range(8)]
@@ -219,7 +238,7 @@
         for h in near:
             update(h, base, w0, w1)
         between[g]()
-        v, q0, q1, _ = eliminate(f0, f1, d[8:], None, None)
+        v, q0, q1, _ = eliminate(f0, f1, d[8:], None)
         out_ref[base + 8 : base + 16, :] = v
         if near:
             w0 = [row_of(q0, r) for r in range(8)]
@@ -280,13 +299,9 @@
     inverse_factor(lambda g: block[8 * g : 8 * g + 8, :], ones[...], inv, [functools.partial(run, p) for p in slots])
 
 
-def in_a_region(scalar):
-    return pl.when(scalar >= 0)
-
-
 def first_kernel(core_ref, *refs):
-    parts_refs, rows_refs, (stat_ref, col0_ref, col1_ref, inv_ref, z_ref, x_ref) = refs[:4], refs[4:8], refs[8:14]
-    flat, ones, inv, inv_r, diagonal, first_r, x0, z_l = refs[14:]
+    parts_refs, rows_refs, (stat_ref, rows_l_ref, rows_r_ref, x_ref, z_ref) = refs[:4], refs[4:8], refs[8:13]
+    flat, ones, inv, inv_r, diagonal, first_r, col0, col1, x, z_l = refs[13:]
     core = core_ref[0]
     gather_chunk(0, core, parts_refs, flat)
     scale = 1.0 / flat[STAT + 8 : STAT + 16, :]
@@ -296,54 +311,65 @@
     make_covariance(0, flat, mean, scale)
     ones[...] = jnp.ones((8, B), jnp.float32)
 
-    @in_a_region(core)
-    def _():
-        def center(k, ref):
-            ref[...] = center_rows(rows_refs, stat_ref[...], k)
-
-        leaf(flat[0:B], ones, inv, [lambda: center(0, x0), lambda: center(1, x_ref)])
-        inv_r[...] = right(inv[...])
-        below = product(left(flat[B : 2 * B, :]), inv_r[...])
-        first_r[...] = right(below)
-        diagonal[...] = flat[8 * B : 9 * B, :] - product(left(below), first_r[...])
-
-    @in_a_region(core)
-    def _():
-        def solve(j):
-            p = product(left(flat[(2 + j) * B : (5 + j) * B, :]), inv_r[...])
-            col0_ref[j * B : (j + 3) * B, :] = p
-
-        def apply(j):
-            change = product(left(col0_ref[j * B : (j + 3) * B, :]), first_r[...])
-            col1_ref[j * B : (j + 3) * B, :] = flat[(9 + j) * B : (12 + j) * B, :] - change
-
-        def whiten():
-            z = product(left(x0[...]), inv_r[...])
-            z_ref[...] = z
-            z_l[...] = left(z)
-
-        def down():
-            x_ref[...] = x_ref[...] - product(z_l[...], first_r[...])
-
-        work = [lambda: solve(0), lambda: solve(3), whiten, lambda: apply(0), lambda: apply(3), down]
-        leaf(diagonal[...], ones, inv_ref, work)
+    def center(k):
+        ref, n = (x, k) if k < 2 else (x_ref, k - 2)
+        ref[n] = center_rows(rows_refs, stat_ref[...], k)
+
+    leaf(flat[0:B], ones, inv, [functools.partial(center, k) for k in range(8)])
+    inv_r[...] = right(inv[...])
+    below = product(left(flat[B : 2 * B, :]), inv_r[...])
+    first_r[...] = right(below)
+    diagonal[...] = flat[8 * B : 9 * B, :] - product(left(below), first_r[...])
+
+    def whiten(k):
+        z = product(left(x[k]), inv_r[...])
+        z_ref[k] = z
+        z_l[...] = left(z)
+
+    def parts(col, j, k):
+        new = col[j * B : (j + 3) * B, :]
+        rows_l_ref[j * B : (j + 3) * B, k * 6 * B : (k + 1) * 6 * B] = left(new)
+        rows_r_ref[j * B : (j + 3) * B, k * 6 * B : (k + 1) * 6 * B] = right(new)
+
+    def down(j, k):
+        change = product(z_l[...], rows_r_ref[j * B : (j + 2) * B, k * 6 * B : (k + 1) * 6 * B])
+        for i in range(2):
+            x_ref[j + i] = x_ref[j + i] - change[:, i * B : (i + 1) * B]
+
+    def solve(j):
+        col0[j * B : (j + 3) * B, :] = product(left(flat[(2 + j) * B : (5 + j) * B, :]), inv_r[...])
+
+    def apply(j):
+        change = product(rows_l_ref[j * B : (j + 3) * B, : 6 * B], first_r[...])
+        col1[j * B : (j + 3) * B, :] = flat[(9 + j) * B : (12 + j) * B, :] - change
+
+    def down1():
+        x[1] = x[1] - product(z_l[...], first_r[...])
+
+    work = [functools.partial(solve, j) for j in (0, 3)]
+    work += [functools.partial(parts, col0, j, 0) for j in (0, 3)]
+    work += [functools.partial(apply, j) for j in (0, 3)]
+    work += [functools.partial(whiten, 0), down1]
+    work += [functools.partial(down, j, 0) for j in (0, 2, 4)]
+    leaf(diagonal[...], ones, inv, work)
+    inv_r[...] = right(inv[...])
+    whiten(1)
+    for j in (0, 3):
+        col0[j * B : (j + 3) * B, :] = product(left(col1[j * B : (j + 3) * B, :]), inv_r[...])
+        parts(col0, j, 1)
+    for j in (0, 2, 4):
+        down(j, 1)
 
 
 def second_kernel(core_ref, *refs):
-    parts_refs, (stat_ref, col0_ref, col1_ref, inv1_ref, z0_ref, x1_ref), rows_refs, out_refs = refs[:4], refs[4:10], refs[10:14], refs[14:18]
-    flat, ones, inv, inv_r, diagonal, panel, x, z_l, rows_l, rows_r, white = refs[18:]
+    parts_refs, (stat_ref, first_l, first_rr, x_ref, z_ref), out_refs = refs[:4], refs[4:9], refs[9:13]
+    flat, ones, inv, inv_r, diagonal, panel, x, z_l, rows_l, rows_r, white = refs[13:]
     core = core_ref[0]
     at = PLACE_IN[1]
-    mean = stat_ref[0:8, :]
     gather_chunk(1, core, parts_refs, flat)
-    make_covariance(1, flat, mean, stat_ref[8:16, :])
+    make_covariance(1, flat, stat_ref[0:8, :], stat_ref[8:16, :])
     ones[...] = jnp.ones((8, B), jnp.float32)
-    inv_r[...] = right(inv1_ref[...])
-    second = product(left(col1_ref[0:B, :]), inv_r[...])
-    panel[2 * B : 3 * B, :] = second
-    both_l = jnp.concatenate([left(col0_ref[0:B, :]), left(second)], axis=1)
-    both_r = jnp.concatenate([right(col0_ref[0:B, :]), right(second)], axis=1)
-    diagonal[...] = flat[0:B, :] - product(both_l, both_r)
+    diagonal[...] = flat[0:B, :] - product(first_l[0:B, :], first_rr[0:B, :])
 
     def start_of(k):
         row = jnp.int32(0)
@@ -351,76 +377,69 @@
             row = jnp.where(k == j, at[j, j] * B, row)
         return pl.multiple_of(row, B)
 
-    def step(k, low):
-        both = low == 2
-        width = 12 * B if both else 6 * B
-
-        def solve(lo, hi):
-            if both:
-                column = col1_ref[(1 + lo) * B : (1 + hi) * B, :]
-                panel[(3 + lo) * B : (3 + hi) * B, :] = product(left(column), inv_r[...])
-            else:
-                size = (hi - lo) * B
-                column = flat[pl.ds(start_of(k - 1) + (2 + lo) * B, size), :]
-                panel[pl.ds(pl.multiple_of((k + 1 + lo) * B, B), size), :] = product(left(column), inv_r[...])
-
-        def whiten():
-            z = product(left(x1_ref[...] if both else x[k - 1]), inv_r[...])
-            white[k - 1] = z
-            if both:
-                white[0] = z0_ref[...]
-                z_l[:, : 6 * B] = left(z0_ref[...])
-            z_l[:, width - 6 * B : width] = left(z)
-
-        def center(j):
-            x[j] = center_rows(rows_refs, stat_ref[...], j)
-
-        def parts(lo, hi):
-            if both:
-                old = col0_ref[(lo - 2) * B : (hi - 2) * B, :]
-                rows_l[lo * B : hi * B, : 6 * B] = left(old)
-                rows_r[lo * B : hi * B, : 6 * B] = right(old)
-            new = panel[lo * B : hi * B, :]
-            rows_l[lo * B : hi * B, width - 6 * B : width] = left(new)
-            rows_r[lo * B : hi * B, width - 6 * B : width] = right(new)
-
-        def down(j):
-            hi = min(j + 2, 8)
-            change = product(z_l[:, :width], rows_r[j * B : hi * B, :width])
-            for i in range(j, hi):
-                x[i] = x[i] - change[:, (i - j) * B : (i - j + 1) * B]
-
-        def update(j, lo, hi):
-            top = min(j + 2, 8)
-            change = product(rows_l[lo * B : hi * B, :width], rows_r[j * B : top * B, :width])
-            for c in range(j, top):
-                first = max(lo, c)
-                n, size = at[first, c] * B, (hi - first) * B
-                flat[n : n + size, :] = flat[n : n + size, :] - change[(first - lo) * B :, (c - j) * B : (c - j + 1) * B]
-
-        def spans(lo, hi):
-            return [(i, min(i + 3, hi)) for i in range(lo, hi, 3)]
-
-        work = [functools.partial(solve, *span) for span in spans(0, 7 - low)]
-        work += [whiten]
-        work += [functools.partial(parts, *span) for span in spans(low, 8)]
-        if both:
-            work += [functools.partial(center, j) for j in range(2, 8)]
-        columns = range(low, 8, 2)
-        work += [functools.partial(update, j, *span) for j in columns for span in spans(j, 8)]
-        work += [functools.partial(down, j) for j in columns]
-        leaf(diagonal[...], ones, inv, work)
+    def update(left_ref, right_ref, skip, j, lo, hi):
+        top = min(j + 2, 8)
+        change = product(left_ref[(lo - skip) * B : (hi - skip) * B, :], right_ref[(j - skip) * B : (top - skip) * B, :])
+        for c in range(j, top):
+            first = max(lo, c)
+            n, size = at[first, c] * B, (hi - first) * B
+            flat[n : n + size, :] = flat[n : n + size, :] - change[(first - lo) * B :, (c - j) * B : (c - j + 1) * B]
+
+    def spans(lo, hi):
+        return [(i, min(i + 3, hi)) for i in range(lo, hi, 3)]
+
+    def updates(left_ref, right_ref, skip, low):
+        return [
+            functools.partial(update, left_ref, right_ref, skip, j, *span) for j in range(low, 8, 2) for span in spans(j, 8)
+        ]
+
+    def advance(k):
         inv_r[...] = right(inv[...])
         below = product(left(flat[pl.ds(start_of(k) + B, B), :]), inv_r[...])
         panel[pl.ds(pl.multiple_of((k + 1) * B, B), B), :] = below
         diagonal[...] = flat[pl.ds(start_of(jnp.minimum(k + 1, 7)), B), :] - product(left(below), right(below))
 
-    in_a_region(core)(lambda: step(2, 2))
-    pl.loop(3, 8)(lambda k: step(k, 3))
+    def take(j):
+        x[j] = x_ref[j - 2]
+
+    leaf(diagonal[...], ones, inv, updates(first_l, first_rr, 2, 2) + [functools.partial(take, j) for j in range(2, 8)])
+    advance(2)
+
+    @pl.loop(3, 8)
+    def _(k):
+        def solve(lo, hi):
+            size = (hi - lo) * B
+            column = flat[pl.ds(start_of(k - 1) + (2 + lo) * B, size), :]
+            panel[pl.ds(pl.multiple_of((k + 1 + lo) * B, B), size), :] = product(left(column), inv_r[...])
+
+        def whiten():
+            z = product(left(x[k - 1]), inv_r[...])
+            white[k - 1] = z
+            z_l[...] = left(z)
+
+        def parts(lo, hi):
+            new = panel[lo * B : hi * B, :]
+            rows_l[lo * B : hi * B, :] = left(new)
+            rows_r[lo * B : hi * B, :] = right(new)
+
+        def down(j):
+            hi = min(j + 2, 8)
+            change = product(z_l[...], rows_r[j * B : hi * B, :])
+            for i in range(j, hi):
+                x[i] = x[i] - change[:, (i - j) * B : (i - j + 1) * B]
+
+        work = [functools.partial(solve, *span) for span in spans(0, 4)]
+        work += [whiten]
+        work += [functools.partial(parts, *span) for span in spans(3, 8)]
+        work += updates(rows_l, rows_r, 0, 3)
+        work += [functools.partial(down, j) for j in range(3, 8, 2)]
+        leaf(diagonal[...], ones, inv, work)
+        advance(k)
+
     white[7] = product(left(x[7]), inv_r[...])
     for k in range(8):
         for g in range(4):
-            out_refs[g][:, k * B : (k + 1) * B] = white[k, g * 64 : (g + 1) * 64, :]
+            out_refs[g][:, k * B : (k + 1) * B] = (z_ref if k < 2 else white)[k, g * 64 : (g + 1) * 64, :]
 
 
 def unpack_kernel(sel_ref, *refs):
@@ -504,21 +523,30 @@
         sums = [[doubled(x, turn, i) for i, x in enumerate(parts)] for parts in sums]
     sums = [parts + [swap(x) for x in parts] for parts in sums]
     tile, tall = (B, B), (6 * B, B)
+
+    def bf16(*shape):
+        return jax.ShapeDtypeStruct(shape, jnp.bfloat16)
+
     state = call(
         first_kernel,
-        [f32(16, B), f32(*tall), f32(*tall), f32(*tile), f32(256, B), f32(256, B)],
+        [f32(16, B), bf16(6 * B, 12 * B), bf16(6 * B, 12 * B), f32(6, 256, B), f32(2, 256, B)],
         (core, *sums[0], *rows),
-        scratch((STAT + 16, B), (8, B), tile) + wide((B, 6 * B)) + scratch(tile) + wide((B, 6 * B)) + scratch((256, B)) + wide((256, 6 * B)),
+        scratch((STAT + 16, B), (8, B), tile)
+        + wide((B, 6 * B))
+        + scratch(tile)
+        + wide((B, 6 * B))
+        + scratch(tall, tall, (2, 256, B))
+        + wide((256, 6 * B)),
         flops=6000000000,
     )
     white = call(
         second_kernel,
         [f32(64, 1024)] * 4,
-        (core, *sums[1], *state, *rows),
+        (core, *sums[1], *state),
         scratch((2 * HALVES[1] + 8 * B, B), (8, B), tile)
         + wide((B, 6 * B))
         + scratch(tile, (14 * B, B), (8, 256, B))
-        + wide((256, 12 * B), (8 * B, 12 * B), (8 * B, 12 * B))
+        + wide((256, 6 * B), (8 * B, 6 * B), (8 * B, 6 * B))
         + scratch((8, 256, B)),
         flops=20000000000,
     )

time: 136 us -> 132 us (0.971)
  Pallas kernels: 33.6 us -> 31.4 us
  starting transfers between devices: 40 us -> 38.3 us
    pallas_call x6, Pallas kernels: 33.6 us -> 31.4 us  [call(): pl.pallas_call(kernel, out_shape=outs, in_specs=[SMEM] * scalars + [VMEM]...]
    ppermute x32, starting transfers between devices: 40 us -> 38.3 us  [permute(): return lax.ppermute(x, AXES, [(n, to(n)) for n in range(128)])]
  transfers between devices with their start and end apart: 32 -> 32, of which waited for: 15 -> 16; matrix products, arithmetic and copies ran while one was open for 1% -> 1% of each run, Pallas kernels for 6% -> 6%
where the time goes in v1:
time: 132 us
  waiting for transfers between devices  60 us (45%)
  starting transfers between devices  38.3 us (29%)
  Pallas kernels  31.4 us (24%)
  other arithmetic  1.33 us (1%)
    ppermute x32, waiting for transfers between devices, permute(): return lax.ppermute(x, AXES, [(n, to(n)) for n in range(128)])  60 us
    ppermute x32, starting transfers between devices, permute(): return lax.ppermute(x, AXES, [(n, to(n)) for n in range(128)])  38.3 us
    pallas_call x6, Pallas kernels, call(): pl.pallas_call(kernel, out_shape=outs, in_specs=[SMEM] * scalars + [VMEM]...  31.4 us
  transfers between devices with their start and end apart: 32, of which 16 were waited for; matrix products, arithmetic and copies ran while one was open for 1% of the time, Pallas kernels for 6%

profile of v1, /device:TPU:1, one launch (start us, length us, event | category | flops | bytes accessed | tf_op | source)
XLA Modules:
  0.0 132.2 jit_solution(1547598803613468666)
XLA Ops:
  0.0 1.4 %collective-permute-start.1 = (f32[128,1024]{1,0:T(8,128)}, f32[128,1024]{1,0:T(8,128)S(1)}, u32[]{:S(2)}, u32[]{:S(2)}) collective-permute-start(f32[128,1024]{1,0:T(8,128)} %x_ref.1), channel_id=1, source_target_pairs={{0,16},{1,17},{2,18},{3,19},{4,20},{5,21},{6,22},{7,23},{8,24},{9,... | collective-permute-start | bytes 1572872 | tf_op jit(solution)/shard_map/ppermute | solution.py:47
  5.4 6.4 %collective-permute-start.2 = (f32[64,1024]{1,0:T(8,128)S(1)}, f32[64,1024]{1,0:T(8,128)S(1)}, u32[]{:S(2)}, u32[]{:S(2)}) collective-permute-start(f32[64,1024]{1,0:T(8,128)S(1)} %get-tuple-element.24), channel_id=1, source_target_pairs={{0,111},{1,110},{2,109},{3,108},{4,107},{5,106},{6,105},{7,104},{8... | collective-permute-start | bytes 786440 | tf_op jit(solution)/shard_map/ppermute | solution.py:47
  11.8 3.0 %collective-permute-start.3 = (f32[64,1024]{1,0:T(8,128)S(1)}, f32[64,1024]{1,0:T(8,128)S(1)}, u32[]{:S(2)}, u32[]{:S(2)}) collective-permute-start(f32[64,1024]{1,0:T(8,128)S(1)} %get-tuple-element.25), channel_id=1, source_target_pairs={{0,0},{1,1},{2,2},{3,3},{4,4},{5,5},{6,6},{7,7},{8,8},{9,9},{10,10... | collective-permute-start | bytes 786440 | tf_op jit(solution)/shard_map/ppermute | solution.py:47
  14.9 1.4 %collective-permute-start.4 = (f32[64,1024]{1,0:T(8,128)S(1)}, f32[64,1024]{1,0:T(8,128)S(1)}, u32[]{:S(2)}, u32[]{:S(2)}) collective-permute-start(f32[64,1024]{1,0:T(8,128)S(1)} %get-tuple-element.26), channel_id=1, source_target_pairs={{0,12},{1,13},{2,14},{3,15},{4,8},{5,9},{6,10},{7,11},{8,4},{9,5},... | collective-permute-start | bytes 786440 | tf_op jit(solution)/shard_map/ppermute | solution.py:47
  16.2 2.5 %collective-permute-start.5 = (f32[64,1024]{1,0:T(8,128)S(1)}, f32[64,1024]{1,0:T(8,128)S(1)}, u32[]{:S(2)}, u32[]{:S(2)}) collective-permute-start(f32[64,1024]{1,0:T(8,128)S(1)} %get-tuple-element.27), channel_id=1, source_target_pairs={{0,3},{1,2},{2,1},{3,0},{4,7},{5,6},{6,5},{7,4},{8,11},{9,10},{10,... | collective-permute-start | bytes 786440 | tf_op jit(solution)/shard_map/ppermute | solution.py:47
  18.8 5.1 %collective-permute-done.3.refs_1_.refs_5_ = f32[64,1024]{1,0:T(8,128)S(1)} collective-permute-done((f32[64,1024]{1,0:T(8,128)S(1)}, f32[64,1024]{1,0:T(8,128)S(1)}, u32[]{:S(2)}, u32[]{:S(2)}) %collective-permute-start.3) | collective-permute-done | bytes 262176 | tf_op jit(solution)/shard_map/ppermute | solution.py:47
  23.9 3.0 %collective-permute-done.4.refs_2_.refs_6_ = f32[64,1024]{1,0:T(8,128)S(1)} collective-permute-done((f32[64,1024]{1,0:T(8,128)S(1)}, f32[64,1024]{1,0:T(8,128)S(1)}, u32[]{:S(2)}, u32[]{:S(2)}) %collective-permute-start.4) | collective-permute-done | bytes 262176 | tf_op jit(solution)/shard_map/ppermute | solution.py:47
  26.9 1.8 %shard_map.38 = (f32[1344,128]{1,0:T(8,128)S(1)}, f32[1344,128]{1,0:T(8,128)S(1)}) custom-call(s32[1]{0:T(128)} %bitcast.core_ref, f32[64,1024]{1,0:T(8,128)S(1)} %collective-permute-done.2.refs_0_.refs_4_, f32[64,1024]{1,0:T(8,128)S(1)} %collective-permute-done.3.refs_1_.refs_5_, f32[64,1024]{1,0:T(8,128)S(1)} %collective-permute-done.4.refs_2_.refs_6_, ...), custom_call_target="tpu_custom_call" | custom-call | flops 1000000 | bytes 4000000 | tf_op jit(solution)/shard_map/pallas_call | solution.py:462
  32.7 9.6 %collective-permute-done.16 = f32[648,128]{1,0:T(8,128)S(1)} collective-permute-done((f32[648,128]{1,0:T(8,128)S(1)}, f32[648,128]{1,0:T(8,128)S(1)}, u32[]{:S(2)}, u32[]{:S(2)}) %collective-permute-start.16) | collective-permute-done | bytes 331808 | tf_op jit(solution)/shard_map/ppermute | solution.py:47
  42.5 1.5 %collective-permute-start.8 = (f32[896,128]{1,0:T(8,128)S(1)}, f32[896,128]{1,0:T(8,128)S(1)}, u32[]{:S(2)}, u32[]{:S(2)}) collective-permute-start(f32[896,128]{1,0:T(8,128)S(1)} %add.69), channel_id=1, source_target_pairs={{0,1},{1,0},{2,3},{3,2},{4,5},{5,4},{6,7},{7,6},{8,9},{9,8},{10,11... | collective-permute-start | bytes 1376264 | tf_op jit(solution)/shard_map/ppermute | solution.py:47
  44.1 4.5 %collective-permute-done.17 = f32[648,128]{1,0:T(8,128)S(1)} collective-permute-done((f32[648,128]{1,0:T(8,128)S(1)}, f32[648,128]{1,0:T(8,128)S(1)}, u32[]{:S(2)}, u32[]{:S(2)}) %collective-permute-start.17) | collective-permute-done | bytes 331808 | tf_op jit(solution)/shard_map/ppermute | solution.py:47
  49.4 15.8 %collective-permute-done.19 = f32[320,128]{1,0:T(8,128)S(1)} collective-permute-done((f32[320,128]{1,0:T(8,128)S(1)}, f32[320,128]{1,0:T(8,128)S(1)}, u32[]{:S(2)}, u32[]{:S(2)}) %collective-permute-start.19) | collective-permute-done | bytes 163872 | tf_op jit(solution)/shard_map/ppermute | solution.py:47
  67.6 3.9 %collective-permute-done.20 = f32[320,128]{1,0:T(8,128)S(1)} collective-permute-done((f32[320,128]{1,0:T(8,128)S(1)}, f32[320,128]{1,0:T(8,128)S(1)}, u32[]{:S(2)}, u32[]{:S(2)}) %collective-permute-start.20) | collective-permute-done | bytes 163872 | tf_op jit(solution)/shard_map/ppermute | solution.py:47
  71.7 4.7 %collective-permute-done.11 = f32[448,128]{1,0:T(8,128)S(1)} collective-permute-done((f32[448,128]{1,0:T(8,128)S(1)}, f32[448,128]{1,0:T(8,128)S(1)}, u32[]{:S(2)}, u32[]{:S(2)}) %collective-permute-start.11) | collective-permute-done | bytes 229408 | tf_op jit(solution)/shard_map/ppermute | solution.py:47
  77.0 1.3 %collective-permute-start.23 = (f32[320,128]{1,0:T(8,128)S(1)}, f32[320,128]{1,0:T(8,128)S(1)}, u32[]{:S(2)}, u32[]{:S(2)}) collective-permute-start(f32[320,128]{1,0:T(8,128)S(1)} %add.83.refs_1_), channel_id=1, source_target_pairs={{0,16},{1,17},{2,18},{3,19},{4,20},{5,21},{6,22},{7,23},{8,24},{9,... | collective-permute-start | bytes 491528 | tf_op jit(solution)/shard_map/ppermute | solution.py:47
  78.4 5.0 %collective-permute-done.12 = f32[448,128]{1,0:T(8,128)S(1)} collective-permute-done((f32[448,128]{1,0:T(8,128)S(1)}, f32[448,128]{1,0:T(8,128)S(1)}, u32[]{:S(2)}, u32[]{:S(2)}) %collective-permute-start.12) | collective-permute-done | bytes 229408 | tf_op jit(solution)/shard_map/ppermute | solution.py:47
  83.4 1.3 %collective-permute-start.14 = (f32[448,128]{1,0:T(8,128)S(1)}, f32[448,128]{1,0:T(8,128)S(1)}, u32[]{:S(2)}, u32[]{:S(2)}) collective-permute-start(f32[448,128]{1,0:T(8,128)S(1)} %add.75.refs_1_), channel_id=1, source_target_pairs={{0,16},{1,17},{2,18},{3,19},{4,20},{5,21},{6,22},{7,23},{8,24},{9,... | collective-permute-start | bytes 688136 | tf_op jit(solution)/shard_map/ppermute | solution.py:47
  85.1 6.7 %shard_map.40 = (f32[16,128]{1,0:T(8,128)S(1)}, bf16[768,1536]{1,0:T(8,128)(2,1)S(1)}, bf16[768,1536]{1,0:T(8,128)(2,1)S(1)}, f32[6,256,128]{2,1,0:T(8,128)S(1)}, f32[2,256,128]{2,1,0:T(8,128)S(1)}) custom-call(s32[1]{0:T(128)} %bitcast.core_ref, f32[648,128]{1,0:T(8,128)S(1)} %add.79.refs_0_, f32[320,128]{1,0:T(8,128)S(1)} %add.83.refs_1_, ...), custom_call_target="tpu_custom_call" | custom-call | flops 6000000000 | bytes 4000000 | tf_op jit(solution)/shard_map/pallas_call | solution.py:462
  91.9 19.2 %shard_map.41 = (f32[64,1024]{1,0:T(8,128)S(1)}, f32[64,1024]{1,0:T(8,128)S(1)}, f32[64,1024]{1,0:T(8,128)S(1)}, f32[64,1024]{1,0:T(8,128)S(1)}) custom-call(s32[1]{0:T(128)} %bitcast.core_ref, f32[896,128]{1,0:T(8,128)S(1)} %add.71.refs_0_, f32[448,128]{1,0:T(8,128)S(1)} %add.75.refs_1_, f32[896,128]{1,0:T(8,128)S(1)} %collective-permute-done.13.refs_2_, ...), custom_call_target="tpu_custom_call" | custom-call | flops 20000000000 | bytes 4000000 | tf_op jit(solution)/shard_map/pallas_call | solution.py:462
  111.0 2.2 %collective-permute-start.24 = (f32[64,1024]{1,0:T(8,128)S(1)}, f32[64,1024]{1,0:T(8,128)S(1)}, u32[]{:S(2)}, u32[]{:S(2)}) collective-permute-start(f32[64,1024]{1,0:T(8,128)S(1)} %get-tuple-element.37), channel_id=1, source_target_pairs={{0,111},{1,110},{2,109},{3,108},{4,107},{5,106},{6,105},{7,104},{8... | collective-permute-start | bytes 786440 | tf_op jit(solution)/shard_map/ppermute | solution.py:47
  113.2 7.1 %collective-permute-start.25 = (f32[64,1024]{1,0:T(8,128)S(1)}, f32[64,1024]{1,0:T(8,128)S(1)}, u32[]{:S(2)}, u32[]{:S(2)}) collective-permute-start(f32[64,1024]{1,0:T(8,128)S(1)} %get-tuple-element.38), channel_id=1, source_target_pairs={{0,0},{1,1},{2,2},{3,3},{4,4},{5,5},{6,6},{7,7},{8,8},{9,9},{10,10... | collective-permute-start | bytes 786440 | tf_op jit(solution)/shard_map/ppermute | solution.py:47
  120.8 4.1 %collective-permute-start.28 = (f32[64,1024]{1,0:T(8,128)S(1)}, f32[64,1024]{1,0:T(8,128)S(1)}, u32[]{:S(2)}, u32[]{:S(2)}) collective-permute-start(f32[64,1024]{1,0:T(8,128)S(1)} %collective-permute-done.24.refs_0_), channel_id=1, source_target_pairs={{0,16},{1,17},{2,18},{3,19},{4,20},{5,21},{6,22},{7,23},{8,24},{9,... | collective-permute-start | bytes 786440 | tf_op jit(solution)/shard_map/ppermute | solution.py:47
  124.8 2.0 %collective-permute-done.25.refs_1_ = f32[64,1024]{1,0:T(8,128)S(1)} collective-permute-done((f32[64,1024]{1,0:T(8,128)S(1)}, f32[64,1024]{1,0:T(8,128)S(1)}, u32[]{:S(2)}, u32[]{:S(2)}) %collective-permute-start.25) | collective-permute-done | bytes 262176 | tf_op jit(solution)/shard_map/ppermute | solution.py:47
  126.8 2.2 %collective-permute-done.26.refs_2_ = f32[64,1024]{1,0:T(8,128)S(1)} collective-permute-done((f32[64,1024]{1,0:T(8,128)S(1)}, f32[64,1024]{1,0:T(8,128)S(1)}, u32[]{:S(2)}, u32[]{:S(2)}) %collective-permute-start.26) | collective-permute-done | bytes 262176 | tf_op jit(solution)/shard_map/ppermute | solution.py:47
  (66 shorter events, 16.2 us)
Async XLA Ops:
  5.4 13.4 %collective-permute-start.2 = (f32[64,1024]{1,0:T(8,128)S(1)}, f32[64,1024]{1,0:T(8,128)S(1)}, u32[]{:S(2)}, u32[]{:S(2)}) collective-permute-start(f32[64,1024]{1,0:T(8,128)S(1)} %get-tuple-element.24), channel_id=1, source_target_pairs={{0,111},{1,110},{2,109},{3,108},{4,107},{5,106},{6,105},{7,104},{8... | collective-permute-start | bytes 786440 | tf_op jit(solution)/shard_map/ppermute | solution.py:47
  11.8 12.0 %collective-permute-start.3 = (f32[64,1024]{1,0:T(8,128)S(1)}, f32[64,1024]{1,0:T(8,128)S(1)}, u32[]{:S(2)}, u32[]{:S(2)}) collective-permute-start(f32[64,1024]{1,0:T(8,128)S(1)} %get-tuple-element.25), channel_id=1, source_target_pairs={{0,0},{1,1},{2,2},{3,3},{4,4},{5,5},{6,6},{7,7},{8,8},{9,9},{10,10... | collective-permute-start | bytes 786440 | tf_op jit(solution)/shard_map/ppermute | solution.py:47
  14.9 12.0 %collective-permute-start.4 = (f32[64,1024]{1,0:T(8,128)S(1)}, f32[64,1024]{1,0:T(8,128)S(1)}, u32[]{:S(2)}, u32[]{:S(2)}) collective-permute-start(f32[64,1024]{1,0:T(8,128)S(1)} %get-tuple-element.26), channel_id=1, source_target_pairs={{0,12},{1,13},{2,14},{3,15},{4,8},{5,9},{6,10},{7,11},{8,4},{9,5},... | collective-permute-start | bytes 786440 | tf_op jit(solution)/shard_map/ppermute | solution.py:47
  16.2 10.7 %collective-permute-start.5 = (f32[64,1024]{1,0:T(8,128)S(1)}, f32[64,1024]{1,0:T(8,128)S(1)}, u32[]{:S(2)}, u32[]{:S(2)}) collective-permute-start(f32[64,1024]{1,0:T(8,128)S(1)} %get-tuple-element.27), channel_id=1, source_target_pairs={{0,3},{1,2},{2,1},{3,0},{4,7},{5,6},{6,5},{7,4},{8,11},{9,10},{10,... | collective-permute-start | bytes 786440 | tf_op jit(solution)/shard_map/ppermute | solution.py:47
  31.0 11.4 %collective-permute-start.7 = (f32[896,128]{1,0:T(8,128)S(1)}, f32[896,128]{1,0:T(8,128)S(1)}, u32[]{:S(2)}, u32[]{:S(2)}) collective-permute-start(f32[896,128]{1,0:T(8,128)S(1)} %slice_add_fusion), channel_id=1, source_target_pairs={{0,4},{1,5},{2,6},{3,7},{4,0},{5,1},{6,2},{7,3},{8,12},{9,13},{10,... | collective-permute-start | bytes 1376264 | tf_op jit(solution)/shard_map/ppermute | solution.py:47
  32.1 10.1 %collective-permute-start.16 = (f32[648,128]{1,0:T(8,128)S(1)}, f32[648,128]{1,0:T(8,128)S(1)}, u32[]{:S(2)}, u32[]{:S(2)}) collective-permute-start(f32[648,128]{1,0:T(8,128)S(1)} %slice_add_fusion.1), channel_id=1, source_target_pairs={{0,4},{1,5},{2,6},{3,7},{4,0},{5,1},{6,2},{7,3},{8,12},{9,13},{10,... | collective-permute-start | bytes 995336 | tf_op jit(solution)/shard_map/ppermute | solution.py:47
  42.3 6.3 %collective-permute-start.17 = (f32[648,128]{1,0:T(8,128)S(1)}, f32[648,128]{1,0:T(8,128)S(1)}, u32[]{:S(2)}, u32[]{:S(2)}) collective-permute-start(f32[648,128]{1,0:T(8,128)S(1)} %add.77), channel_id=1, source_target_pairs={{0,1},{1,0},{2,3},{3,2},{4,5},{5,4},{6,7},{7,6},{8,9},{9,8},{10,11... | collective-permute-start | bytes 995336 | tf_op jit(solution)/shard_map/ppermute | solution.py:47
  42.5 24.5 %collective-permute-start.8 = (f32[896,128]{1,0:T(8,128)S(1)}, f32[896,128]{1,0:T(8,128)S(1)}, u32[]{:S(2)}, u32[]{:S(2)}) collective-permute-start(f32[896,128]{1,0:T(8,128)S(1)} %add.69), channel_id=1, source_target_pairs={{0,1},{1,0},{2,3},{3,2},{4,5},{5,4},{6,7},{7,6},{8,9},{9,8},{10,11... | collective-permute-start | bytes 1376264 | tf_op jit(solution)/shard_map/ppermute | solution.py:47
  44.0 21.8 %collective-permute-start.10 = (f32[448,128]{1,0:T(8,128)S(1)}, f32[448,128]{1,0:T(8,128)S(1)}, u32[]{:S(2)}, u32[]{:S(2)}) collective-permute-start(f32[448,128]{1,0:T(8,128)S(1)} %slice_add_fusion.2), channel_id=1, source_target_pairs={{0,32},{1,33},{2,34},{3,35},{4,36},{5,37},{6,38},{7,39},{8,40},{9,... | collective-permute-start | bytes 688136 | tf_op jit(solution)/shard_map/ppermute | solution.py:47
  48.7 18.8 %collective-permute-start.18 = (f32[648,128]{1,0:T(8,128)S(1)}, f32[648,128]{1,0:T(8,128)S(1)}, u32[]{:S(2)}, u32[]{:S(2)}) collective-permute-start(f32[648,128]{1,0:T(8,128)S(1)} %add.78), channel_id=1, source_target_pairs={{0,32},{1,33},{2,34},{3,35},{4,36},{5,37},{6,38},{7,39},{8,40},{9,... | collective-permute-start | bytes 995336 | tf_op jit(solution)/shard_map/ppermute | solution.py:47
  49.2 16.0 %collective-permute-start.19 = (f32[320,128]{1,0:T(8,128)S(1)}, f32[320,128]{1,0:T(8,128)S(1)}, u32[]{:S(2)}, u32[]{:S(2)}) collective-permute-start(f32[320,128]{1,0:T(8,128)S(1)} %slice_add_fusion.3), channel_id=1, source_target_pairs={{0,32},{1,33},{2,34},{3,35},{4,36},{5,37},{6,38},{7,39},{8,40},{9,... | collective-permute-start | bytes 491528 | tf_op jit(solution)/shard_map/ppermute | solution.py:47
  65.3 6.3 %collective-permute-start.20 = (f32[320,128]{1,0:T(8,128)S(1)}, f32[320,128]{1,0:T(8,128)S(1)}, u32[]{:S(2)}, u32[]{:S(2)}) collective-permute-start(f32[320,128]{1,0:T(8,128)S(1)} %add.81), channel_id=1, source_target_pairs={{0,4},{1,5},{2,6},{3,7},{4,0},{5,1},{6,2},{7,3},{8,12},{9,13},{10,... | collective-permute-start | bytes 491528 | tf_op jit(solution)/shard_map/ppermute | solution.py:47
  65.8 10.7 %collective-permute-start.11 = (f32[448,128]{1,0:T(8,128)S(1)}, f32[448,128]{1,0:T(8,128)S(1)}, u32[]{:S(2)}, u32[]{:S(2)}) collective-permute-start(f32[448,128]{1,0:T(8,128)S(1)} %add.73), channel_id=1, source_target_pairs={{0,4},{1,5},{2,6},{3,7},{4,0},{5,1},{6,2},{7,3},{8,12},{9,13},{10,... | collective-permute-start | bytes 688136 | tf_op jit(solution)/shard_map/ppermute | solution.py:47
  67.0 17.7 %collective-permute-start.9 = (f32[896,128]{1,0:T(8,128)S(1)}, f32[896,128]{1,0:T(8,128)S(1)}, u32[]{:S(2)}, u32[]{:S(2)}) collective-permute-start(f32[896,128]{1,0:T(8,128)S(1)} %add.70), channel_id=1, source_target_pairs={{0,32},{1,33},{2,34},{3,35},{4,36},{5,37},{6,38},{7,39},{8,40},{9,... | collective-permute-start | bytes 1376264 | tf_op jit(solution)/shard_map/ppermute | solution.py:47
  67.5 17.5 %collective-permute-start.22 = (f32[648,128]{1,0:T(8,128)S(1)}, f32[648,128]{1,0:T(8,128)S(1)}, u32[]{:S(2)}, u32[]{:S(2)}) collective-permute-start(f32[648,128]{1,0:T(8,128)S(1)} %add.79.refs_0_), channel_id=1, source_target_pairs={{0,16},{1,17},{2,18},{3,19},{4,20},{5,21},{6,22},{7,23},{8,24},{9,... | collective-permute-start | bytes 995336 | tf_op jit(solution)/shard_map/ppermute | solution.py:47
  76.5 6.8 %collective-permute-start.12 = (f32[448,128]{1,0:T(8,128)S(1)}, f32[448,128]{1,0:T(8,128)S(1)}, u32[]{:S(2)}, u32[]{:S(2)}) collective-permute-start(f32[448,128]{1,0:T(8,128)S(1)} %add.74), channel_id=1, source_target_pairs={{0,1},{1,0},{2,3},{3,2},{4,5},{5,4},{6,7},{7,6},{8,9},{9,8},{10,11... | collective-permute-start | bytes 688136 | tf_op jit(solution)/shard_map/ppermute | solution.py:47
  77.0 8.0 %collective-permute-start.23 = (f32[320,128]{1,0:T(8,128)S(1)}, f32[320,128]{1,0:T(8,128)S(1)}, u32[]{:S(2)}, u32[]{:S(2)}) collective-permute-start(f32[320,128]{1,0:T(8,128)S(1)} %add.83.refs_1_), channel_id=1, source_target_pairs={{0,16},{1,17},{2,18},{3,19},{4,20},{5,21},{6,22},{7,23},{8,24},{9,... | collective-permute-start | bytes 491528 | tf_op jit(solution)/shard_map/ppermute | solution.py:47
  83.4 8.5 %collective-permute-start.14 = (f32[448,128]{1,0:T(8,128)S(1)}, f32[448,128]{1,0:T(8,128)S(1)}, u32[]{:S(2)}, u32[]{:S(2)}) collective-permute-start(f32[448,128]{1,0:T(8,128)S(1)} %add.75.refs_1_), channel_id=1, source_target_pairs={{0,16},{1,17},{2,18},{3,19},{4,20},{5,21},{6,22},{7,23},{8,24},{9,... | collective-permute-start | bytes 688136 | tf_op jit(solution)/shard_map/ppermute | solution.py:47
  84.8 7.1 %collective-permute-start.13 = (f32[896,128]{1,0:T(8,128)S(1)}, f32[896,128]{1,0:T(8,128)S(1)}, u32[]{:S(2)}, u32[]{:S(2)}) collective-permute-start(f32[896,128]{1,0:T(8,128)S(1)} %add.71.refs_0_), channel_id=1, source_target_pairs={{0,16},{1,17},{2,18},{3,19},{4,20},{5,21},{6,22},{7,23},{8,24},{9,... | collective-permute-start | bytes 1376264 | tf_op jit(solution)/shard_map/ppermute | solution.py:47
  111.0 9.7 %collective-permute-start.24 = (f32[64,1024]{1,0:T(8,128)S(1)}, f32[64,1024]{1,0:T(8,128)S(1)}, u32[]{:S(2)}, u32[]{:S(2)}) collective-permute-start(f32[64,1024]{1,0:T(8,128)S(1)} %get-tuple-element.37), channel_id=1, source_target_pairs={{0,111},{1,110},{2,109},{3,108},{4,107},{5,106},{6,105},{7,104},{8... | collective-permute-start | bytes 786440 | tf_op jit(solution)/shard_map/ppermute | solution.py:47
  113.2 13.6 %collective-permute-start.25 = (f32[64,1024]{1,0:T(8,128)S(1)}, f32[64,1024]{1,0:T(8,128)S(1)}, u32[]{:S(2)}, u32[]{:S(2)}) collective-permute-start(f32[64,1024]{1,0:T(8,128)S(1)} %get-tuple-element.38), channel_id=1, source_target_pairs={{0,0},{1,1},{2,2},{3,3},{4,4},{5,5},{6,6},{7,7},{8,8},{9,9},{10,10... | collective-permute-start | bytes 786440 | tf_op jit(solution)/shard_map/ppermute | solution.py:47
  120.3 8.8 %collective-permute-start.26 = (f32[64,1024]{1,0:T(8,128)S(1)}, f32[64,1024]{1,0:T(8,128)S(1)}, u32[]{:S(2)}, u32[]{:S(2)}) collective-permute-start(f32[64,1024]{1,0:T(8,128)S(1)} %get-tuple-element.39), channel_id=1, source_target_pairs={{0,12},{1,13},{2,14},{3,15},{4,8},{5,9},{6,10},{7,11},{8,4},{9,5},... | collective-permute-start | bytes 786440 | tf_op jit(solution)/shard_map/ppermute | solution.py:47
  120.4 8.7 %collective-permute-start.27 = (f32[64,1024]{1,0:T(8,128)S(1)}, f32[64,1024]{1,0:T(8,128)S(1)}, u32[]{:S(2)}, u32[]{:S(2)}) collective-permute-start(f32[64,1024]{1,0:T(8,128)S(1)} %get-tuple-element.40), channel_id=1, source_target_pairs={{0,3},{1,2},{2,1},{3,0},{4,7},{5,6},{6,5},{7,4},{8,11},{9,10},{10,... | collective-permute-start | bytes 786440 | tf_op jit(solution)/shard_map/ppermute | solution.py:47
  120.8 8.8 %collective-permute-start.28 = (f32[64,1024]{1,0:T(8,128)S(1)}, f32[64,1024]{1,0:T(8,128)S(1)}, u32[]{:S(2)}, u32[]{:S(2)}) collective-permute-start(f32[64,1024]{1,0:T(8,128)S(1)} %collective-permute-done.24.refs_0_), channel_id=1, source_target_pairs={{0,16},{1,17},{2,18},{3,19},{4,20},{5,21},{6,22},{7,23},{8,24},{9,... | collective-permute-start | bytes 786440 | tf_op jit(solution)/shard_map/ppermute | solution.py:47
  (9 other events, 21.8 us)

commit v2 on v1

--- a/solution.py
+++ b/solution.py
@@ -83,42 +83,55 @@
     return plain(jnp.concatenate([p, p, p], axis=1), jnp.concatenate([l, m, h], axis=0))
 
 
-def pack_kernel(where_ref, small_ref, ids2_ref, x_ref, x2_ref, *refs):
-    out_refs, sel_ref = refs[:4], refs[4]
+def group_and_rank(where_ref, ids):
+    rows = ids.shape[1]
+    turned = ids ^ where_ref[1]
+    group = jnp.zeros_like(turned)
+    for place, mask in enumerate(CARRIED[0] + CARRIED[1]):
+        group = jnp.where(turned == mask, place, group)
+    group = jnp.broadcast_to((group ^ (4 * where_ref[0])).astype(jnp.float32), (8, rows))
+    onehot = jnp.where(group == iota((8, rows), 0).astype(jnp.float32), 1.0, 0.0)
+    earlier = jnp.where(iota((rows, rows), 0) < iota((rows, rows), 1), 1.0, 0.0).astype(jnp.bfloat16)
+    counted = plain(onehot.astype(jnp.bfloat16), earlier)
+    return group[0:1, :], jnp.sum(counted * onehot, axis=0, keepdims=True)
+
+
+def packed(slot, x):
+    place = jnp.where(slot == iota((B, slot.shape[1]), 0).astype(jnp.float32), 1.0, 0.0)
+    return jnp.where(jnp.sum(place, axis=1, keepdims=True) > 0.5, pick(place, x), EMPTY)
+
+
+def pack_kernel(where_ref, small_ref, x_ref, out_ref, sel_ref):
     rows = x_ref.shape[0]
-    core, home = where_ref[0], where_ref[1]
-    earlier = jnp.where(iota((rows, rows), 0) < iota((rows, rows), 1), 1.0, 0.0).astype(jnp.bfloat16)
-
-    def group_and_rank(ids):
-        turned = ids ^ home
-        group = jnp.zeros_like(turned)
-        for place, mask in enumerate(CARRIED[0] + CARRIED[1]):
-            group = jnp.where(turned == mask, place, group)
-        group = group ^ (4 * core)
-        group = jnp.broadcast_to(group.astype(jnp.float32), (8, rows))
-        onehot = jnp.where(group == iota((8, rows), 0).astype(jnp.float32), 1.0, 0.0)
-        counted = plain(onehot.astype(jnp.bfloat16), earlier)
-        return group[0:1, :], jnp.sum(counted * onehot, axis=0, keepdims=True)
-
-    group, rank = group_and_rank(small_ref[0:1, :])
-    group2, rank2 = group_and_rank(ids2_ref[...])
-    slot = jnp.concatenate([group * 64.0 + rank, group2 * 64.0 + 32.0 + rank2], axis=1)
-    place = jnp.where(slot == iota((256, 2 * rows), 0).astype(jnp.float32), 1.0, 0.0)
-    used = jnp.sum(place, axis=1, keepdims=True)
-    packed = jnp.where(used > 0.5, pick(place, jnp.concatenate([x_ref[...], x2_ref[...]], axis=0)), EMPTY)
-    for g in range(4):
-        out_refs[g][...] = packed[g * 64 : (g + 1) * 64]
-    home_slot = jnp.broadcast_to(group * 32.0 + rank, (rows, rows))
+    group, rank = group_and_rank(where_ref, small_ref[0:1, :])
+    slot = group * 32.0 + rank
+    out_ref[...] = packed(slot, x_ref[...])
+    home_slot = jnp.broadcast_to(slot, (rows, rows))
     want = jnp.broadcast_to(small_ref[1:2, :].astype(jnp.float32), (rows, rows)).T
     picked = jnp.where(want == iota((rows, rows), 1).astype(jnp.float32), home_slot, 0.0)
     sel_ref[...] = jnp.broadcast_to(jnp.sum(picked, axis=1, keepdims=True), (rows, rows))
 
 
+def merge_kernel(where_ref, ids_ref, x_ref, own_ref, *out_refs):
+    group, rank = group_and_rank(where_ref, ids_ref[...])
+    theirs = packed(group * 32.0 + rank, x_ref[...])
+    for g, ref in enumerate(out_refs):
+        ref[:32, :] = own_ref[g * 32 : (g + 1) * 32, :]
+        ref[32:, :] = theirs[g * 32 : (g + 1) * 32]
+
+
 CHUNKS = ((0, 2), (2, 8))
 PLACE_IN = [{p: n for n, p in enumerate((i, k) for k in range(*cols) for i in range(k, 8))} for cols in CHUNKS]
 STAT = len(PLACE_IN[0]) * B
-HALVES = ((STAT + 16) // 2, len(PLACE_IN[1]) * B // 2)
-CUTS = ((0, 648, 968), (0, 896, 1344))
+HALVES = ((STAT + 32) // 2, len(PLACE_IN[1]) * B // 2)
+CUTS = ((0, 640, 976), (0, 896, 1344))
+
+
+def rows_of(chunk, info_ref, which, part, place):
+    start, end = CUTS[chunk][part], CUTS[chunk][part + 1]
+    size = (end - start) // 2
+    bit = info_ref[1 + which] if part == 0 else info_ref[3]
+    return pl.ds(pl.multiple_of(which * HALVES[chunk] + start + (place ^ bit) * size, 8), size)
 
 
 def gram_kernel(chunk, core_ref, *refs):
@@ -134,6 +147,7 @@
         live = [jnp.where(ref[:, 0:B] < 1e29, 1.0, 0.0) for ref in rows_refs]
         count = jnp.sum(jnp.concatenate(live, axis=0), axis=0, keepdims=True)
         flat[STAT + 8 : STAT + 16, :] = jnp.broadcast_to(count, (8, B))
+        flat[STAT + 16 : STAT + 32, :] = jnp.zeros((16, B), jnp.float32)
     xl[first * B :, :] = left(xs[:, first * B :].T)
     for k in range(first, end, 2):
         h, m, l = split(xs[:, k * B : (k + 2) * B])
@@ -141,9 +155,12 @@
         for c in range(2):
             n = PLACE_IN[chunk][k + c, k + c] * B
             flat[n : n + (8 - k - c) * B, :] = two[c * B :, c * B : (c + 1) * B]
-    half = HALVES[chunk]
     for ref, which in ((mine_ref, core_ref[0]), (other_ref, 1 - core_ref[0])):
-        ref[...] = flat[pl.ds(pl.multiple_of(which * half, 8), half), :]
+        for part in range(2):
+            start, end = CUTS[chunk][part : part + 2]
+            for place, row in enumerate((start, (start + end) // 2)):
+                rows = rows_of(chunk, core_ref, which, part, place)
+                ref[row : row + rows.size, :] = flat[rows, :]
 
 
 def row_of(x, j):
@@ -263,10 +280,9 @@
         between[g + 1]()
 
 
-def gather_chunk(chunk, core, refs, flat):
-    for which, ref in enumerate(refs):
-        start = (which // 2 ^ core) * HALVES[chunk] + CUTS[chunk][which % 2]
-        flat[pl.ds(pl.multiple_of(start, 8), ref.shape[0]), :] = ref[...]
+def gather_chunk(chunk, info_ref, refs, flat):
+    for n, ref in enumerate(refs):
+        flat[rows_of(chunk, info_ref, n // 4 ^ info_ref[0], n % 2, n // 2 % 2), :] = ref[...]
 
 
 def make_covariance(chunk, flat, mean, scale):
@@ -300,10 +316,9 @@
 
 
 def first_kernel(core_ref, *refs):
-    parts_refs, rows_refs, (stat_ref, rows_l_ref, rows_r_ref, x_ref, z_ref) = refs[:4], refs[4:8], refs[8:13]
-    flat, ones, inv, inv_r, diagonal, first_r, col0, col1, x, z_l = refs[13:]
-    core = core_ref[0]
-    gather_chunk(0, core, parts_refs, flat)
+    parts_refs, rows_refs, (stat_ref, rows_l_ref, rows_r_ref, x_ref, z_ref) = refs[:8], refs[8:12], refs[12:17]
+    flat, ones, inv, inv_r, diagonal, first_r, col0, col1, x, z_l = refs[17:]
+    gather_chunk(0, core_ref, parts_refs, flat)
     scale = 1.0 / flat[STAT + 8 : STAT + 16, :]
     mean = flat[STAT : STAT + 8, :] * scale
     stat_ref[0:8, :] = mean
@@ -362,11 +377,10 @@
 
 
 def second_kernel(core_ref, *refs):
-    parts_refs, (stat_ref, first_l, first_rr, x_ref, z_ref), out_refs = refs[:4], refs[4:9], refs[9:13]
-    flat, ones, inv, inv_r, diagonal, panel, x, z_l, rows_l, rows_r, white = refs[13:]
-    core = core_ref[0]
+    parts_refs, (stat_ref, first_l, first_rr, x_ref, z_ref), out_refs = refs[:8], refs[8:13], refs[13:17]
+    flat, ones, inv, inv_r, diagonal, panel, x, z_l, rows_l, rows_r, white = refs[17:]
     at = PLACE_IN[1]
-    gather_chunk(1, core, parts_refs, flat)
+    gather_chunk(1, core_ref, parts_refs, flat)
     make_covariance(1, flat, stat_ref[0:8, :], stat_ref[8:16, :])
     ones[...] = jnp.ones((8, B), jnp.float32)
     diagonal[...] = flat[0:B, :] - product(first_l[0:B, :], first_rr[0:B, :])
@@ -483,13 +497,16 @@
 
     ids = domain_ids.reshape(1, B)
     where = jnp.concatenate([core, home])
-    *packed, sel = call(
+    info = jnp.concatenate([core, jnp.stack([w // 4 % 2, w % 2, d // 2 % 2]).astype(jnp.int32)])
+    their_rows = swap(embeddings)
+    own, sel = call(
         pack_kernel,
-        [f32(64, 1024)] * 4 + [f32(B, B)],
-        (where, jnp.concatenate([ids, order]), swap(ids), embeddings, swap(embeddings)),
+        [f32(B, 1024), f32(B, B)],
+        (where, jnp.concatenate([ids, order]), embeddings),
         mib=12,
+        flops=1000000000,
     )
-    rows = exchange(packed)
+    rows = exchange(call(merge_kernel, [f32(64, 1024)] * 4, (where, swap(ids), their_rows, own), mib=12))
 
     def scratch(*shapes, dtype=jnp.float32):
         return [pltpu.VMEM(shape, dtype) for shape in shapes]
@@ -502,26 +519,37 @@
         return call(
             functools.partial(gram_kernel, chunk),
             [f32(half, B)] * 2,
-            (core, *rows),
+            (info, *rows),
             scratch((256, 1024)) + wide((1024, 1536)) + scratch((2 * half, B)),
         )
 
     def across(x, turn, i):
         return permute(x, lambda n: partner(n, (turn + (2 if i else coords(n)[3])) % 3))
 
-    grams = [gram(chunk) for chunk in range(2)]
-    sums = []
+    grams = []
+    for chunk in range(2):
+        grams.append(gram(chunk))
+
+    def doubled(mine, sent, turn, i):
+        theirs = across(sent, turn, i)
+        return mine + theirs
+
+    kept, sent = [], []
     for chunk, (mine, other) in enumerate(grams):
         other = swap(other)
-        sums.append([mine[lo:hi] + other[lo:hi] for lo, hi in zip(CUTS[chunk], CUTS[chunk][1:])])
-
-    def doubled(x, turn, i):
-        partners = across(x, turn, i)
-        return x + partners
-
+        cuts = [(lo, (lo + hi) // 2, hi) for lo, hi in zip(CUTS[chunk], CUTS[chunk][1:])]
+        kept.append([mine[lo:mid] + other[lo:mid] for lo, mid, _ in cuts])
+        sent.append([mine[mid:hi] + other[mid:hi] for _, mid, hi in cuts])
     for turn in range(3):
-        sums = [[doubled(x, turn, i) for i, x in enumerate(parts)] for parts in sums]
-    sums = [parts + [swap(x) for x in parts] for parts in sums]
+        kept = [
+            [doubled(x, y, turn, i) for i, (x, y) in enumerate(zip(kept[chunk], sent[chunk]))]
+            for chunk in range(2)
+        ]
+        sent = kept
+    sums = []
+    for chunk in range(2):
+        parts = kept[chunk] + [across(x, 0, i) for i, x in enumerate(kept[chunk])]
+        sums.append(parts + [swap(x) for x in parts])
     tile, tall = (B, B), (6 * B, B)
 
     def bf16(*shape):
@@ -530,8 +558,8 @@
     state = call(
         first_kernel,
         [f32(16, B), bf16(6 * B, 12 * B), bf16(6 * B, 12 * B), f32(6, 256, B), f32(2, 256, B)],
-        (core, *sums[0], *rows),
-        scratch((STAT + 16, B), (8, B), tile)
+        (info, *sums[0], *rows),
+        scratch((STAT + 32, B), (8, B), tile)
         + wide((B, 6 * B))
         + scratch(tile)
         + wide((B, 6 * B))
@@ -542,7 +570,7 @@
     white = call(
         second_kernel,
         [f32(64, 1024)] * 4,
-        (core, *sums[1], *state),
+        (info, *sums[1], *state),
         scratch((2 * HALVES[1] + 8 * B, B), (8, B), tile)
         + wide((B, 6 * B))
         + scratch(tile, (14 * B, B), (8, 256, B))

time: 132 us -> 120 us (0.909)
  waiting for transfers between devices: 60 us -> 36.4 us
  starting transfers between devices: 38.3 us -> 46.4 us
  Pallas kernels: 31.4 us -> 34.2 us
    ppermute x32 -> x40, waiting for transfers between devices: 60 us -> 36.4 us  [permute(): return lax.ppermute(x, AXES, [(n, to(n)) for n in range(128)])]
    ppermute x32 -> x40, starting transfers between devices: 38.3 us -> 46.4 us  [permute(): return lax.ppermute(x, AXES, [(n, to(n)) for n in range(128)])]
    pallas_call x6 -> x7, Pallas kernels: 31.4 us -> 34.2 us  [call(): pl.pallas_call(kernel, out_shape=outs, in_specs=[SMEM] * scalars + [VMEM]...]
  transfers between devices with their start and end apart: 32 -> 40, of which waited for: 16 -> 14; matrix products, arithmetic and copies ran while one was open for 1% -> 1% of each run, Pallas kernels for 6% -> 9%
where the time goes in v2:
time: 120 us; the launch traced here: 119 us
  starting transfers between devices  46.4 us (39%)
  waiting for transfers between devices  36.4 us (30%)
  Pallas kernels  34.2 us (29%)
    ppermute x40, starting transfers between devices, permute(): return lax.ppermute(x, AXES, [(n, to(n)) for n in range(128)])  46.4 us
    ppermute x40, waiting for transfers between devices, permute(): return lax.ppermute(x, AXES, [(n, to(n)) for n in range(128)])  36.4 us
    pallas_call x7, Pallas kernels, call(): pl.pallas_call(kernel, out_shape=outs, in_specs=[SMEM] * scalars + [VMEM]...  34.2 us
  transfers between devices with their start and end apart: 40, of which 14 were waited for; matrix products, arithmetic and copies ran while one was open for 1% of the time, Pallas kernels for 9%

profile of v2, /device:TPU:1, one launch (start us, length us, event | category | flops | bytes accessed | tf_op | source)
XLA Modules:
  0.0 119.4 jit_solution(16715986495020163099)
XLA Ops:
  5.2 6.4 %collective-permute-start.2 = (f32[64,1024]{1,0:T(8,128)S(1)}, f32[64,1024]{1,0:T(8,128)S(1)}, u32[]{:S(2)}, u32[]{:S(2)}) collective-permute-start(f32[64,1024]{1,0:T(8,128)S(1)} %get-tuple-element.26), channel_id=1, source_target_pairs={{0,111},{1,110},{2,109},{3,108},{4,107},{5,106},{6,105},{7,104},{8... | collective-permute-start | bytes 786440 | tf_op jit(solution)/shard_map/ppermute | solution.py:47
  11.6 3.0 %collective-permute-start.3 = (f32[64,1024]{1,0:T(8,128)S(1)}, f32[64,1024]{1,0:T(8,128)S(1)}, u32[]{:S(2)}, u32[]{:S(2)}) collective-permute-start(f32[64,1024]{1,0:T(8,128)S(1)} %get-tuple-element.27), channel_id=1, source_target_pairs={{0,0},{1,1},{2,2},{3,3},{4,4},{5,5},{6,6},{7,7},{8,8},{9,9},{10,10... | collective-permute-start | bytes 786440 | tf_op jit(solution)/shard_map/ppermute | solution.py:47
  14.6 1.4 %collective-permute-start.4 = (f32[64,1024]{1,0:T(8,128)S(1)}, f32[64,1024]{1,0:T(8,128)S(1)}, u32[]{:S(2)}, u32[]{:S(2)}) collective-permute-start(f32[64,1024]{1,0:T(8,128)S(1)} %get-tuple-element.28), channel_id=1, source_target_pairs={{0,12},{1,13},{2,14},{3,15},{4,8},{5,9},{6,10},{7,11},{8,4},{9,5},... | collective-permute-start | bytes 786440 | tf_op jit(solution)/shard_map/ppermute | solution.py:47
  16.0 2.5 %collective-permute-start.5 = (f32[64,1024]{1,0:T(8,128)S(1)}, f32[64,1024]{1,0:T(8,128)S(1)}, u32[]{:S(2)}, u32[]{:S(2)}) collective-permute-start(f32[64,1024]{1,0:T(8,128)S(1)} %get-tuple-element.29), channel_id=1, source_target_pairs={{0,3},{1,2},{2,1},{3,0},{4,7},{5,6},{6,5},{7,4},{8,11},{9,10},{10,... | collective-permute-start | bytes 786440 | tf_op jit(solution)/shard_map/ppermute | solution.py:47
  18.6 5.1 %collective-permute-done.3.refs_1_.refs_9_ = f32[64,1024]{1,0:T(8,128)S(1)} collective-permute-done((f32[64,1024]{1,0:T(8,128)S(1)}, f32[64,1024]{1,0:T(8,128)S(1)}, u32[]{:S(2)}, u32[]{:S(2)}) %collective-permute-start.3) | collective-permute-done | bytes 262176 | tf_op jit(solution)/shard_map/ppermute | solution.py:47
  23.7 3.0 %collective-permute-done.4.refs_2_.refs_10_ = f32[64,1024]{1,0:T(8,128)S(1)} collective-permute-done((f32[64,1024]{1,0:T(8,128)S(1)}, f32[64,1024]{1,0:T(8,128)S(1)}, u32[]{:S(2)}, u32[]{:S(2)}) %collective-permute-start.4) | collective-permute-done | bytes 262176 | tf_op jit(solution)/shard_map/ppermute | solution.py:47
  26.8 1.8 %shard_map.40 = (f32[976,128]{1,0:T(8,128)S(1)}, f32[976,128]{1,0:T(8,128)S(1)}) custom-call(s32[4]{0:T(128)S(1)} %pad_add_fusion.2.core_ref, f32[64,1024]{1,0:T(8,128)S(1)} %collective-permute-done.2.refs_0_.refs_8_, f32[64,1024]{1,0:T(8,128)S(1)} %collective-permute-done.3.refs_1_.refs_9_, f32[64,1024]{1,0:T(8,128)S(1)} %collective-permute-done.4.refs_2_.refs_10_, ...), custom_call_target="tpu_custom_call" | custom-call | flops 1000000 | bytes 4000000 | tf_op jit(solution)/shard_map/pallas_call | solution.py:476
  28.6 2.3 %shard_map.39 = (f32[1344,128]{1,0:T(8,128)S(1)}, f32[1344,128]{1,0:T(8,128)S(1)}) custom-call(s32[4]{0:T(128)S(1)} %pad_add_fusion.2.core_ref, f32[64,1024]{1,0:T(8,128)S(1)} %collective-permute-done.2.refs_0_.refs_8_, f32[64,1024]{1,0:T(8,128)S(1)} %collective-permute-done.3.refs_1_.refs_9_, f32[64,1024]{1,0:T(8,128)S(1)} %collective-permute-done.4.refs_2_.refs_10_, ...), custom_call_target="tpu_custom_call" | custom-call | flops 1000000 | bytes 4000000 | tf_op jit(solution)/shard_map/pallas_call | solution.py:476
  31.8 4.3 %collective-permute-done.20 = f32[320,128]{1,0:T(8,128)S(1)} collective-permute-done((f32[320,128]{1,0:T(8,128)S(1)}, f32[320,128]{1,0:T(8,128)S(1)}, u32[]{:S(2)}, u32[]{:S(2)}) %collective-permute-start.20) | collective-permute-done | bytes 163872 | tf_op jit(solution)/shard_map/ppermute | solution.py:47
  36.4 1.5 %collective-permute-start.10 = (f32[224,128]{1,0:T(8,128)S(1)}, f32[224,128]{1,0:T(8,128)S(1)}, u32[]{:S(2)}, u32[]{:S(2)}) collective-permute-start(f32[224,128]{1,0:T(8,128)S(1)} %slice_add_fusion.4), channel_id=1, source_target_pairs={{0,32},{1,33},{2,34},{3,35},{4,36},{5,37},{6,38},{7,39},{8,40},{9,... | collective-permute-start | bytes 344072 | tf_op jit(solution)/shard_map/ppermute | solution.py:47
  38.0 4.8 %collective-permute-done.7 = f32[448,128]{1,0:T(8,128)S(1)} collective-permute-done((f32[448,128]{1,0:T(8,128)S(1)}, f32[448,128]{1,0:T(8,128)S(1)}, u32[]{:S(2)}, u32[]{:S(2)}) %collective-permute-start.7) | collective-permute-done | bytes 229408 | tf_op jit(solution)/shard_map/ppermute | solution.py:47
  45.5 2.6 %collective-permute-done.8 = f32[448,128]{1,0:T(8,128)S(1)} collective-permute-done((f32[448,128]{1,0:T(8,128)S(1)}, f32[448,128]{1,0:T(8,128)S(1)}, u32[]{:S(2)}, u32[]{:S(2)}) %collective-permute-start.8) | collective-permute-done | bytes 229408 | tf_op jit(solution)/shard_map/ppermute | solution.py:47
  51.3 4.1 %collective-permute-done.24 = f32[168,128]{1,0:T(8,128)S(1)} collective-permute-done((f32[168,128]{1,0:T(8,128)S(1)}, f32[168,128]{1,0:T(8,128)S(1)}, u32[]{:S(2)}, u32[]{:S(2)}) %collective-permute-start.24) | collective-permute-done | bytes 86048 | tf_op jit(solution)/shard_map/ppermute | solution.py:47
  55.5 1.5 %collective-permute-start.12 = (f32[224,128]{1,0:T(8,128)S(1)}, f32[224,128]{1,0:T(8,128)S(1)}, u32[]{:S(2)}, u32[]{:S(2)}) collective-permute-start(f32[224,128]{1,0:T(8,128)S(1)} %add.102), channel_id=1, source_target_pairs={{0,1},{1,0},{2,3},{3,2},{4,5},{5,4},{6,7},{7,6},{8,9},{9,8},{10,11... | collective-permute-start | bytes 344072 | tf_op jit(solution)/shard_map/ppermute | solution.py:47
  57.1 2.4 %collective-permute-done.25 = f32[168,128]{1,0:T(8,128)S(1)} collective-permute-done((f32[168,128]{1,0:T(8,128)S(1)}, f32[168,128]{1,0:T(8,128)S(1)}, u32[]{:S(2)}, u32[]{:S(2)}) %collective-permute-start.25) | collective-permute-done | bytes 86048 | tf_op jit(solution)/shard_map/ppermute | solution.py:47
  59.6 2.7 %collective-permute-start.29 = (f32[168,128]{1,0:T(8,128)S(1)}, f32[168,128]{1,0:T(8,128)S(1)}, u32[]{:S(2)}, u32[]{:S(2)}) collective-permute-start(f32[168,128]{1,0:T(8,128)S(1)} %add.113.refs_1_), channel_id=1, source_target_pairs={{0,16},{1,17},{2,18},{3,19},{4,20},{5,21},{6,22},{7,23},{8,24},{9,... | collective-permute-start | bytes 258056 | tf_op jit(solution)/shard_map/ppermute | solution.py:47
  64.6 2.3 %collective-permute-start.31 = (f32[168,128]{1,0:T(8,128)S(1)}, f32[168,128]{1,0:T(8,128)S(1)}, u32[]{:S(2)}, u32[]{:S(2)}) collective-permute-start(f32[168,128]{1,0:T(8,128)S(1)} %collective-permute-done.27.refs_3_), channel_id=1, source_target_pairs={{0,16},{1,17},{2,18},{3,19},{4,20},{5,21},{6,22},{7,23},{8,24},{9,... | collective-permute-start | bytes 258056 | tf_op jit(solution)/shard_map/ppermute | solution.py:47
  68.1 2.1 %collective-permute-start.18 = (f32[224,128]{1,0:T(8,128)S(1)}, f32[224,128]{1,0:T(8,128)S(1)}, u32[]{:S(2)}, u32[]{:S(2)}) collective-permute-start(f32[224,128]{1,0:T(8,128)S(1)} %collective-permute-done.14.refs_3_), channel_id=1, source_target_pairs={{0,16},{1,17},{2,18},{3,19},{4,20},{5,21},{6,22},{7,23},{8,24},{9,... | collective-permute-start | bytes 344072 | tf_op jit(solution)/shard_map/ppermute | solution.py:47
  70.8 7.2 %shard_map.41 = (f32[16,128]{1,0:T(8,128)S(1)}, bf16[768,1536]{1,0:T(8,128)(2,1)S(1)}, bf16[768,1536]{1,0:T(8,128)(2,1)S(1)}, f32[6,256,128]{2,1,0:T(8,128)S(1)}, f32[2,256,128]{2,1,0:T(8,128)S(1)}) custom-call(s32[4]{0:T(128)S(1)} %pad_add_fusion.2.core_ref, f32[320,128]{1,0:T(8,128)S(1)} %add.108.refs_0_, f32[168,128]{1,0:T(8,128)S(1)} %add.113.refs_1_, ...), custom_call_target="tpu_custom_call" | custom-call | flops 6000000000 | bytes 4000000 | tf_op jit(solution)/shard_map/pallas_call | solution.py:476
  78.0 19.7 %shard_map.42 = (f32[64,1024]{1,0:T(8,128)S(1)}, f32[64,1024]{1,0:T(8,128)S(1)}, f32[64,1024]{1,0:T(8,128)S(1)}, f32[64,1024]{1,0:T(8,128)S(1)}) custom-call(s32[4]{0:T(128)S(1)} %pad_add_fusion.2.core_ref, f32[448,128]{1,0:T(8,128)S(1)} %add.98.refs_0_, f32[224,128]{1,0:T(8,128)S(1)} %add.103.refs_1_, f32[448,128]{1,0:T(8,128)S(1)} %collective-permute-done.13.refs_2_, ...), custom_call_target="tpu_custom_call" | custom-call | flops 20000000000 | bytes 4000000 | tf_op jit(solution)/shard_map/pallas_call | solution.py:476
  97.8 2.9 %collective-permute-start.32 = (f32[64,1024]{1,0:T(8,128)S(1)}, f32[64,1024]{1,0:T(8,128)S(1)}, u32[]{:S(2)}, u32[]{:S(2)}) collective-permute-start(f32[64,1024]{1,0:T(8,128)S(1)} %get-tuple-element.39), channel_id=1, source_target_pairs={{0,111},{1,110},{2,109},{3,108},{4,107},{5,106},{6,105},{7,104},{8... | collective-permute-start | bytes 786440 | tf_op jit(solution)/shard_map/ppermute | solution.py:47
  100.6 6.9 %collective-permute-start.33 = (f32[64,1024]{1,0:T(8,128)S(1)}, f32[64,1024]{1,0:T(8,128)S(1)}, u32[]{:S(2)}, u32[]{:S(2)}) collective-permute-start(f32[64,1024]{1,0:T(8,128)S(1)} %get-tuple-element.40), channel_id=1, source_target_pairs={{0,0},{1,1},{2,2},{3,3},{4,4},{5,5},{6,6},{7,7},{8,8},{9,9},{10,10... | collective-permute-start | bytes 786440 | tf_op jit(solution)/shard_map/ppermute | solution.py:47
  110.4 3.3 %collective-permute-done.33.refs_1_ = f32[64,1024]{1,0:T(8,128)S(1)} collective-permute-done((f32[64,1024]{1,0:T(8,128)S(1)}, f32[64,1024]{1,0:T(8,128)S(1)}, u32[]{:S(2)}, u32[]{:S(2)}) %collective-permute-start.33) | collective-permute-done | bytes 262176 | tf_op jit(solution)/shard_map/ppermute | solution.py:47
  113.7 2.6 %collective-permute-done.34.refs_2_ = f32[64,1024]{1,0:T(8,128)S(1)} collective-permute-done((f32[64,1024]{1,0:T(8,128)S(1)}, f32[64,1024]{1,0:T(8,128)S(1)}, u32[]{:S(2)}, u32[]{:S(2)}) %collective-permute-start.34) | collective-permute-done | bytes 262176 | tf_op jit(solution)/shard_map/ppermute | solution.py:47
  (84 shorter events, 22.8 us)
Async XLA Ops:
  5.2 13.4 %collective-permute-start.2 = (f32[64,1024]{1,0:T(8,128)S(1)}, f32[64,1024]{1,0:T(8,128)S(1)}, u32[]{:S(2)}, u32[]{:S(2)}) collective-permute-start(f32[64,1024]{1,0:T(8,128)S(1)} %get-tuple-element.26), channel_id=1, source_target_pairs={{0,111},{1,110},{2,109},{3,108},{4,107},{5,106},{6,105},{7,104},{8... | collective-permute-start | bytes 786440 | tf_op jit(solution)/shard_map/ppermute | solution.py:47
  11.6 12.2 %collective-permute-start.3 = (f32[64,1024]{1,0:T(8,128)S(1)}, f32[64,1024]{1,0:T(8,128)S(1)}, u32[]{:S(2)}, u32[]{:S(2)}) collective-permute-start(f32[64,1024]{1,0:T(8,128)S(1)} %get-tuple-element.27), channel_id=1, source_target_pairs={{0,0},{1,1},{2,2},{3,3},{4,4},{5,5},{6,6},{7,7},{8,8},{9,9},{10,10... | collective-permute-start | bytes 786440 | tf_op jit(solution)/shard_map/ppermute | solution.py:47
  14.6 12.2 %collective-permute-start.4 = (f32[64,1024]{1,0:T(8,128)S(1)}, f32[64,1024]{1,0:T(8,128)S(1)}, u32[]{:S(2)}, u32[]{:S(2)}) collective-permute-start(f32[64,1024]{1,0:T(8,128)S(1)} %get-tuple-element.28), channel_id=1, source_target_pairs={{0,12},{1,13},{2,14},{3,15},{4,8},{5,9},{6,10},{7,11},{8,4},{9,5},... | collective-permute-start | bytes 786440 | tf_op jit(solution)/shard_map/ppermute | solution.py:47
  16.0 10.8 %collective-permute-start.5 = (f32[64,1024]{1,0:T(8,128)S(1)}, f32[64,1024]{1,0:T(8,128)S(1)}, u32[]{:S(2)}, u32[]{:S(2)}) collective-permute-start(f32[64,1024]{1,0:T(8,128)S(1)} %get-tuple-element.29), channel_id=1, source_target_pairs={{0,3},{1,2},{2,1},{3,0},{4,7},{5,6},{6,5},{7,4},{8,11},{9,10},{10,... | collective-permute-start | bytes 786440 | tf_op jit(solution)/shard_map/ppermute | solution.py:47
  31.7 16.8 %collective-permute-start.23 = (f32[168,128]{1,0:T(8,128)S(1)}, f32[168,128]{1,0:T(8,128)S(1)}, u32[]{:S(2)}, u32[]{:S(2)}) collective-permute-start(f32[168,128]{1,0:T(8,128)S(1)} %slice_add_fusion.6), channel_id=1, source_target_pairs={{0,32},{1,33},{2,34},{3,35},{4,36},{5,37},{6,38},{7,39},{8,40},{9,... | collective-permute-start | bytes 258056 | tf_op jit(solution)/shard_map/ppermute | solution.py:47
  36.1 8.3 %collective-permute-start.21 = (f32[320,128]{1,0:T(8,128)S(1)}, f32[320,128]{1,0:T(8,128)S(1)}, u32[]{:S(2)}, u32[]{:S(2)}) collective-permute-start(f32[320,128]{1,0:T(8,128)S(1)} %fusion.1), channel_id=1, source_target_pairs={{0,1},{1,0},{2,3},{3,2},{4,5},{5,4},{6,7},{7,6},{8,9},{9,8},{10,11... | collective-permute-start | bytes 491528 | tf_op jit(solution)/shard_map/ppermute | solution.py:47
  36.4 7.4 %collective-permute-start.10 = (f32[224,128]{1,0:T(8,128)S(1)}, f32[224,128]{1,0:T(8,128)S(1)}, u32[]{:S(2)}, u32[]{:S(2)}) collective-permute-start(f32[224,128]{1,0:T(8,128)S(1)} %slice_add_fusion.4), channel_id=1, source_target_pairs={{0,32},{1,33},{2,34},{3,35},{4,36},{5,37},{6,38},{7,39},{8,40},{9,... | collective-permute-start | bytes 344072 | tf_op jit(solution)/shard_map/ppermute | solution.py:47
  43.8 11.6 %collective-permute-start.11 = (f32[224,128]{1,0:T(8,128)S(1)}, f32[224,128]{1,0:T(8,128)S(1)}, u32[]{:S(2)}, u32[]{:S(2)}) collective-permute-start(f32[224,128]{1,0:T(8,128)S(1)} %fusion.2), channel_id=1, source_target_pairs={{0,4},{1,5},{2,6},{3,7},{4,0},{5,1},{6,2},{7,3},{8,12},{9,13},{10,... | collective-permute-start | bytes 344072 | tf_op jit(solution)/shard_map/ppermute | solution.py:47
  48.1 8.9 %collective-permute-start.9 = (f32[448,128]{1,0:T(8,128)S(1)}, f32[448,128]{1,0:T(8,128)S(1)}, u32[]{:S(2)}, u32[]{:S(2)}) collective-permute-start(f32[448,128]{1,0:T(8,128)S(1)} %add.97), channel_id=1, source_target_pairs={{0,32},{1,33},{2,34},{3,35},{4,36},{5,37},{6,38},{7,39},{8,40},{9,... | collective-permute-start | bytes 688136 | tf_op jit(solution)/shard_map/ppermute | solution.py:47
  48.5 6.8 %collective-permute-start.24 = (f32[168,128]{1,0:T(8,128)S(1)}, f32[168,128]{1,0:T(8,128)S(1)}, u32[]{:S(2)}, u32[]{:S(2)}) collective-permute-start(f32[168,128]{1,0:T(8,128)S(1)} %fusion.3), channel_id=1, source_target_pairs={{0,4},{1,5},{2,6},{3,7},{4,0},{5,1},{6,2},{7,3},{8,12},{9,13},{10,... | collective-permute-start | bytes 258056 | tf_op jit(solution)/shard_map/ppermute | solution.py:47
  50.6 12.7 %collective-permute-start.26 = (f32[320,128]{1,0:T(8,128)S(1)}, f32[320,128]{1,0:T(8,128)S(1)}, u32[]{:S(2)}, u32[]{:S(2)}) collective-permute-start(f32[320,128]{1,0:T(8,128)S(1)} %add.108.refs_0_), channel_id=1, source_target_pairs={{0,4},{1,5},{2,6},{3,7},{4,0},{5,1},{6,2},{7,3},{8,12},{9,13},{10,... | collective-permute-start | bytes 491528 | tf_op jit(solution)/shard_map/ppermute | solution.py:47
  55.5 6.9 %collective-permute-start.12 = (f32[224,128]{1,0:T(8,128)S(1)}, f32[224,128]{1,0:T(8,128)S(1)}, u32[]{:S(2)}, u32[]{:S(2)}) collective-permute-start(f32[224,128]{1,0:T(8,128)S(1)} %add.102), channel_id=1, source_target_pairs={{0,1},{1,0},{2,3},{3,2},{4,5},{5,4},{6,7},{7,6},{8,9},{9,8},{10,11... | collective-permute-start | bytes 344072 | tf_op jit(solution)/shard_map/ppermute | solution.py:47
  57.0 13.2 %collective-permute-start.13 = (f32[448,128]{1,0:T(8,128)S(1)}, f32[448,128]{1,0:T(8,128)S(1)}, u32[]{:S(2)}, u32[]{:S(2)}) collective-permute-start(f32[448,128]{1,0:T(8,128)S(1)} %add.98.refs_0_), channel_id=1, source_target_pairs={{0,4},{1,5},{2,6},{3,7},{4,0},{5,1},{6,2},{7,3},{8,12},{9,13},{10,... | collective-permute-start | bytes 688136 | tf_op jit(solution)/shard_map/ppermute | solution.py:47
  62.4 7.9 %collective-permute-start.28 = (f32[320,128]{1,0:T(8,128)S(1)}, f32[320,128]{1,0:T(8,128)S(1)}, u32[]{:S(2)}, u32[]{:S(2)}) collective-permute-start(f32[320,128]{1,0:T(8,128)S(1)} %add.108.refs_0_), channel_id=1, source_target_pairs={{0,16},{1,17},{2,18},{3,19},{4,20},{5,21},{6,22},{7,23},{8,24},{9,... | collective-permute-start | bytes 491528 | tf_op jit(solution)/shard_map/ppermute | solution.py:47
  63.3 7.4 %collective-permute-start.30 = (f32[320,128]{1,0:T(8,128)S(1)}, f32[320,128]{1,0:T(8,128)S(1)}, u32[]{:S(2)}, u32[]{:S(2)}) collective-permute-start(f32[320,128]{1,0:T(8,128)S(1)} %collective-permute-done.26.refs_2_), channel_id=1, source_target_pairs={{0,16},{1,17},{2,18},{3,19},{4,20},{5,21},{6,22},{7,23},{8,24},{9,... | collective-permute-start | bytes 491528 | tf_op jit(solution)/shard_map/ppermute | solution.py:47
  67.8 10.2 %collective-permute-start.16 = (f32[224,128]{1,0:T(8,128)S(1)}, f32[224,128]{1,0:T(8,128)S(1)}, u32[]{:S(2)}, u32[]{:S(2)}) collective-permute-start(f32[224,128]{1,0:T(8,128)S(1)} %add.103.refs_1_), channel_id=1, source_target_pairs={{0,16},{1,17},{2,18},{3,19},{4,20},{5,21},{6,22},{7,23},{8,24},{9,... | collective-permute-start | bytes 344072 | tf_op jit(solution)/shard_map/ppermute | solution.py:47
  68.1 9.9 %collective-permute-start.18 = (f32[224,128]{1,0:T(8,128)S(1)}, f32[224,128]{1,0:T(8,128)S(1)}, u32[]{:S(2)}, u32[]{:S(2)}) collective-permute-start(f32[224,128]{1,0:T(8,128)S(1)} %collective-permute-done.14.refs_3_), channel_id=1, source_target_pairs={{0,16},{1,17},{2,18},{3,19},{4,20},{5,21},{6,22},{7,23},{8,24},{9,... | collective-permute-start | bytes 344072 | tf_op jit(solution)/shard_map/ppermute | solution.py:47
  70.2 7.8 %collective-permute-start.15 = (f32[448,128]{1,0:T(8,128)S(1)}, f32[448,128]{1,0:T(8,128)S(1)}, u32[]{:S(2)}, u32[]{:S(2)}) collective-permute-start(f32[448,128]{1,0:T(8,128)S(1)} %add.98.refs_0_), channel_id=1, source_target_pairs={{0,16},{1,17},{2,18},{3,19},{4,20},{5,21},{6,22},{7,23},{8,24},{9,... | collective-permute-start | bytes 688136 | tf_op jit(solution)/shard_map/ppermute | solution.py:47
  70.2 7.8 %collective-permute-start.17 = (f32[448,128]{1,0:T(8,128)S(1)}, f32[448,128]{1,0:T(8,128)S(1)}, u32[]{:S(2)}, u32[]{:S(2)}) collective-permute-start(f32[448,128]{1,0:T(8,128)S(1)} %collective-permute-done.13.refs_2_), channel_id=1, source_target_pairs={{0,16},{1,17},{2,18},{3,19},{4,20},{5,21},{6,22},{7,23},{8,24},{9,... | collective-permute-start | bytes 688136 | tf_op jit(solution)/shard_map/ppermute | solution.py:47
  97.8 11.4 %collective-permute-start.32 = (f32[64,1024]{1,0:T(8,128)S(1)}, f32[64,1024]{1,0:T(8,128)S(1)}, u32[]{:S(2)}, u32[]{:S(2)}) collective-permute-start(f32[64,1024]{1,0:T(8,128)S(1)} %get-tuple-element.39), channel_id=1, source_target_pairs={{0,111},{1,110},{2,109},{3,108},{4,107},{5,106},{6,105},{7,104},{8... | collective-permute-start | bytes 786440 | tf_op jit(solution)/shard_map/ppermute | solution.py:47
  100.6 13.1 %collective-permute-start.33 = (f32[64,1024]{1,0:T(8,128)S(1)}, f32[64,1024]{1,0:T(8,128)S(1)}, u32[]{:S(2)}, u32[]{:S(2)}) collective-permute-start(f32[64,1024]{1,0:T(8,128)S(1)} %get-tuple-element.40), channel_id=1, source_target_pairs={{0,0},{1,1},{2,2},{3,3},{4,4},{5,5},{6,6},{7,7},{8,8},{9,9},{10,10... | collective-permute-start | bytes 786440 | tf_op jit(solution)/shard_map/ppermute | solution.py:47
  107.5 8.8 %collective-permute-start.34 = (f32[64,1024]{1,0:T(8,128)S(1)}, f32[64,1024]{1,0:T(8,128)S(1)}, u32[]{:S(2)}, u32[]{:S(2)}) collective-permute-start(f32[64,1024]{1,0:T(8,128)S(1)} %get-tuple-element.41), channel_id=1, source_target_pairs={{0,12},{1,13},{2,14},{3,15},{4,8},{5,9},{6,10},{7,11},{8,4},{9,5},... | collective-permute-start | bytes 786440 | tf_op jit(solution)/shard_map/ppermute | solution.py:47
  107.6 8.7 %collective-permute-start.35 = (f32[64,1024]{1,0:T(8,128)S(1)}, f32[64,1024]{1,0:T(8,128)S(1)}, u32[]{:S(2)}, u32[]{:S(2)}) collective-permute-start(f32[64,1024]{1,0:T(8,128)S(1)} %get-tuple-element.42), channel_id=1, source_target_pairs={{0,3},{1,2},{2,1},{3,0},{4,7},{5,6},{6,5},{7,4},{8,11},{9,10},{10,... | collective-permute-start | bytes 786440 | tf_op jit(solution)/shard_map/ppermute | solution.py:47
  109.2 7.6 %collective-permute-start.36 = (f32[64,1024]{1,0:T(8,128)S(1)}, f32[64,1024]{1,0:T(8,128)S(1)}, u32[]{:S(2)}, u32[]{:S(2)}) collective-permute-start(f32[64,1024]{1,0:T(8,128)S(1)} %collective-permute-done.32.refs_0_), channel_id=1, source_target_pairs={{0,16},{1,17},{2,18},{3,19},{4,20},{5,21},{6,22},{7,23},{8,24},{9,... | collective-permute-start | bytes 786440 | tf_op jit(solution)/shard_map/ppermute | solution.py:47
  (17 other events, 66.1 us)

commit v3 on v2

--- a/solution.py
+++ b/solution.py
@@ -123,15 +123,8 @@
 CHUNKS = ((0, 2), (2, 8))
 PLACE_IN = [{p: n for n, p in enumerate((i, k) for k in range(*cols) for i in range(k, 8))} for cols in CHUNKS]
 STAT = len(PLACE_IN[0]) * B
-HALVES = ((STAT + 32) // 2, len(PLACE_IN[1]) * B // 2)
-CUTS = ((0, 640, 976), (0, 896, 1344))
-
-
-def rows_of(chunk, info_ref, which, part, place):
-    start, end = CUTS[chunk][part], CUTS[chunk][part + 1]
-    size = (end - start) // 2
-    bit = info_ref[1 + which] if part == 0 else info_ref[3]
-    return pl.ds(pl.multiple_of(which * HALVES[chunk] + start + (place ^ bit) * size, 8), size)
+HALVES = ((STAT + 16) // 2, len(PLACE_IN[1]) * B // 2)
+CUTS = ((0, 648, 968), (0, 896, 1344))
 
 
 def gram_kernel(chunk, core_ref, *refs):
@@ -147,7 +140,6 @@
         live = [jnp.where(ref[:, 0:B] < 1e29, 1.0, 0.0) for ref in rows_refs]
         count = jnp.sum(jnp.concatenate(live, axis=0), axis=0, keepdims=True)
         flat[STAT + 8 : STAT + 16, :] = jnp.broadcast_to(count, (8, B))
-        flat[STAT + 16 : STAT + 32, :] = jnp.zeros((16, B), jnp.float32)
     xl[first * B :, :] = left(xs[:, first * B :].T)
     for k in range(first, end, 2):
         h, m, l = split(xs[:, k * B : (k + 2) * B])
@@ -155,12 +147,9 @@
         for c in range(2):
             n = PLACE_IN[chunk][k + c, k + c] * B
             flat[n : n + (8 - k - c) * B, :] = two[c * B :, c * B : (c + 1) * B]
+    half = HALVES[chunk]
     for ref, which in ((mine_ref, core_ref[0]), (other_ref, 1 - core_ref[0])):
-        for part in range(2):
-            start, end = CUTS[chunk][part : part + 2]
-            for place, row in enumerate((start, (start + end) // 2)):
-                rows = rows_of(chunk, core_ref, which, part, place)
-                ref[row : row + rows.size, :] = flat[rows, :]
+        ref[...] = flat[pl.ds(pl.multiple_of(which * half, 8), half), :]
 
 
 def row_of(x, j):
@@ -280,9 +269,10 @@
         between[g + 1]()
 
 
-def gather_chunk(chunk, info_ref, refs, flat):
-    for n, ref in enumerate(refs):
-        flat[rows_of(chunk, info_ref, n // 4 ^ info_ref[0], n % 2, n // 2 % 2), :] = ref[...]
+def gather_chunk(chunk, core, refs, flat):
+    for which, ref in enumerate(refs):
+        start = (which // 2 ^ core) * HALVES[chunk] + CUTS[chunk][which % 2]
+        flat[pl.ds(pl.multiple_of(start, 8), ref.shape[0]), :] = ref[...]
 
 
 def make_covariance(chunk, flat, mean, scale):
@@ -315,10 +305,9 @@
     inverse_factor(lambda g: block[8 * g : 8 * g + 8, :], ones[...], inv, [functools.partial(run, p) for p in slots])
 
 
-def first_kernel(core_ref, *refs):
-    parts_refs, rows_refs, (stat_ref, rows_l_ref, rows_r_ref, x_ref, z_ref) = refs[:8], refs[8:12], refs[12:17]
-    flat, ones, inv, inv_r, diagonal, first_r, col0, col1, x, z_l = refs[17:]
-    gather_chunk(0, core_ref, parts_refs, flat)
+def column0_kernel(core_ref, *refs):
+    parts_refs, rows_refs, (flat, stat_ref, inv, x_ref), (ones,) = refs[:4], refs[4:8], refs[8:12], refs[12:]
+    gather_chunk(0, core_ref[0], parts_refs, flat)
     scale = 1.0 / flat[STAT + 8 : STAT + 16, :]
     mean = flat[STAT : STAT + 8, :] * scale
     stat_ref[0:8, :] = mean
@@ -327,17 +316,20 @@
     ones[...] = jnp.ones((8, B), jnp.float32)
 
     def center(k):
-        ref, n = (x, k) if k < 2 else (x_ref, k - 2)
-        ref[n] = center_rows(rows_refs, stat_ref[...], k)
+        x_ref[k] = center_rows(rows_refs, stat_ref[...], k)
 
     leaf(flat[0:B], ones, inv, [functools.partial(center, k) for k in range(8)])
-    inv_r[...] = right(inv[...])
+
+
+def column1_kernel(flat, inv0, x, rows_l_ref, rows_r_ref, x_ref, z_ref, ones, inv, inv_r, diagonal, first_r, col0, col1, x1, z_l):
+    ones[...] = jnp.ones((8, B), jnp.float32)
+    inv_r[...] = right(inv0[...])
     below = product(left(flat[B : 2 * B, :]), inv_r[...])
     first_r[...] = right(below)
     diagonal[...] = flat[8 * B : 9 * B, :] - product(left(below), first_r[...])
 
     def whiten(k):
-        z = product(left(x[k]), inv_r[...])
+        z = product(left(x1[...] if k else x[0]), inv_r[...])
         z_ref[k] = z
         z_l[...] = left(z)
 
@@ -349,7 +341,8 @@
     def down(j, k):
         change = product(z_l[...], rows_r_ref[j * B : (j + 2) * B, k * 6 * B : (k + 1) * 6 * B])
         for i in range(2):
-            x_ref[j + i] = x_ref[j + i] - change[:, i * B : (i + 1) * B]
+            old = x_ref[j + i] if k else x[j + i + 2]
+            x_ref[j + i] = old - change[:, i * B : (i + 1) * B]
 
     def solve(j):
         col0[j * B : (j + 3) * B, :] = product(left(flat[(2 + j) * B : (5 + j) * B, :]), inv_r[...])
@@ -359,7 +352,7 @@
         col1[j * B : (j + 3) * B, :] = flat[(9 + j) * B : (12 + j) * B, :] - change
 
     def down1():
-        x[1] = x[1] - product(z_l[...], first_r[...])
+        x1[...] = x[1] - product(z_l[...], first_r[...])
 
     work = [functools.partial(solve, j) for j in (0, 3)]
     work += [functools.partial(parts, col0, j, 0) for j in (0, 3)]
@@ -377,10 +370,11 @@
 
 
 def second_kernel(core_ref, *refs):
-    parts_refs, (stat_ref, first_l, first_rr, x_ref, z_ref), out_refs = refs[:8], refs[8:13], refs[13:17]
-    flat, ones, inv, inv_r, diagonal, panel, x, z_l, rows_l, rows_r, white = refs[17:]
+    parts_refs, (stat_ref, first_l, first_rr, x_ref, z_ref), out_refs = refs[:4], refs[4:9], refs[9:13]
+    flat, ones, inv, inv_r, diagonal, panel, x, z_l, rows_l, rows_r, white = refs[13:]
+    core = core_ref[0]
     at = PLACE_IN[1]
-    gather_chunk(1, core_ref, parts_refs, flat)
+    gather_chunk(1, core, parts_refs, flat)
     make_covariance(1, flat, stat_ref[0:8, :], stat_ref[8:16, :])
     ones[...] = jnp.ones((8, B), jnp.float32)
     diagonal[...] = flat[0:B, :] - product(first_l[0:B, :], first_rr[0:B, :])
@@ -419,8 +413,7 @@
     leaf(diagonal[...], ones, inv, updates(first_l, first_rr, 2, 2) + [functools.partial(take, j) for j in range(2, 8)])
     advance(2)
 
-    @pl.loop(3, 8)
-    def _(k):
+    def step(low, k):
         def solve(lo, hi):
             size = (hi - lo) * B
             column = flat[pl.ds(start_of(k - 1) + (2 + lo) * B, size), :]
@@ -442,14 +435,16 @@
             for i in range(j, hi):
                 x[i] = x[i] - change[:, (i - j) * B : (i - j + 1) * B]
 
-        work = [functools.partial(solve, *span) for span in spans(0, 4)]
+        work = [functools.partial(solve, *span) for span in spans(0, 7 - low)]
         work += [whiten]
-        work += [functools.partial(parts, *span) for span in spans(3, 8)]
-        work += updates(rows_l, rows_r, 0, 3)
-        work += [functools.partial(down, j) for j in range(3, 8, 2)]
+        work += [functools.partial(parts, *span) for span in spans(low, 8)]
+        work += updates(rows_l, rows_r, 0, low)
+        work += [functools.partial(down, j) for j in range(low, 8, 2)]
         leaf(diagonal[...], ones, inv, work)
         advance(k)
 
+    for low, end in ((3, 5), (5, 8)):
+        pl.loop(low, end)(functools.partial(step, low))
     white[7] = product(left(x[7]), inv_r[...])
     for k in range(8):
         for g in range(4):
@@ -497,7 +492,6 @@
 
     ids = domain_ids.reshape(1, B)
     where = jnp.concatenate([core, home])
-    info = jnp.concatenate([core, jnp.stack([w // 4 % 2, w % 2, d // 2 % 2]).astype(jnp.int32)])
     their_rows = swap(embeddings)
     own, sel = call(
         pack_kernel,
@@ -519,7 +513,7 @@
         return call(
             functools.partial(gram_kernel, chunk),
             [f32(half, B)] * 2,
-            (info, *rows),
+            (core, *rows),
             scratch((256, 1024)) + wide((1024, 1536)) + scratch((2 * half, B)),
         )
 
@@ -530,47 +524,49 @@
     for chunk in range(2):
         grams.append(gram(chunk))
 
-    def doubled(mine, sent, turn, i):
-        theirs = across(sent, turn, i)
-        return mine + theirs
-
-    kept, sent = [], []
+    sums = []
     for chunk, (mine, other) in enumerate(grams):
         other = swap(other)
-        cuts = [(lo, (lo + hi) // 2, hi) for lo, hi in zip(CUTS[chunk], CUTS[chunk][1:])]
-        kept.append([mine[lo:mid] + other[lo:mid] for lo, mid, _ in cuts])
-        sent.append([mine[mid:hi] + other[mid:hi] for _, mid, hi in cuts])
+        sums.append([mine[lo:hi] + other[lo:hi] for lo, hi in zip(CUTS[chunk], CUTS[chunk][1:])])
+
+    def doubled(x, turn, i):
+        partners = across(x, turn, i)
+        return x + partners
+
     for turn in range(3):
-        kept = [
-            [doubled(x, y, turn, i) for i, (x, y) in enumerate(zip(kept[chunk], sent[chunk]))]
-            for chunk in range(2)
-        ]
-        sent = kept
-    sums = []
-    for chunk in range(2):
-        parts = kept[chunk] + [across(x, 0, i) for i, x in enumerate(kept[chunk])]
-        sums.append(parts + [swap(x) for x in parts])
+        sums = [[doubled(x, turn, i) for i, x in enumerate(parts)] for parts in sums]
+    for parts in sums:
+        for i in range(2):
+            parts.append(swap(parts[i]))
     tile, tall = (B, B), (6 * B, B)
 
     def bf16(*shape):
         return jax.ShapeDtypeStruct(shape, jnp.bfloat16)
 
+    flat, stat, inv, x = call(
+        column0_kernel,
+        [f32(STAT + 16, B), f32(16, B), f32(*tile), f32(8, 256, B)],
+        (core, *sums[0], *rows),
+        scratch((8, B)),
+        flops=3000000000,
+    )
     state = call(
-        first_kernel,
-        [f32(16, B), bf16(6 * B, 12 * B), bf16(6 * B, 12 * B), f32(6, 256, B), f32(2, 256, B)],
-        (info, *sums[0], *rows),
-        scratch((STAT + 32, B), (8, B), tile)
+        column1_kernel,
+        [bf16(6 * B, 12 * B), bf16(6 * B, 12 * B), f32(6, 256, B), f32(2, 256, B)],
+        (flat, inv, x),
+        scratch((8, B), tile)
         + wide((B, 6 * B))
         + scratch(tile)
         + wide((B, 6 * B))
-        + scratch(tall, tall, (2, 256, B))
+        + scratch(tall, tall, (256, B))
         + wide((256, 6 * B)),
-        flops=6000000000,
+        scalars=0,
+        flops=3000000000,
     )
     white = call(
         second_kernel,
         [f32(64, 1024)] * 4,
-        (info, *sums[1], *state),
+        (core, *sums[1], stat, *state),
         scratch((2 * HALVES[1] + 8 * B, B), (8, B), tile)
         + wide((B, 6 * B))
         + scratch(tile, (14 * B, B), (8, 256, B))

time: 120 us -> 132 us (1.10)
  waiting for transfers between devices: 36.4 us -> 58.8 us
  starting transfers between devices: 46.4 us -> 38.5 us
  Pallas kernels: 34.2 us -> 32.3 us
    ppermute x40 -> x32, waiting for transfers between devices: 36.4 us -> 58.8 us  [permute(): return lax.ppermute(x, AXES, [(n, to(n)) for n in range(128)])]
    ppermute x40 -> x32, starting transfers between devices: 46.4 us -> 38.5 us  [permute(): return lax.ppermute(x, AXES, [(n, to(n)) for n in range(128)])]
    pallas_call x7 -> x8, Pallas kernels: 34.2 us -> 32.3 us  [call(): pl.pallas_call(kernel, out_shape=outs, in_specs=[SMEM] * scalars + [VMEM]...]
  transfers between devices with their start and end apart: 40 -> 32, of which waited for: 14 -> 15; matrix products, arithmetic and copies ran while one was open for 1% -> 1% of each run, Pallas kernels for 9% -> 7%
where the time goes in v3:
time: 132 us
  waiting for transfers between devices  58.8 us (45%)
  starting transfers between devices  38.5 us (29%)
  Pallas kernels  32.3 us (24%)
  other arithmetic  1.37 us (1%)
    ppermute x32, waiting for transfers between devices, permute(): return lax.ppermute(x, AXES, [(n, to(n)) for n in range(128)])  58.8 us
    ppermute x32, starting transfers between devices, permute(): return lax.ppermute(x, AXES, [(n, to(n)) for n in range(128)])  38.5 us
    pallas_call x8, Pallas kernels, call(): pl.pallas_call(kernel, out_shape=outs, in_specs=[SMEM] * scalars + [VMEM]...  32.3 us
  transfers between devices with their start and end apart: 32, of which 15 were waited for; matrix products, arithmetic and copies ran while one was open for 1% of the time, Pallas kernels for 7%

profile of v3, /device:TPU:1, one launch (start us, length us, event | category | flops | bytes accessed | tf_op | source)
XLA Modules:
  0.0 132.2 jit_solution(2672955404101412908)
XLA Ops:
  0.0 1.4 %collective-permute-start.1 = (f32[128,1024]{1,0:T(8,128)}, f32[128,1024]{1,0:T(8,128)S(1)}, u32[]{:S(2)}, u32[]{:S(2)}) collective-permute-start(f32[128,1024]{1,0:T(8,128)} %x_ref.1), channel_id=1, source_target_pairs={{0,16},{1,17},{2,18},{3,19},{4,20},{5,21},{6,22},{7,23},{8,24},{9,... | collective-permute-start | bytes 1572872 | tf_op jit(solution)/shard_map/ppermute | solution.py:47
  5.2 6.4 %collective-permute-start.2 = (f32[64,1024]{1,0:T(8,128)S(1)}, f32[64,1024]{1,0:T(8,128)S(1)}, u32[]{:S(2)}, u32[]{:S(2)}) collective-permute-start(f32[64,1024]{1,0:T(8,128)S(1)} %get-tuple-element.29), channel_id=1, source_target_pairs={{0,111},{1,110},{2,109},{3,108},{4,107},{5,106},{6,105},{7,104},{8... | collective-permute-start | bytes 786440 | tf_op jit(solution)/shard_map/ppermute | solution.py:47
  11.6 3.0 %collective-permute-start.3 = (f32[64,1024]{1,0:T(8,128)S(1)}, f32[64,1024]{1,0:T(8,128)S(1)}, u32[]{:S(2)}, u32[]{:S(2)}) collective-permute-start(f32[64,1024]{1,0:T(8,128)S(1)} %get-tuple-element.30), channel_id=1, source_target_pairs={{0,0},{1,1},{2,2},{3,3},{4,4},{5,5},{6,6},{7,7},{8,8},{9,9},{10,10... | collective-permute-start | bytes 786440 | tf_op jit(solution)/shard_map/ppermute | solution.py:47
  14.6 1.4 %collective-permute-start.4 = (f32[64,1024]{1,0:T(8,128)S(1)}, f32[64,1024]{1,0:T(8,128)S(1)}, u32[]{:S(2)}, u32[]{:S(2)}) collective-permute-start(f32[64,1024]{1,0:T(8,128)S(1)} %get-tuple-element.31), channel_id=1, source_target_pairs={{0,12},{1,13},{2,14},{3,15},{4,8},{5,9},{6,10},{7,11},{8,4},{9,5},... | collective-permute-start | bytes 786440 | tf_op jit(solution)/shard_map/ppermute | solution.py:47
  16.0 2.5 %collective-permute-start.5 = (f32[64,1024]{1,0:T(8,128)S(1)}, f32[64,1024]{1,0:T(8,128)S(1)}, u32[]{:S(2)}, u32[]{:S(2)}) collective-permute-start(f32[64,1024]{1,0:T(8,128)S(1)} %get-tuple-element.32), channel_id=1, source_target_pairs={{0,3},{1,2},{2,1},{3,0},{4,7},{5,6},{6,5},{7,4},{8,11},{9,10},{10,... | collective-permute-start | bytes 786440 | tf_op jit(solution)/shard_map/ppermute | solution.py:47
  18.5 5.2 %collective-permute-done.3.refs_1_.refs_5_ = f32[64,1024]{1,0:T(8,128)S(1)} collective-permute-done((f32[64,1024]{1,0:T(8,128)S(1)}, f32[64,1024]{1,0:T(8,128)S(1)}, u32[]{:S(2)}, u32[]{:S(2)}) %collective-permute-start.3) | collective-permute-done | bytes 262176 | tf_op jit(solution)/shard_map/ppermute | solution.py:47
  23.7 3.0 %collective-permute-done.4.refs_2_.refs_6_ = f32[64,1024]{1,0:T(8,128)S(1)} collective-permute-done((f32[64,1024]{1,0:T(8,128)S(1)}, f32[64,1024]{1,0:T(8,128)S(1)}, u32[]{:S(2)}, u32[]{:S(2)}) %collective-permute-start.4) | collective-permute-done | bytes 262176 | tf_op jit(solution)/shard_map/ppermute | solution.py:47
  26.8 1.8 %shard_map.39 = (f32[1344,128]{1,0:T(8,128)S(1)}, f32[1344,128]{1,0:T(8,128)S(1)}) custom-call(s32[1]{0:T(128)} %bitcast.core_ref, f32[64,1024]{1,0:T(8,128)S(1)} %collective-permute-done.2.refs_0_.refs_4_, f32[64,1024]{1,0:T(8,128)S(1)} %collective-permute-done.3.refs_1_.refs_5_, f32[64,1024]{1,0:T(8,128)S(1)} %collective-permute-done.4.refs_2_.refs_6_, ...), custom_call_target="tpu_custom_call" | custom-call | flops 1000000 | bytes 4000000 | tf_op jit(solution)/shard_map/pallas_call | solution.py:471
  32.5 9.6 %collective-permute-done.16 = f32[648,128]{1,0:T(8,128)S(1)} collective-permute-done((f32[648,128]{1,0:T(8,128)S(1)}, f32[648,128]{1,0:T(8,128)S(1)}, u32[]{:S(2)}, u32[]{:S(2)}) %collective-permute-start.16) | collective-permute-done | bytes 331808 | tf_op jit(solution)/shard_map/ppermute | solution.py:47
  42.3 1.5 %collective-permute-start.8 = (f32[896,128]{1,0:T(8,128)S(1)}, f32[896,128]{1,0:T(8,128)S(1)}, u32[]{:S(2)}, u32[]{:S(2)}) collective-permute-start(f32[896,128]{1,0:T(8,128)S(1)} %add.69), channel_id=1, source_target_pairs={{0,1},{1,0},{2,3},{3,2},{4,5},{5,4},{6,7},{7,6},{8,9},{9,8},{10,11... | collective-permute-start | bytes 1376264 | tf_op jit(solution)/shard_map/ppermute | solution.py:47
  44.0 4.5 %collective-permute-done.17 = f32[648,128]{1,0:T(8,128)S(1)} collective-permute-done((f32[648,128]{1,0:T(8,128)S(1)}, f32[648,128]{1,0:T(8,128)S(1)}, u32[]{:S(2)}, u32[]{:S(2)}) %collective-permute-start.17) | collective-permute-done | bytes 331808 | tf_op jit(solution)/shard_map/ppermute | solution.py:47
  49.2 15.9 %collective-permute-done.19 = f32[320,128]{1,0:T(8,128)S(1)} collective-permute-done((f32[320,128]{1,0:T(8,128)S(1)}, f32[320,128]{1,0:T(8,128)S(1)}, u32[]{:S(2)}, u32[]{:S(2)}) %collective-permute-start.19) | collective-permute-done | bytes 163872 | tf_op jit(solution)/shard_map/ppermute | solution.py:47
  67.5 3.9 %collective-permute-done.20 = f32[320,128]{1,0:T(8,128)S(1)} collective-permute-done((f32[320,128]{1,0:T(8,128)S(1)}, f32[320,128]{1,0:T(8,128)S(1)}, u32[]{:S(2)}, u32[]{:S(2)}) %collective-permute-start.20) | collective-permute-done | bytes 163872 | tf_op jit(solution)/shard_map/ppermute | solution.py:47
  71.6 4.7 %collective-permute-done.11 = f32[448,128]{1,0:T(8,128)S(1)} collective-permute-done((f32[448,128]{1,0:T(8,128)S(1)}, f32[448,128]{1,0:T(8,128)S(1)}, u32[]{:S(2)}, u32[]{:S(2)}) %collective-permute-start.11) | collective-permute-done | bytes 229408 | tf_op jit(solution)/shard_map/ppermute | solution.py:47
  76.9 1.4 %collective-permute-start.23 = (f32[320,128]{1,0:T(8,128)S(1)}, f32[320,128]{1,0:T(8,128)S(1)}, u32[]{:S(2)}, u32[]{:S(2)}) collective-permute-start(f32[320,128]{1,0:T(8,128)S(1)} %add.83.refs_1_), channel_id=1, source_target_pairs={{0,16},{1,17},{2,18},{3,19},{4,20},{5,21},{6,22},{7,23},{8,24},{9,... | collective-permute-start | bytes 491528 | tf_op jit(solution)/shard_map/ppermute | solution.py:47
  78.2 4.9 %collective-permute-done.12 = f32[448,128]{1,0:T(8,128)S(1)} collective-permute-done((f32[448,128]{1,0:T(8,128)S(1)}, f32[448,128]{1,0:T(8,128)S(1)}, u32[]{:S(2)}, u32[]{:S(2)}) %collective-permute-start.12) | collective-permute-done | bytes 229408 | tf_op jit(solution)/shard_map/ppermute | solution.py:47
  84.9 2.8 %shard_map.41 = (f32[1936,128]{1,0:T(8,128)S(1)}, f32[16,128]{1,0:T(8,128)S(1)}, f32[128,128]{1,0:T(8,128)S(1)}, f32[8,256,128]{2,1,0:T(8,128)S(1)}) custom-call(s32[1]{0:T(128)} %bitcast.core_ref, f32[648,128]{1,0:T(8,128)S(1)} %add.79.refs_0_, f32[320,128]{1,0:T(8,128)S(1)} %add.83.refs_1_, f32[648,128]{1,0:T(8,128)S(1)} %collective-permute-done.22.refs_2_, ...), custom_call_target="tpu_custom_call" | custom-call | flops 3000000000 | bytes 4000000 | tf_op jit(solution)/shard_map/pallas_call | solution.py:471
  87.8 4.0 %shard_map.42 = (bf16[768,1536]{1,0:T(8,128)(2,1)S(1)}, bf16[768,1536]{1,0:T(8,128)(2,1)S(1)}, f32[6,256,128]{2,1,0:T(8,128)S(1)}, f32[2,256,128]{2,1,0:T(8,128)S(1)}) custom-call(f32[1936,128]{1,0:T(8,128)S(1)} %get-tuple-element.38.flat, f32[128,128]{1,0:T(8,128)S(1)} %get-tuple-element.39.inv0, f32[8,256,128]{2,1,0:T(8,128)S(1)} %get-tuple-element.40.x), custom_call_target="tpu_custom_call" | custom-call | flops 3000000000 | bytes 4000000 | tf_op jit(solution)/shard_map/pallas_call | solution.py:471
  91.8 19.2 %shard_map.43 = (f32[64,1024]{1,0:T(8,128)S(1)}, f32[64,1024]{1,0:T(8,128)S(1)}, f32[64,1024]{1,0:T(8,128)S(1)}, f32[64,1024]{1,0:T(8,128)S(1)}) custom-call(s32[1]{0:T(128)} %bitcast.core_ref, f32[896,128]{1,0:T(8,128)S(1)} %add.71.refs_0_, f32[448,128]{1,0:T(8,128)S(1)} %add.75.refs_1_, f32[896,128]{1,0:T(8,128)S(1)} %collective-permute-done.13.refs_2_, ...), custom_call_target="tpu_custom_call" | custom-call | flops 20000000000 | bytes 4000000 | tf_op jit(solution)/shard_map/pallas_call | solution.py:471
  111.0 2.1 %collective-permute-start.24 = (f32[64,1024]{1,0:T(8,128)S(1)}, f32[64,1024]{1,0:T(8,128)S(1)}, u32[]{:S(2)}, u32[]{:S(2)}) collective-permute-start(f32[64,1024]{1,0:T(8,128)S(1)} %get-tuple-element.45), channel_id=1, source_target_pairs={{0,111},{1,110},{2,109},{3,108},{4,107},{5,106},{6,105},{7,104},{8... | collective-permute-start | bytes 786440 | tf_op jit(solution)/shard_map/ppermute | solution.py:47
  113.2 6.8 %collective-permute-start.25 = (f32[64,1024]{1,0:T(8,128)S(1)}, f32[64,1024]{1,0:T(8,128)S(1)}, u32[]{:S(2)}, u32[]{:S(2)}) collective-permute-start(f32[64,1024]{1,0:T(8,128)S(1)} %get-tuple-element.46), channel_id=1, source_target_pairs={{0,0},{1,1},{2,2},{3,3},{4,4},{5,5},{6,6},{7,7},{8,8},{9,9},{10,10... | collective-permute-start | bytes 786440 | tf_op jit(solution)/shard_map/ppermute | solution.py:47
  120.6 4.4 %collective-permute-start.28 = (f32[64,1024]{1,0:T(8,128)S(1)}, f32[64,1024]{1,0:T(8,128)S(1)}, u32[]{:S(2)}, u32[]{:S(2)}) collective-permute-start(f32[64,1024]{1,0:T(8,128)S(1)} %collective-permute-done.24.refs_0_), channel_id=1, source_target_pairs={{0,16},{1,17},{2,18},{3,19},{4,20},{5,21},{6,22},{7,23},{8,24},{9,... | collective-permute-start | bytes 786440 | tf_op jit(solution)/shard_map/ppermute | solution.py:47
  125.1 1.5 %collective-permute-done.25.refs_1_ = f32[64,1024]{1,0:T(8,128)S(1)} collective-permute-done((f32[64,1024]{1,0:T(8,128)S(1)}, f32[64,1024]{1,0:T(8,128)S(1)}, u32[]{:S(2)}, u32[]{:S(2)}) %collective-permute-start.25) | collective-permute-done | bytes 262176 | tf_op jit(solution)/shard_map/ppermute | solution.py:47
  126.5 2.5 %collective-permute-done.26.refs_2_ = f32[64,1024]{1,0:T(8,128)S(1)} collective-permute-done((f32[64,1024]{1,0:T(8,128)S(1)}, f32[64,1024]{1,0:T(8,128)S(1)}, u32[]{:S(2)}, u32[]{:S(2)}) %collective-permute-start.26) | collective-permute-done | bytes 262176 | tf_op jit(solution)/shard_map/ppermute | solution.py:47
  (68 shorter events, 17.4 us)
Async XLA Ops:
  5.2 13.4 %collective-permute-start.2 = (f32[64,1024]{1,0:T(8,128)S(1)}, f32[64,1024]{1,0:T(8,128)S(1)}, u32[]{:S(2)}, u32[]{:S(2)}) collective-permute-start(f32[64,1024]{1,0:T(8,128)S(1)} %get-tuple-element.29), channel_id=1, source_target_pairs={{0,111},{1,110},{2,109},{3,108},{4,107},{5,106},{6,105},{7,104},{8... | collective-permute-start | bytes 786440 | tf_op jit(solution)/shard_map/ppermute | solution.py:47
  11.6 12.2 %collective-permute-start.3 = (f32[64,1024]{1,0:T(8,128)S(1)}, f32[64,1024]{1,0:T(8,128)S(1)}, u32[]{:S(2)}, u32[]{:S(2)}) collective-permute-start(f32[64,1024]{1,0:T(8,128)S(1)} %get-tuple-element.30), channel_id=1, source_target_pairs={{0,0},{1,1},{2,2},{3,3},{4,4},{5,5},{6,6},{7,7},{8,8},{9,9},{10,10... | collective-permute-start | bytes 786440 | tf_op jit(solution)/shard_map/ppermute | solution.py:47
  14.6 12.2 %collective-permute-start.4 = (f32[64,1024]{1,0:T(8,128)S(1)}, f32[64,1024]{1,0:T(8,128)S(1)}, u32[]{:S(2)}, u32[]{:S(2)}) collective-permute-start(f32[64,1024]{1,0:T(8,128)S(1)} %get-tuple-element.31), channel_id=1, source_target_pairs={{0,12},{1,13},{2,14},{3,15},{4,8},{5,9},{6,10},{7,11},{8,4},{9,5},... | collective-permute-start | bytes 786440 | tf_op jit(solution)/shard_map/ppermute | solution.py:47
  16.0 10.8 %collective-permute-start.5 = (f32[64,1024]{1,0:T(8,128)S(1)}, f32[64,1024]{1,0:T(8,128)S(1)}, u32[]{:S(2)}, u32[]{:S(2)}) collective-permute-start(f32[64,1024]{1,0:T(8,128)S(1)} %get-tuple-element.32), channel_id=1, source_target_pairs={{0,3},{1,2},{2,1},{3,0},{4,7},{5,6},{6,5},{7,4},{8,11},{9,10},{10,... | collective-permute-start | bytes 786440 | tf_op jit(solution)/shard_map/ppermute | solution.py:47
  30.9 11.4 %collective-permute-start.7 = (f32[896,128]{1,0:T(8,128)S(1)}, f32[896,128]{1,0:T(8,128)S(1)}, u32[]{:S(2)}, u32[]{:S(2)}) collective-permute-start(f32[896,128]{1,0:T(8,128)S(1)} %slice_add_fusion), channel_id=1, source_target_pairs={{0,4},{1,5},{2,6},{3,7},{4,0},{5,1},{6,2},{7,3},{8,12},{9,13},{10,... | collective-permute-start | bytes 1376264 | tf_op jit(solution)/shard_map/ppermute | solution.py:47
  32.0 10.1 %collective-permute-start.16 = (f32[648,128]{1,0:T(8,128)S(1)}, f32[648,128]{1,0:T(8,128)S(1)}, u32[]{:S(2)}, u32[]{:S(2)}) collective-permute-start(f32[648,128]{1,0:T(8,128)S(1)} %slice_add_fusion.1), channel_id=1, source_target_pairs={{0,4},{1,5},{2,6},{3,7},{4,0},{5,1},{6,2},{7,3},{8,12},{9,13},{10,... | collective-permute-start | bytes 995336 | tf_op jit(solution)/shard_map/ppermute | solution.py:47
  42.2 6.3 %collective-permute-start.17 = (f32[648,128]{1,0:T(8,128)S(1)}, f32[648,128]{1,0:T(8,128)S(1)}, u32[]{:S(2)}, u32[]{:S(2)}) collective-permute-start(f32[648,128]{1,0:T(8,128)S(1)} %add.77), channel_id=1, source_target_pairs={{0,1},{1,0},{2,3},{3,2},{4,5},{5,4},{6,7},{7,6},{8,9},{9,8},{10,11... | collective-permute-start | bytes 995336 | tf_op jit(solution)/shard_map/ppermute | solution.py:47
  42.3 24.5 %collective-permute-start.8 = (f32[896,128]{1,0:T(8,128)S(1)}, f32[896,128]{1,0:T(8,128)S(1)}, u32[]{:S(2)}, u32[]{:S(2)}) collective-permute-start(f32[896,128]{1,0:T(8,128)S(1)} %add.69), channel_id=1, source_target_pairs={{0,1},{1,0},{2,3},{3,2},{4,5},{5,4},{6,7},{7,6},{8,9},{9,8},{10,11... | collective-permute-start | bytes 1376264 | tf_op jit(solution)/shard_map/ppermute | solution.py:47
  43.9 21.7 %collective-permute-start.10 = (f32[448,128]{1,0:T(8,128)S(1)}, f32[448,128]{1,0:T(8,128)S(1)}, u32[]{:S(2)}, u32[]{:S(2)}) collective-permute-start(f32[448,128]{1,0:T(8,128)S(1)} %slice_add_fusion.2), channel_id=1, source_target_pairs={{0,32},{1,33},{2,34},{3,35},{4,36},{5,37},{6,38},{7,39},{8,40},{9,... | collective-permute-start | bytes 688136 | tf_op jit(solution)/shard_map/ppermute | solution.py:47
  48.6 18.8 %collective-permute-start.18 = (f32[648,128]{1,0:T(8,128)S(1)}, f32[648,128]{1,0:T(8,128)S(1)}, u32[]{:S(2)}, u32[]{:S(2)}) collective-permute-start(f32[648,128]{1,0:T(8,128)S(1)} %add.78), channel_id=1, source_target_pairs={{0,32},{1,33},{2,34},{3,35},{4,36},{5,37},{6,38},{7,39},{8,40},{9,... | collective-permute-start | bytes 995336 | tf_op jit(solution)/shard_map/ppermute | solution.py:47
  49.1 16.0 %collective-permute-start.19 = (f32[320,128]{1,0:T(8,128)S(1)}, f32[320,128]{1,0:T(8,128)S(1)}, u32[]{:S(2)}, u32[]{:S(2)}) collective-permute-start(f32[320,128]{1,0:T(8,128)S(1)} %slice_add_fusion.3), channel_id=1, source_target_pairs={{0,32},{1,33},{2,34},{3,35},{4,36},{5,37},{6,38},{7,39},{8,40},{9,... | collective-permute-start | bytes 491528 | tf_op jit(solution)/shard_map/ppermute | solution.py:47
  65.1 6.3 %collective-permute-start.20 = (f32[320,128]{1,0:T(8,128)S(1)}, f32[320,128]{1,0:T(8,128)S(1)}, u32[]{:S(2)}, u32[]{:S(2)}) collective-permute-start(f32[320,128]{1,0:T(8,128)S(1)} %add.81), channel_id=1, source_target_pairs={{0,4},{1,5},{2,6},{3,7},{4,0},{5,1},{6,2},{7,3},{8,12},{9,13},{10,... | collective-permute-start | bytes 491528 | tf_op jit(solution)/shard_map/ppermute | solution.py:47
  65.6 10.7 %collective-permute-start.11 = (f32[448,128]{1,0:T(8,128)S(1)}, f32[448,128]{1,0:T(8,128)S(1)}, u32[]{:S(2)}, u32[]{:S(2)}) collective-permute-start(f32[448,128]{1,0:T(8,128)S(1)} %add.73), channel_id=1, source_target_pairs={{0,4},{1,5},{2,6},{3,7},{4,0},{5,1},{6,2},{7,3},{8,12},{9,13},{10,... | collective-permute-start | bytes 688136 | tf_op jit(solution)/shard_map/ppermute | solution.py:47
  66.9 17.7 %collective-permute-start.9 = (f32[896,128]{1,0:T(8,128)S(1)}, f32[896,128]{1,0:T(8,128)S(1)}, u32[]{:S(2)}, u32[]{:S(2)}) collective-permute-start(f32[896,128]{1,0:T(8,128)S(1)} %add.70), channel_id=1, source_target_pairs={{0,32},{1,33},{2,34},{3,35},{4,36},{5,37},{6,38},{7,39},{8,40},{9,... | collective-permute-start | bytes 1376264 | tf_op jit(solution)/shard_map/ppermute | solution.py:47
  67.4 17.5 %collective-permute-start.22 = (f32[648,128]{1,0:T(8,128)S(1)}, f32[648,128]{1,0:T(8,128)S(1)}, u32[]{:S(2)}, u32[]{:S(2)}) collective-permute-start(f32[648,128]{1,0:T(8,128)S(1)} %add.79.refs_0_), channel_id=1, source_target_pairs={{0,16},{1,17},{2,18},{3,19},{4,20},{5,21},{6,22},{7,23},{8,24},{9,... | collective-permute-start | bytes 995336 | tf_op jit(solution)/shard_map/ppermute | solution.py:47
  76.4 6.8 %collective-permute-start.12 = (f32[448,128]{1,0:T(8,128)S(1)}, f32[448,128]{1,0:T(8,128)S(1)}, u32[]{:S(2)}, u32[]{:S(2)}) collective-permute-start(f32[448,128]{1,0:T(8,128)S(1)} %add.74), channel_id=1, source_target_pairs={{0,1},{1,0},{2,3},{3,2},{4,5},{5,4},{6,7},{7,6},{8,9},{9,8},{10,11... | collective-permute-start | bytes 688136 | tf_op jit(solution)/shard_map/ppermute | solution.py:47
  76.9 8.0 %collective-permute-start.23 = (f32[320,128]{1,0:T(8,128)S(1)}, f32[320,128]{1,0:T(8,128)S(1)}, u32[]{:S(2)}, u32[]{:S(2)}) collective-permute-start(f32[320,128]{1,0:T(8,128)S(1)} %add.83.refs_1_), channel_id=1, source_target_pairs={{0,16},{1,17},{2,18},{3,19},{4,20},{5,21},{6,22},{7,23},{8,24},{9,... | collective-permute-start | bytes 491528 | tf_op jit(solution)/shard_map/ppermute | solution.py:47
  83.2 8.6 %collective-permute-start.14 = (f32[448,128]{1,0:T(8,128)S(1)}, f32[448,128]{1,0:T(8,128)S(1)}, u32[]{:S(2)}, u32[]{:S(2)}) collective-permute-start(f32[448,128]{1,0:T(8,128)S(1)} %add.75.refs_1_), channel_id=1, source_target_pairs={{0,16},{1,17},{2,18},{3,19},{4,20},{5,21},{6,22},{7,23},{8,24},{9,... | collective-permute-start | bytes 688136 | tf_op jit(solution)/shard_map/ppermute | solution.py:47
  84.6 7.2 %collective-permute-start.13 = (f32[896,128]{1,0:T(8,128)S(1)}, f32[896,128]{1,0:T(8,128)S(1)}, u32[]{:S(2)}, u32[]{:S(2)}) collective-permute-start(f32[896,128]{1,0:T(8,128)S(1)} %add.71.refs_0_), channel_id=1, source_target_pairs={{0,16},{1,17},{2,18},{3,19},{4,20},{5,21},{6,22},{7,23},{8,24},{9,... | collective-permute-start | bytes 1376264 | tf_op jit(solution)/shard_map/ppermute | solution.py:47
  111.0 9.6 %collective-permute-start.24 = (f32[64,1024]{1,0:T(8,128)S(1)}, f32[64,1024]{1,0:T(8,128)S(1)}, u32[]{:S(2)}, u32[]{:S(2)}) collective-permute-start(f32[64,1024]{1,0:T(8,128)S(1)} %get-tuple-element.45), channel_id=1, source_target_pairs={{0,111},{1,110},{2,109},{3,108},{4,107},{5,106},{6,105},{7,104},{8... | collective-permute-start | bytes 786440 | tf_op jit(solution)/shard_map/ppermute | solution.py:47
  113.2 13.4 %collective-permute-start.25 = (f32[64,1024]{1,0:T(8,128)S(1)}, f32[64,1024]{1,0:T(8,128)S(1)}, u32[]{:S(2)}, u32[]{:S(2)}) collective-permute-start(f32[64,1024]{1,0:T(8,128)S(1)} %get-tuple-element.46), channel_id=1, source_target_pairs={{0,0},{1,1},{2,2},{3,3},{4,4},{5,5},{6,6},{7,7},{8,8},{9,9},{10,10... | collective-permute-start | bytes 786440 | tf_op jit(solution)/shard_map/ppermute | solution.py:47
  120.0 9.0 %collective-permute-start.26 = (f32[64,1024]{1,0:T(8,128)S(1)}, f32[64,1024]{1,0:T(8,128)S(1)}, u32[]{:S(2)}, u32[]{:S(2)}) collective-permute-start(f32[64,1024]{1,0:T(8,128)S(1)} %get-tuple-element.47), channel_id=1, source_target_pairs={{0,12},{1,13},{2,14},{3,15},{4,8},{5,9},{6,10},{7,11},{8,4},{9,5},... | collective-permute-start | bytes 786440 | tf_op jit(solution)/shard_map/ppermute | solution.py:47
  120.3 8.7 %collective-permute-start.27 = (f32[64,1024]{1,0:T(8,128)S(1)}, f32[64,1024]{1,0:T(8,128)S(1)}, u32[]{:S(2)}, u32[]{:S(2)}) collective-permute-start(f32[64,1024]{1,0:T(8,128)S(1)} %get-tuple-element.48), channel_id=1, source_target_pairs={{0,3},{1,2},{2,1},{3,0},{4,7},{5,6},{6,5},{7,4},{8,11},{9,10},{10,... | collective-permute-start | bytes 786440 | tf_op jit(solution)/shard_map/ppermute | solution.py:47
  120.6 8.9 %collective-permute-start.28 = (f32[64,1024]{1,0:T(8,128)S(1)}, f32[64,1024]{1,0:T(8,128)S(1)}, u32[]{:S(2)}, u32[]{:S(2)}) collective-permute-start(f32[64,1024]{1,0:T(8,128)S(1)} %collective-permute-done.24.refs_0_), channel_id=1, source_target_pairs={{0,16},{1,17},{2,18},{3,19},{4,20},{5,21},{6,22},{7,23},{8,24},{9,... | collective-permute-start | bytes 786440 | tf_op jit(solution)/shard_map/ppermute | solution.py:47
  (9 other events, 24.1 us)

commit v4 on v3

--- a/solution.py
+++ b/solution.py
@@ -125,6 +125,16 @@
 STAT = len(PLACE_IN[0]) * B
 HALVES = ((STAT + 16) // 2, len(PLACE_IN[1]) * B // 2)
 CUTS = ((0, 648, 968), (0, 896, 1344))
+
+
+def rows_of(chunk, info_ref, which, part, place):
+    start, end = CUTS[chunk][part], CUTS[chunk][part + 1]
+    first, size = which * HALVES[chunk] + start, end - start
+    if chunk == 1:
+        size //= 2
+        bit = info_ref[1 + which] if part == 0 else info_ref[3]
+        first += (place ^ bit) * size
+    return pl.ds(pl.multiple_of(first, 8), size)
 
 
 def gram_kernel(chunk, core_ref, *refs):
@@ -147,9 +157,13 @@
         for c in range(2):
             n = PLACE_IN[chunk][k + c, k + c] * B
             flat[n : n + (8 - k - c) * B, :] = two[c * B :, c * B : (c + 1) * B]
-    half = HALVES[chunk]
     for ref, which in ((mine_ref, core_ref[0]), (other_ref, 1 - core_ref[0])):
-        ref[...] = flat[pl.ds(pl.multiple_of(which * half, 8), half), :]
+        row = 0
+        for part in range(2):
+            for place in range(1 + chunk):
+                rows = rows_of(chunk, core_ref, which, part, place)
+                ref[row : row + rows.size, :] = flat[rows, :]
+                row += rows.size
 
 
 def row_of(x, j):
@@ -269,10 +283,9 @@
         between[g + 1]()
 
 
-def gather_chunk(chunk, core, refs, flat):
-    for which, ref in enumerate(refs):
-        start = (which // 2 ^ core) * HALVES[chunk] + CUTS[chunk][which % 2]
-        flat[pl.ds(pl.multiple_of(start, 8), ref.shape[0]), :] = ref[...]
+def gather_chunk(chunk, info_ref, refs, flat):
+    for n, ref in enumerate(refs):
+        flat[rows_of(chunk, info_ref, n // (len(refs) // 2) ^ info_ref[0], n % 2, n // 2 % 2), :] = ref[...]
 
 
 def make_covariance(chunk, flat, mean, scale):
@@ -307,7 +320,7 @@
 
 def column0_kernel(core_ref, *refs):
     parts_refs, rows_refs, (flat, stat_ref, inv, x_ref), (ones,) = refs[:4], refs[4:8], refs[8:12], refs[12:]
-    gather_chunk(0, core_ref[0], parts_refs, flat)
+    gather_chunk(0, core_ref, parts_refs, flat)
     scale = 1.0 / flat[STAT + 8 : STAT + 16, :]
     mean = flat[STAT : STAT + 8, :] * scale
     stat_ref[0:8, :] = mean
@@ -370,11 +383,10 @@
 
 
 def second_kernel(core_ref, *refs):
-    parts_refs, (stat_ref, first_l, first_rr, x_ref, z_ref), out_refs = refs[:4], refs[4:9], refs[9:13]
-    flat, ones, inv, inv_r, diagonal, panel, x, z_l, rows_l, rows_r, white = refs[13:]
-    core = core_ref[0]
+    parts_refs, (stat_ref, first_l, first_rr, x_ref, z_ref), out_refs = refs[:8], refs[8:13], refs[13:17]
+    flat, ones, inv, inv_r, diagonal, panel, x, z_l, rows_l, rows_r, white = refs[17:]
     at = PLACE_IN[1]
-    gather_chunk(1, core, parts_refs, flat)
+    gather_chunk(1, core_ref, parts_refs, flat)
     make_covariance(1, flat, stat_ref[0:8, :], stat_ref[8:16, :])
     ones[...] = jnp.ones((8, B), jnp.float32)
     diagonal[...] = flat[0:B, :] - product(first_l[0:B, :], first_rr[0:B, :])
@@ -492,6 +504,7 @@
 
     ids = domain_ids.reshape(1, B)
     where = jnp.concatenate([core, home])
+    info = jnp.concatenate([core, jnp.stack([w // 4 % 2, w % 2, d // 2 % 2]).astype(jnp.int32)])
     their_rows = swap(embeddings)
     own, sel = call(
         pack_kernel,
@@ -513,7 +526,7 @@
         return call(
             functools.partial(gram_kernel, chunk),
             [f32(half, B)] * 2,
-            (core, *rows),
+            (info, *rows),
             scratch((256, 1024)) + wide((1024, 1536)) + scratch((2 * half, B)),
         )
 
@@ -524,20 +537,24 @@
     for chunk in range(2):
         grams.append(gram(chunk))
 
-    sums = []
+    def doubled(mine, sent, turn, i):
+        theirs = across(sent, turn, i)
+        return mine + theirs
+
+    sums, sent = [], []
     for chunk, (mine, other) in enumerate(grams):
         other = swap(other)
-        sums.append([mine[lo:hi] + other[lo:hi] for lo, hi in zip(CUTS[chunk], CUTS[chunk][1:])])
-
-    def doubled(x, turn, i):
-        partners = across(x, turn, i)
-        return x + partners
-
+        spans = list(zip(CUTS[chunk], CUTS[chunk][1:]))
+        kept = [(lo, (lo + hi) // 2 if chunk else hi) for lo, hi in spans]
+        sums.append([mine[lo:hi] + other[lo:hi] for lo, hi in kept])
+        sent.append([mine[lo:hi] + other[lo:hi] for (_, lo), (_, hi) in zip(kept, spans)] if chunk else sums[0])
     for turn in range(3):
-        sums = [[doubled(x, turn, i) for i, x in enumerate(parts)] for parts in sums]
+        sums = [[doubled(sums[chunk][i], sent[chunk][i], turn, i) for i in range(2)] for chunk in range(2)]
+        sent = sums
+    sums[1] = sums[1] + [across(x, 0, i) for i, x in enumerate(sums[1])]
     for parts in sums:
-        for i in range(2):
-            parts.append(swap(parts[i]))
+        for x in parts[:]:
+            parts.append(swap(x))
     tile, tall = (B, B), (6 * B, B)
 
     def bf16(*shape):
@@ -546,7 +563,7 @@
     flat, stat, inv, x = call(
         column0_kernel,
         [f32(STAT + 16, B), f32(16, B), f32(*tile), f32(8, 256, B)],
-        (core, *sums[0], *rows),
+        (info, *sums[0], *rows),
         scratch((8, B)),
         flops=3000000000,
     )
@@ -566,7 +583,7 @@
     white = call(
         second_kernel,
         [f32(64, 1024)] * 4,
-        (core, *sums[1], stat, *state),
+        (info, *sums[1], stat, *state),
         scratch((2 * HALVES[1] + 8 * B, B), (8, B), tile)
         + wide((B, 6 * B))
         + scratch(tile, (14 * B, B), (8, 256, B))

time: 132 us -> 117 us (0.89)
  waiting for transfers between devices: 58.8 us -> 41.9 us
  Pallas kernels: 32.3 us -> 34.3 us
    ppermute x32 -> x36, waiting for transfers between devices: 58.8 us -> 41.9 us  [permute(): return lax.ppermute(x, AXES, [(n, to(n)) for n in range(128)])]
    pallas_call x8, Pallas kernels: 32.3 us -> 34.3 us  [call(): pl.pallas_call(kernel, out_shape=outs, in_specs=[SMEM] * scalars + [VMEM]...]
    ppermute x32 -> x36, starting transfers between devices: 38.5 us -> 38.2 us  [permute(): return lax.ppermute(x, AXES, [(n, to(n)) for n in range(128)])]
  transfers between devices with their start and end apart: 32 -> 36, of which waited for: 15 -> 18; matrix products, arithmetic and copies ran while one was open for 1% -> 1% of each run, Pallas kernels for 7% -> 9%
where the time goes in v4:
time: 117 us
  waiting for transfers between devices  41.9 us (36%)
  starting transfers between devices  38.2 us (33%)
  Pallas kernels  34.3 us (29%)
  other arithmetic  1.29 us (1%)
    ppermute x36, waiting for transfers between devices, permute(): return lax.ppermute(x, AXES, [(n, to(n)) for n in range(128)])  41.9 us
    ppermute x36, starting transfers between devices, permute(): return lax.ppermute(x, AXES, [(n, to(n)) for n in range(128)])  38.2 us
    pallas_call x8, Pallas kernels, call(): pl.pallas_call(kernel, out_shape=outs, in_specs=[SMEM] * scalars + [VMEM]...  34.3 us
  transfers between devices with their start and end apart: 36, of which 18 were waited for; matrix products, arithmetic and copies ran while one was open for 1% of the time, Pallas kernels for 9%

profile of v4, /device:TPU:1, one launch (start us, length us, event | category | flops | bytes accessed | tf_op | source)
XLA Modules:
  0.0 117.0 jit_solution(13490583973715547224)
XLA Ops:
  5.2 6.4 %collective-permute-start.2 = (f32[64,1024]{1,0:T(8,128)S(1)}, f32[64,1024]{1,0:T(8,128)S(1)}, u32[]{:S(2)}, u32[]{:S(2)}) collective-permute-start(f32[64,1024]{1,0:T(8,128)S(1)} %get-tuple-element.29), channel_id=1, source_target_pairs={{0,111},{1,110},{2,109},{3,108},{4,107},{5,106},{6,105},{7,104},{8... | collective-permute-start | bytes 786440 | tf_op jit(solution)/shard_map/ppermute | solution.py:47
  11.6 3.0 %collective-permute-start.3 = (f32[64,1024]{1,0:T(8,128)S(1)}, f32[64,1024]{1,0:T(8,128)S(1)}, u32[]{:S(2)}, u32[]{:S(2)}) collective-permute-start(f32[64,1024]{1,0:T(8,128)S(1)} %get-tuple-element.30), channel_id=1, source_target_pairs={{0,0},{1,1},{2,2},{3,3},{4,4},{5,5},{6,6},{7,7},{8,8},{9,9},{10,10... | collective-permute-start | bytes 786440 | tf_op jit(solution)/shard_map/ppermute | solution.py:47
  16.0 2.5 %collective-permute-start.5 = (f32[64,1024]{1,0:T(8,128)S(1)}, f32[64,1024]{1,0:T(8,128)S(1)}, u32[]{:S(2)}, u32[]{:S(2)}) collective-permute-start(f32[64,1024]{1,0:T(8,128)S(1)} %get-tuple-element.32), channel_id=1, source_target_pairs={{0,3},{1,2},{2,1},{3,0},{4,7},{5,6},{6,5},{7,4},{8,11},{9,10},{10,... | collective-permute-start | bytes 786440 | tf_op jit(solution)/shard_map/ppermute | solution.py:47
  18.6 5.1 %collective-permute-done.3.refs_1_.refs_5_ = f32[64,1024]{1,0:T(8,128)S(1)} collective-permute-done((f32[64,1024]{1,0:T(8,128)S(1)}, f32[64,1024]{1,0:T(8,128)S(1)}, u32[]{:S(2)}, u32[]{:S(2)}) %collective-permute-start.3) | collective-permute-done | bytes 262176 | tf_op jit(solution)/shard_map/ppermute | solution.py:47
  23.7 3.0 %collective-permute-done.4.refs_2_.refs_6_ = f32[64,1024]{1,0:T(8,128)S(1)} collective-permute-done((f32[64,1024]{1,0:T(8,128)S(1)}, f32[64,1024]{1,0:T(8,128)S(1)}, u32[]{:S(2)}, u32[]{:S(2)}) %collective-permute-start.4) | collective-permute-done | bytes 262176 | tf_op jit(solution)/shard_map/ppermute | solution.py:47
  26.8 1.7 %shard_map.40 = (f32[968,128]{1,0:T(8,128)S(1)}, f32[968,128]{1,0:T(8,128)S(1)}) custom-call(s32[4]{0:T(128)S(1)} %pad_add_fusion.2.core_ref, f32[64,1024]{1,0:T(8,128)S(1)} %collective-permute-done.2.refs_0_.refs_4_, f32[64,1024]{1,0:T(8,128)S(1)} %collective-permute-done.3.refs_1_.refs_5_, f32[64,1024]{1,0:T(8,128)S(1)} %collective-permute-done.4.refs_2_.refs_6_, ...), custom_call_target="tpu_custom_call" | custom-call | flops 1000000 | bytes 4000000 | tf_op jit(solution)/shard_map/pallas_call | solution.py:483
  28.6 2.3 %shard_map.39 = (f32[1344,128]{1,0:T(8,128)S(1)}, f32[1344,128]{1,0:T(8,128)S(1)}) custom-call(s32[4]{0:T(128)S(1)} %pad_add_fusion.2.core_ref, f32[64,1024]{1,0:T(8,128)S(1)} %collective-permute-done.2.refs_0_.refs_4_, f32[64,1024]{1,0:T(8,128)S(1)} %collective-permute-done.3.refs_1_.refs_5_, f32[64,1024]{1,0:T(8,128)S(1)} %collective-permute-done.4.refs_2_.refs_6_, ...), custom_call_target="tpu_custom_call" | custom-call | flops 1000000 | bytes 4000000 | tf_op jit(solution)/shard_map/pallas_call | solution.py:483
  31.7 1.6 %collective-permute-done.6 = f32[1344,128]{1,0:T(8,128)S(1)} collective-permute-done((f32[1344,128]{1,0:T(8,128)S(1)}, f32[1344,128]{1,0:T(8,128)S(1)}, u32[]{:S(2)}, u32[]{:S(2)}) %collective-permute-start.6) | collective-permute-done | bytes 688160 | tf_op jit(solution)/shard_map/ppermute | solution.py:47
  33.6 4.3 %collective-permute-done.20 = f32[648,128]{1,0:T(8,128)S(1)} collective-permute-done((f32[648,128]{1,0:T(8,128)S(1)}, f32[648,128]{1,0:T(8,128)S(1)}, u32[]{:S(2)}, u32[]{:S(2)}) %collective-permute-start.20) | collective-permute-done | bytes 331808 | tf_op jit(solution)/shard_map/ppermute | solution.py:47
  38.0 2.3 %collective-permute-done.7 = f32[448,128]{1,0:T(8,128)S(1)} collective-permute-done((f32[448,128]{1,0:T(8,128)S(1)}, f32[448,128]{1,0:T(8,128)S(1)}, u32[]{:S(2)}, u32[]{:S(2)}) %collective-permute-start.7) | collective-permute-done | bytes 229408 | tf_op jit(solution)/shard_map/ppermute | solution.py:47
  42.1 2.2 %collective-permute-done.21 = f32[648,128]{1,0:T(8,128)S(1)} collective-permute-done((f32[648,128]{1,0:T(8,128)S(1)}, f32[648,128]{1,0:T(8,128)S(1)}, u32[]{:S(2)}, u32[]{:S(2)}) %collective-permute-start.21) | collective-permute-done | bytes 331808 | tf_op jit(solution)/shard_map/ppermute | solution.py:47
  46.0 2.0 %collective-permute-done.8 = f32[448,128]{1,0:T(8,128)S(1)} collective-permute-done((f32[448,128]{1,0:T(8,128)S(1)}, f32[448,128]{1,0:T(8,128)S(1)}, u32[]{:S(2)}, u32[]{:S(2)}) %collective-permute-start.8) | collective-permute-done | bytes 229408 | tf_op jit(solution)/shard_map/ppermute | solution.py:47
  49.7 2.3 %collective-permute-done.22 = f32[648,128]{1,0:T(8,128)S(1)} collective-permute-done((f32[648,128]{1,0:T(8,128)S(1)}, f32[648,128]{1,0:T(8,128)S(1)}, u32[]{:S(2)}, u32[]{:S(2)}) %collective-permute-start.22) | collective-permute-done | bytes 331808 | tf_op jit(solution)/shard_map/ppermute | solution.py:47
  53.4 2.0 %collective-permute-done.24 = f32[320,128]{1,0:T(8,128)S(1)} collective-permute-done((f32[320,128]{1,0:T(8,128)S(1)}, f32[320,128]{1,0:T(8,128)S(1)}, u32[]{:S(2)}, u32[]{:S(2)}) %collective-permute-start.24) | collective-permute-done | bytes 163872 | tf_op jit(solution)/shard_map/ppermute | solution.py:47
  55.6 3.5 %collective-permute-done.11 = f32[224,128]{1,0:T(8,128)S(1)} collective-permute-done((f32[224,128]{1,0:T(8,128)S(1)}, f32[224,128]{1,0:T(8,128)S(1)}, u32[]{:S(2)}, u32[]{:S(2)}) %collective-permute-start.11) | collective-permute-done | bytes 114720 | tf_op jit(solution)/shard_map/ppermute | solution.py:47
  63.4 4.0 %collective-permute-done.14.refs_3_ = f32[224,128]{1,0:T(8,128)S(1)} collective-permute-done((f32[224,128]{1,0:T(8,128)S(1)}, f32[224,128]{1,0:T(8,128)S(1)}, u32[]{:S(2)}, u32[]{:S(2)}) %collective-permute-start.14) | collective-permute-done | bytes 114720 | tf_op jit(solution)/shard_map/ppermute | solution.py:47
  68.2 3.4 %shard_map.41 = (f32[1936,128]{1,0:T(8,128)S(1)}, f32[16,128]{1,0:T(8,128)S(1)}, f32[128,128]{1,0:T(8,128)S(1)}, f32[8,256,128]{2,1,0:T(8,128)S(1)}) custom-call(s32[4]{0:T(128)S(1)} %pad_add_fusion.2.core_ref, f32[648,128]{1,0:T(8,128)S(1)} %add.101.refs_0_, f32[320,128]{1,0:T(8,128)S(1)} %add.105.refs_1_, f32[648,128]{1,0:T(8,128)S(1)} %collective-permute-done.26.refs_2_, ...), custom_call_target="tpu_custom_call" | custom-call | flops 3000000000 | bytes 4000000 | tf_op jit(solution)/shard_map/pallas_call | solution.py:483
  71.5 4.0 %shard_map.42 = (bf16[768,1536]{1,0:T(8,128)(2,1)S(1)}, bf16[768,1536]{1,0:T(8,128)(2,1)S(1)}, f32[6,256,128]{2,1,0:T(8,128)S(1)}, f32[2,256,128]{2,1,0:T(8,128)S(1)}) custom-call(f32[1936,128]{1,0:T(8,128)S(1)} %get-tuple-element.38.flat, f32[128,128]{1,0:T(8,128)S(1)} %get-tuple-element.39.inv0, f32[8,256,128]{2,1,0:T(8,128)S(1)} %get-tuple-element.40.x), custom_call_target="tpu_custom_call" | custom-call | flops 3000000000 | bytes 4000000 | tf_op jit(solution)/shard_map/pallas_call | solution.py:483
  75.6 19.7 %shard_map.43 = (f32[64,1024]{1,0:T(8,128)S(1)}, f32[64,1024]{1,0:T(8,128)S(1)}, f32[64,1024]{1,0:T(8,128)S(1)}, f32[64,1024]{1,0:T(8,128)S(1)}) custom-call(s32[4]{0:T(128)S(1)} %pad_add_fusion.2.core_ref, f32[448,128]{1,0:T(8,128)S(1)} %add.92.refs_0_, f32[224,128]{1,0:T(8,128)S(1)} %add.97.refs_1_, f32[448,128]{1,0:T(8,128)S(1)} %collective-permute-done.13.refs_2_, ...), custom_call_target="tpu_custom_call" | custom-call | flops 20000000000 | bytes 4000000 | tf_op jit(solution)/shard_map/pallas_call | solution.py:483
  95.3 3.0 %collective-permute-start.28 = (f32[64,1024]{1,0:T(8,128)S(1)}, f32[64,1024]{1,0:T(8,128)S(1)}, u32[]{:S(2)}, u32[]{:S(2)}) collective-permute-start(f32[64,1024]{1,0:T(8,128)S(1)} %get-tuple-element.45), channel_id=1, source_target_pairs={{0,111},{1,110},{2,109},{3,108},{4,107},{5,106},{6,105},{7,104},{8... | collective-permute-start | bytes 786440 | tf_op jit(solution)/shard_map/ppermute | solution.py:47
  98.3 6.2 %collective-permute-start.29 = (f32[64,1024]{1,0:T(8,128)S(1)}, f32[64,1024]{1,0:T(8,128)S(1)}, u32[]{:S(2)}, u32[]{:S(2)}) collective-permute-start(f32[64,1024]{1,0:T(8,128)S(1)} %get-tuple-element.46), channel_id=1, source_target_pairs={{0,0},{1,1},{2,2},{3,3},{4,4},{5,5},{6,6},{7,7},{8,8},{9,9},{10,10... | collective-permute-start | bytes 786440 | tf_op jit(solution)/shard_map/ppermute | solution.py:47
  105.7 2.4 %collective-permute-start.32 = (f32[64,1024]{1,0:T(8,128)S(1)}, f32[64,1024]{1,0:T(8,128)S(1)}, u32[]{:S(2)}, u32[]{:S(2)}) collective-permute-start(f32[64,1024]{1,0:T(8,128)S(1)} %collective-permute-done.28.refs_0_), channel_id=1, source_target_pairs={{0,16},{1,17},{2,18},{3,19},{4,20},{5,21},{6,22},{7,23},{8,24},{9,... | collective-permute-start | bytes 786440 | tf_op jit(solution)/shard_map/ppermute | solution.py:47
  108.1 3.4 %collective-permute-done.29.refs_1_ = f32[64,1024]{1,0:T(8,128)S(1)} collective-permute-done((f32[64,1024]{1,0:T(8,128)S(1)}, f32[64,1024]{1,0:T(8,128)S(1)}, u32[]{:S(2)}, u32[]{:S(2)}) %collective-permute-start.29) | collective-permute-done | bytes 262176 | tf_op jit(solution)/shard_map/ppermute | solution.py:47
  111.5 2.3 %collective-permute-done.30.refs_2_ = f32[64,1024]{1,0:T(8,128)S(1)} collective-permute-done((f32[64,1024]{1,0:T(8,128)S(1)}, f32[64,1024]{1,0:T(8,128)S(1)}, u32[]{:S(2)}, u32[]{:S(2)}) %collective-permute-start.30) | collective-permute-done | bytes 262176 | tf_op jit(solution)/shard_map/ppermute | solution.py:47
  (77 shorter events, 24.0 us)
Async XLA Ops:
  5.2 13.4 %collective-permute-start.2 = (f32[64,1024]{1,0:T(8,128)S(1)}, f32[64,1024]{1,0:T(8,128)S(1)}, u32[]{:S(2)}, u32[]{:S(2)}) collective-permute-start(f32[64,1024]{1,0:T(8,128)S(1)} %get-tuple-element.29), channel_id=1, source_target_pairs={{0,111},{1,110},{2,109},{3,108},{4,107},{5,106},{6,105},{7,104},{8... | collective-permute-start | bytes 786440 | tf_op jit(solution)/shard_map/ppermute | solution.py:47
  11.6 12.2 %collective-permute-start.3 = (f32[64,1024]{1,0:T(8,128)S(1)}, f32[64,1024]{1,0:T(8,128)S(1)}, u32[]{:S(2)}, u32[]{:S(2)}) collective-permute-start(f32[64,1024]{1,0:T(8,128)S(1)} %get-tuple-element.30), channel_id=1, source_target_pairs={{0,0},{1,1},{2,2},{3,3},{4,4},{5,5},{6,6},{7,7},{8,8},{9,9},{10,10... | collective-permute-start | bytes 786440 | tf_op jit(solution)/shard_map/ppermute | solution.py:47
  14.6 12.2 %collective-permute-start.4 = (f32[64,1024]{1,0:T(8,128)S(1)}, f32[64,1024]{1,0:T(8,128)S(1)}, u32[]{:S(2)}, u32[]{:S(2)}) collective-permute-start(f32[64,1024]{1,0:T(8,128)S(1)} %get-tuple-element.31), channel_id=1, source_target_pairs={{0,12},{1,13},{2,14},{3,15},{4,8},{5,9},{6,10},{7,11},{8,4},{9,5},... | collective-permute-start | bytes 786440 | tf_op jit(solution)/shard_map/ppermute | solution.py:47
  16.0 10.8 %collective-permute-start.5 = (f32[64,1024]{1,0:T(8,128)S(1)}, f32[64,1024]{1,0:T(8,128)S(1)}, u32[]{:S(2)}, u32[]{:S(2)}) collective-permute-start(f32[64,1024]{1,0:T(8,128)S(1)} %get-tuple-element.32), channel_id=1, source_target_pairs={{0,3},{1,2},{2,1},{3,0},{4,7},{5,6},{6,5},{7,4},{8,11},{9,10},{10,... | collective-permute-start | bytes 786440 | tf_op jit(solution)/shard_map/ppermute | solution.py:47
  31.6 6.3 %collective-permute-start.20 = (f32[648,128]{1,0:T(8,128)S(1)}, f32[648,128]{1,0:T(8,128)S(1)}, u32[]{:S(2)}, u32[]{:S(2)}) collective-permute-start(f32[648,128]{1,0:T(8,128)S(1)} %slice_add_fusion), channel_id=1, source_target_pairs={{0,4},{1,5},{2,6},{3,7},{4,0},{5,1},{6,2},{7,3},{8,12},{9,13},{10,... | collective-permute-start | bytes 995336 | tf_op jit(solution)/shard_map/ppermute | solution.py:47
  33.3 7.0 %collective-permute-start.7 = (f32[448,128]{1,0:T(8,128)S(1)}, f32[448,128]{1,0:T(8,128)S(1)}, u32[]{:S(2)}, u32[]{:S(2)}) collective-permute-start(f32[448,128]{1,0:T(8,128)S(1)} %slice_add_fusion.1), channel_id=1, source_target_pairs={{0,4},{1,5},{2,6},{3,7},{4,0},{5,1},{6,2},{7,3},{8,12},{9,13},{10,... | collective-permute-start | bytes 688136 | tf_op jit(solution)/shard_map/ppermute | solution.py:47
  33.5 11.3 %collective-permute-start.23 = (f32[320,128]{1,0:T(8,128)S(1)}, f32[320,128]{1,0:T(8,128)S(1)}, u32[]{:S(2)}, u32[]{:S(2)}) collective-permute-start(f32[320,128]{1,0:T(8,128)S(1)} %slice_add_fusion.3), channel_id=1, source_target_pairs={{0,32},{1,33},{2,34},{3,35},{4,36},{5,37},{6,38},{7,39},{8,40},{9,... | collective-permute-start | bytes 491528 | tf_op jit(solution)/shard_map/ppermute | solution.py:47
  40.4 7.6 %collective-permute-start.8 = (f32[448,128]{1,0:T(8,128)S(1)}, f32[448,128]{1,0:T(8,128)S(1)}, u32[]{:S(2)}, u32[]{:S(2)}) collective-permute-start(f32[448,128]{1,0:T(8,128)S(1)} %fusion), channel_id=1, source_target_pairs={{0,1},{1,0},{2,3},{3,2},{4,5},{5,4},{6,7},{7,6},{8,9},{9,8},{10,11... | collective-permute-start | bytes 688136 | tf_op jit(solution)/shard_map/ppermute | solution.py:47
  40.5 8.4 %collective-permute-start.10 = (f32[224,128]{1,0:T(8,128)S(1)}, f32[224,128]{1,0:T(8,128)S(1)}, u32[]{:S(2)}, u32[]{:S(2)}) collective-permute-start(f32[224,128]{1,0:T(8,128)S(1)} %slice_add_fusion.4), channel_id=1, source_target_pairs={{0,32},{1,33},{2,34},{3,35},{4,36},{5,37},{6,38},{7,39},{8,40},{9,... | collective-permute-start | bytes 344072 | tf_op jit(solution)/shard_map/ppermute | solution.py:47
  44.3 7.6 %collective-permute-start.22 = (f32[648,128]{1,0:T(8,128)S(1)}, f32[648,128]{1,0:T(8,128)S(1)}, u32[]{:S(2)}, u32[]{:S(2)}) collective-permute-start(f32[648,128]{1,0:T(8,128)S(1)} %add.100), channel_id=1, source_target_pairs={{0,32},{1,33},{2,34},{3,35},{4,36},{5,37},{6,38},{7,39},{8,40},{9,... | collective-permute-start | bytes 995336 | tf_op jit(solution)/shard_map/ppermute | solution.py:47
  44.9 10.6 %collective-permute-start.24 = (f32[320,128]{1,0:T(8,128)S(1)}, f32[320,128]{1,0:T(8,128)S(1)}, u32[]{:S(2)}, u32[]{:S(2)}) collective-permute-start(f32[320,128]{1,0:T(8,128)S(1)} %add.103), channel_id=1, source_target_pairs={{0,4},{1,5},{2,6},{3,7},{4,0},{5,1},{6,2},{7,3},{8,12},{9,13},{10,... | collective-permute-start | bytes 491528 | tf_op jit(solution)/shard_map/ppermute | solution.py:47
  48.0 11.4 %collective-permute-start.9 = (f32[448,128]{1,0:T(8,128)S(1)}, f32[448,128]{1,0:T(8,128)S(1)}, u32[]{:S(2)}, u32[]{:S(2)}) collective-permute-start(f32[448,128]{1,0:T(8,128)S(1)} %add.91), channel_id=1, source_target_pairs={{0,32},{1,33},{2,34},{3,35},{4,36},{5,37},{6,38},{7,39},{8,40},{9,... | collective-permute-start | bytes 688136 | tf_op jit(solution)/shard_map/ppermute | solution.py:47
  48.9 10.2 %collective-permute-start.11 = (f32[224,128]{1,0:T(8,128)S(1)}, f32[224,128]{1,0:T(8,128)S(1)}, u32[]{:S(2)}, u32[]{:S(2)}) collective-permute-start(f32[224,128]{1,0:T(8,128)S(1)} %fusion.1), channel_id=1, source_target_pairs={{0,4},{1,5},{2,6},{3,7},{4,0},{5,1},{6,2},{7,3},{8,12},{9,13},{10,... | collective-permute-start | bytes 344072 | tf_op jit(solution)/shard_map/ppermute | solution.py:47
  52.0 16.2 %collective-permute-start.26 = (f32[648,128]{1,0:T(8,128)S(1)}, f32[648,128]{1,0:T(8,128)S(1)}, u32[]{:S(2)}, u32[]{:S(2)}) collective-permute-start(f32[648,128]{1,0:T(8,128)S(1)} %add.101.refs_0_), channel_id=1, source_target_pairs={{0,16},{1,17},{2,18},{3,19},{4,20},{5,21},{6,22},{7,23},{8,24},{9,... | collective-permute-start | bytes 995336 | tf_op jit(solution)/shard_map/ppermute | solution.py:47
  59.5 8.4 %collective-permute-start.13 = (f32[448,128]{1,0:T(8,128)S(1)}, f32[448,128]{1,0:T(8,128)S(1)}, u32[]{:S(2)}, u32[]{:S(2)}) collective-permute-start(f32[448,128]{1,0:T(8,128)S(1)} %add.92.refs_0_), channel_id=1, source_target_pairs={{0,4},{1,5},{2,6},{3,7},{4,0},{5,1},{6,2},{7,3},{8,12},{9,13},{10,... | collective-permute-start | bytes 688136 | tf_op jit(solution)/shard_map/ppermute | solution.py:47
  63.4 12.2 %collective-permute-start.16 = (f32[224,128]{1,0:T(8,128)S(1)}, f32[224,128]{1,0:T(8,128)S(1)}, u32[]{:S(2)}, u32[]{:S(2)}) collective-permute-start(f32[224,128]{1,0:T(8,128)S(1)} %add.97.refs_1_), channel_id=1, source_target_pairs={{0,16},{1,17},{2,18},{3,19},{4,20},{5,21},{6,22},{7,23},{8,24},{9,... | collective-permute-start | bytes 344072 | tf_op jit(solution)/shard_map/ppermute | solution.py:47
  67.4 8.2 %collective-permute-start.18 = (f32[224,128]{1,0:T(8,128)S(1)}, f32[224,128]{1,0:T(8,128)S(1)}, u32[]{:S(2)}, u32[]{:S(2)}) collective-permute-start(f32[224,128]{1,0:T(8,128)S(1)} %collective-permute-done.14.refs_3_), channel_id=1, source_target_pairs={{0,16},{1,17},{2,18},{3,19},{4,20},{5,21},{6,22},{7,23},{8,24},{9,... | collective-permute-start | bytes 344072 | tf_op jit(solution)/shard_map/ppermute | solution.py:47
  67.6 7.9 %collective-permute-start.15 = (f32[448,128]{1,0:T(8,128)S(1)}, f32[448,128]{1,0:T(8,128)S(1)}, u32[]{:S(2)}, u32[]{:S(2)}) collective-permute-start(f32[448,128]{1,0:T(8,128)S(1)} %add.92.refs_0_), channel_id=1, source_target_pairs={{0,16},{1,17},{2,18},{3,19},{4,20},{5,21},{6,22},{7,23},{8,24},{9,... | collective-permute-start | bytes 688136 | tf_op jit(solution)/shard_map/ppermute | solution.py:47
  67.9 7.7 %collective-permute-start.17 = (f32[448,128]{1,0:T(8,128)S(1)}, f32[448,128]{1,0:T(8,128)S(1)}, u32[]{:S(2)}, u32[]{:S(2)}) collective-permute-start(f32[448,128]{1,0:T(8,128)S(1)} %collective-permute-done.13.refs_2_), channel_id=1, source_target_pairs={{0,16},{1,17},{2,18},{3,19},{4,20},{5,21},{6,22},{7,23},{8,24},{9,... | collective-permute-start | bytes 688136 | tf_op jit(solution)/shard_map/ppermute | solution.py:47
  95.3 10.4 %collective-permute-start.28 = (f32[64,1024]{1,0:T(8,128)S(1)}, f32[64,1024]{1,0:T(8,128)S(1)}, u32[]{:S(2)}, u32[]{:S(2)}) collective-permute-start(f32[64,1024]{1,0:T(8,128)S(1)} %get-tuple-element.45), channel_id=1, source_target_pairs={{0,111},{1,110},{2,109},{3,108},{4,107},{5,106},{6,105},{7,104},{8... | collective-permute-start | bytes 786440 | tf_op jit(solution)/shard_map/ppermute | solution.py:47
  98.3 13.2 %collective-permute-start.29 = (f32[64,1024]{1,0:T(8,128)S(1)}, f32[64,1024]{1,0:T(8,128)S(1)}, u32[]{:S(2)}, u32[]{:S(2)}) collective-permute-start(f32[64,1024]{1,0:T(8,128)S(1)} %get-tuple-element.46), channel_id=1, source_target_pairs={{0,0},{1,1},{2,2},{3,3},{4,4},{5,5},{6,6},{7,7},{8,8},{9,9},{10,10... | collective-permute-start | bytes 786440 | tf_op jit(solution)/shard_map/ppermute | solution.py:47
  104.5 9.3 %collective-permute-start.30 = (f32[64,1024]{1,0:T(8,128)S(1)}, f32[64,1024]{1,0:T(8,128)S(1)}, u32[]{:S(2)}, u32[]{:S(2)}) collective-permute-start(f32[64,1024]{1,0:T(8,128)S(1)} %get-tuple-element.47), channel_id=1, source_target_pairs={{0,12},{1,13},{2,14},{3,15},{4,8},{5,9},{6,10},{7,11},{8,4},{9,5},... | collective-permute-start | bytes 786440 | tf_op jit(solution)/shard_map/ppermute | solution.py:47
  104.5 9.3 %collective-permute-start.31 = (f32[64,1024]{1,0:T(8,128)S(1)}, f32[64,1024]{1,0:T(8,128)S(1)}, u32[]{:S(2)}, u32[]{:S(2)}) collective-permute-start(f32[64,1024]{1,0:T(8,128)S(1)} %get-tuple-element.48), channel_id=1, source_target_pairs={{0,3},{1,2},{2,1},{3,0},{4,7},{5,6},{6,5},{7,4},{8,11},{9,10},{10,... | collective-permute-start | bytes 786440 | tf_op jit(solution)/shard_map/ppermute | solution.py:47
  105.7 8.6 %collective-permute-start.32 = (f32[64,1024]{1,0:T(8,128)S(1)}, f32[64,1024]{1,0:T(8,128)S(1)}, u32[]{:S(2)}, u32[]{:S(2)}) collective-permute-start(f32[64,1024]{1,0:T(8,128)S(1)} %collective-permute-done.28.refs_0_), channel_id=1, source_target_pairs={{0,16},{1,17},{2,18},{3,19},{4,20},{5,21},{6,22},{7,23},{8,24},{9,... | collective-permute-start | bytes 786440 | tf_op jit(solution)/shard_map/ppermute | solution.py:47
  (13 other events, 46.3 us)

commit v5 on v4

--- a/solution.py
+++ b/solution.py
@@ -47,6 +47,18 @@
     return lax.ppermute(x, AXES, [(n, to(n)) for n in range(128)])
 
 
+def core_of(place_ref):
+    return place_ref[0] & 1
+
+
+def bit_of(place_ref, axis):
+    return (place_ref[0] >> (1 + axis)) & 1
+
+
+def home_of(place_ref):
+    return place_ref[0] >> 4
+
+
 def iota(shape, axis):
     return lax.broadcasted_iota(jnp.int32, shape, axis)
 
@@ -85,11 +97,11 @@
 
 def group_and_rank(where_ref, ids):
     rows = ids.shape[1]
-    turned = ids ^ where_ref[1]
+    turned = ids ^ home_of(where_ref)
     group = jnp.zeros_like(turned)
     for place, mask in enumerate(CARRIED[0] + CARRIED[1]):
         group = jnp.where(turned == mask, place, group)
-    group = jnp.broadcast_to((group ^ (4 * where_ref[0])).astype(jnp.float32), (8, rows))
+    group = jnp.broadcast_to((group ^ (4 * core_of(where_ref))).astype(jnp.float32), (8, rows))
     onehot = jnp.where(group == iota((8, rows), 0).astype(jnp.float32), 1.0, 0.0)
     earlier = jnp.where(iota((rows, rows), 0) < iota((rows, rows), 1), 1.0, 0.0).astype(jnp.bfloat16)
     counted = plain(onehot.astype(jnp.bfloat16), earlier)
@@ -132,7 +144,7 @@
     first, size = which * HALVES[chunk] + start, end - start
     if chunk == 1:
         size //= 2
-        bit = info_ref[1 + which] if part == 0 else info_ref[3]
+        bit = bit_of(info_ref, which if part == 0 else 2)
         first += (place ^ bit) * size
     return pl.ds(pl.multiple_of(first, 8), size)
 
@@ -157,7 +169,7 @@
         for c in range(2):
             n = PLACE_IN[chunk][k + c, k + c] * B
             flat[n : n + (8 - k - c) * B, :] = two[c * B :, c * B : (c + 1) * B]
-    for ref, which in ((mine_ref, core_ref[0]), (other_ref, 1 - core_ref[0])):
+    for ref, which in ((mine_ref, core_of(core_ref)), (other_ref, 1 - core_of(core_ref))):
         row = 0
         for part in range(2):
             for place in range(1 + chunk):
@@ -285,7 +297,7 @@
 
 def gather_chunk(chunk, info_ref, refs, flat):
     for n, ref in enumerate(refs):
-        flat[rows_of(chunk, info_ref, n // (len(refs) // 2) ^ info_ref[0], n % 2, n // 2 % 2), :] = ref[...]
+        flat[rows_of(chunk, info_ref, n // (len(refs) // 2) ^ core_of(info_ref), n % 2, n // 2 % 2), :] = ref[...]
 
 
 def make_covariance(chunk, flat, mean, scale):
@@ -493,8 +505,8 @@
 
 def whiten(embeddings, domain_ids, order):
     d, w = lax.axis_index("dom"), lax.axis_index("wide")
-    core = (d % 2).reshape(1).astype(jnp.int32)
-    home = ((w // 8) * 4 + (w % 4) // 2 * 2 + d // 4).reshape(1).astype(jnp.int32)
+    home = (w // 8) * 4 + (w % 4) // 2 * 2 + d // 4
+    info = (d % 2 + w // 4 % 2 * 2 + w % 2 * 4 + d // 2 % 2 * 8 + home * 16).reshape(1).astype(jnp.int32)
 
     def swap(x):
         return permute(x, lambda n: partner(n, 3))
@@ -503,17 +515,15 @@
         return [permute(x, lambda n, turn=turn: toward(n, turn)) for turn, x in enumerate(arrays)]
 
     ids = domain_ids.reshape(1, B)
-    where = jnp.concatenate([core, home])
-    info = jnp.concatenate([core, jnp.stack([w // 4 % 2, w % 2, d // 2 % 2]).astype(jnp.int32)])
     their_rows = swap(embeddings)
     own, sel = call(
         pack_kernel,
         [f32(B, 1024), f32(B, B)],
-        (where, jnp.concatenate([ids, order]), embeddings),
+        (info, jnp.concatenate([ids, order]), embeddings),
         mib=12,
         flops=1000000000,
     )
-    rows = exchange(call(merge_kernel, [f32(64, 1024)] * 4, (where, swap(ids), their_rows, own), mib=12))
+    rows = exchange(call(merge_kernel, [f32(64, 1024)] * 4, (info, swap(ids), their_rows, own), mib=12))
 
     def scratch(*shapes, dtype=jnp.float32):
         return [pltpu.VMEM(shape, dtype) for shape in shapes]

time: 117 us -> 114 us (0.974)
  Pallas kernels: 34.3 us -> 31.4 us
    pallas_call x8, Pallas kernels: 34.3 us -> 31.4 us  [call(): pl.pallas_call(kernel, out_shape=outs, in_specs=[SMEM] * scalars + [VMEM]...]
  transfers between devices with their start and end apart: 36 -> 36, of which waited for: 18 -> 18; matrix products, arithmetic and copies ran while one was open for 1% -> 1% of each run, Pallas kernels for 9% -> 8%
where the time goes in v5:
time: 114 us
  waiting for transfers between devices  41.9 us (37%)
  starting transfers between devices  38.3 us (34%)
  Pallas kernels  31.4 us (28%)
    ppermute x36, waiting for transfers between devices, permute(): return lax.ppermute(x, AXES, [(n, to(n)) for n in range(128)])  41.9 us
    ppermute x36, starting transfers between devices, permute(): return lax.ppermute(x, AXES, [(n, to(n)) for n in range(128)])  38.3 us
    pallas_call x8, Pallas kernels, call(): pl.pallas_call(kernel, out_shape=outs, in_specs=[SMEM] * scalars + [VMEM]...  31.4 us
  transfers between devices with their start and end apart: 36, of which 18 were waited for; matrix products, arithmetic and copies ran while one was open for 1% of the time, Pallas kernels for 8%

profile of v5, /device:TPU:1, one launch (start us, length us, event | category | flops | bytes accessed | tf_op | source)
XLA Modules:
  0.0 113.9 jit_solution(2792847339495075217)
XLA Ops:
  4.0 6.4 %collective-permute-start.2 = (f32[64,1024]{1,0:T(8,128)S(1)}, f32[64,1024]{1,0:T(8,128)S(1)}, u32[]{:S(2)}, u32[]{:S(2)}) collective-permute-start(f32[64,1024]{1,0:T(8,128)S(1)} %get-tuple-element.29), channel_id=1, source_target_pairs={{0,111},{1,110},{2,109},{3,108},{4,107},{5,106},{6,105},{7,104},{8... | collective-permute-start | bytes 786440 | tf_op jit(solution)/shard_map/ppermute | solution.py:47
  10.4 3.0 %collective-permute-start.3 = (f32[64,1024]{1,0:T(8,128)S(1)}, f32[64,1024]{1,0:T(8,128)S(1)}, u32[]{:S(2)}, u32[]{:S(2)}) collective-permute-start(f32[64,1024]{1,0:T(8,128)S(1)} %get-tuple-element.30), channel_id=1, source_target_pairs={{0,0},{1,1},{2,2},{3,3},{4,4},{5,5},{6,6},{7,7},{8,8},{9,9},{10,10... | collective-permute-start | bytes 786440 | tf_op jit(solution)/shard_map/ppermute | solution.py:47
  14.8 2.5 %collective-permute-start.5 = (f32[64,1024]{1,0:T(8,128)S(1)}, f32[64,1024]{1,0:T(8,128)S(1)}, u32[]{:S(2)}, u32[]{:S(2)}) collective-permute-start(f32[64,1024]{1,0:T(8,128)S(1)} %get-tuple-element.32), channel_id=1, source_target_pairs={{0,3},{1,2},{2,1},{3,0},{4,7},{5,6},{6,5},{7,4},{8,11},{9,10},{10,... | collective-permute-start | bytes 786440 | tf_op jit(solution)/shard_map/ppermute | solution.py:47
  17.4 5.2 %collective-permute-done.3.refs_1_.refs_5_ = f32[64,1024]{1,0:T(8,128)S(1)} collective-permute-done((f32[64,1024]{1,0:T(8,128)S(1)}, f32[64,1024]{1,0:T(8,128)S(1)}, u32[]{:S(2)}, u32[]{:S(2)}) %collective-permute-start.3) | collective-permute-done | bytes 262176 | tf_op jit(solution)/shard_map/ppermute | solution.py:47
  22.6 3.0 %collective-permute-done.4.refs_2_.refs_6_ = f32[64,1024]{1,0:T(8,128)S(1)} collective-permute-done((f32[64,1024]{1,0:T(8,128)S(1)}, f32[64,1024]{1,0:T(8,128)S(1)}, u32[]{:S(2)}, u32[]{:S(2)}) %collective-permute-start.4) | collective-permute-done | bytes 262176 | tf_op jit(solution)/shard_map/ppermute | solution.py:47
  27.1 1.8 %shard_map.39 = (f32[1344,128]{1,0:T(8,128)S(1)}, f32[1344,128]{1,0:T(8,128)S(1)}) custom-call(s32[1]{0:T(128)} %bitcast.where_ref.core_ref, f32[64,1024]{1,0:T(8,128)S(1)} %collective-permute-done.2.refs_0_.refs_4_, f32[64,1024]{1,0:T(8,128)S(1)} %collective-permute-done.3.refs_1_.refs_5_, f32[64,1024]{1,0:T(8,128)S(1)} %collective-permute-done.4.refs_2_.refs_6_, ...), custom_call_target="tpu_custom_call" | custom-call | flops 1000000 | bytes 4000000 | tf_op jit(solution)/shard_map/pallas_call | solution.py:495
  29.7 1.5 %collective-permute-done.6 = f32[1344,128]{1,0:T(8,128)S(1)} collective-permute-done((f32[1344,128]{1,0:T(8,128)S(1)}, f32[1344,128]{1,0:T(8,128)S(1)}, u32[]{:S(2)}, u32[]{:S(2)}) %collective-permute-start.6) | collective-permute-done | bytes 688160 | tf_op jit(solution)/shard_map/ppermute | solution.py:47
  31.6 4.3 %collective-permute-done.20 = f32[648,128]{1,0:T(8,128)S(1)} collective-permute-done((f32[648,128]{1,0:T(8,128)S(1)}, f32[648,128]{1,0:T(8,128)S(1)}, u32[]{:S(2)}, u32[]{:S(2)}) %collective-permute-start.20) | collective-permute-done | bytes 331808 | tf_op jit(solution)/shard_map/ppermute | solution.py:47
  36.0 2.3 %collective-permute-done.7 = f32[448,128]{1,0:T(8,128)S(1)} collective-permute-done((f32[448,128]{1,0:T(8,128)S(1)}, f32[448,128]{1,0:T(8,128)S(1)}, u32[]{:S(2)}, u32[]{:S(2)}) %collective-permute-start.7) | collective-permute-done | bytes 229408 | tf_op jit(solution)/shard_map/ppermute | solution.py:47
  38.5 1.5 %collective-permute-start.10 = (f32[224,128]{1,0:T(8,128)S(1)}, f32[224,128]{1,0:T(8,128)S(1)}, u32[]{:S(2)}, u32[]{:S(2)}) collective-permute-start(f32[224,128]{1,0:T(8,128)S(1)} %slice_add_fusion.4), channel_id=1, source_target_pairs={{0,32},{1,33},{2,34},{3,35},{4,36},{5,37},{6,38},{7,39},{8,40},{9,... | collective-permute-start | bytes 344072 | tf_op jit(solution)/shard_map/ppermute | solution.py:47
  40.0 2.2 %collective-permute-done.21 = f32[648,128]{1,0:T(8,128)S(1)} collective-permute-done((f32[648,128]{1,0:T(8,128)S(1)}, f32[648,128]{1,0:T(8,128)S(1)}, u32[]{:S(2)}, u32[]{:S(2)}) %collective-permute-start.21) | collective-permute-done | bytes 331808 | tf_op jit(solution)/shard_map/ppermute | solution.py:47
  44.0 2.0 %collective-permute-done.8 = f32[448,128]{1,0:T(8,128)S(1)} collective-permute-done((f32[448,128]{1,0:T(8,128)S(1)}, f32[448,128]{1,0:T(8,128)S(1)}, u32[]{:S(2)}, u32[]{:S(2)}) %collective-permute-start.8) | collective-permute-done | bytes 229408 | tf_op jit(solution)/shard_map/ppermute | solution.py:47
  47.6 2.2 %collective-permute-done.22 = f32[648,128]{1,0:T(8,128)S(1)} collective-permute-done((f32[648,128]{1,0:T(8,128)S(1)}, f32[648,128]{1,0:T(8,128)S(1)}, u32[]{:S(2)}, u32[]{:S(2)}) %collective-permute-start.22) | collective-permute-done | bytes 331808 | tf_op jit(solution)/shard_map/ppermute | solution.py:47
  51.4 2.0 %collective-permute-done.24 = f32[320,128]{1,0:T(8,128)S(1)} collective-permute-done((f32[320,128]{1,0:T(8,128)S(1)}, f32[320,128]{1,0:T(8,128)S(1)}, u32[]{:S(2)}, u32[]{:S(2)}) %collective-permute-start.24) | collective-permute-done | bytes 163872 | tf_op jit(solution)/shard_map/ppermute | solution.py:47
  53.6 3.5 %collective-permute-done.11 = f32[224,128]{1,0:T(8,128)S(1)} collective-permute-done((f32[224,128]{1,0:T(8,128)S(1)}, f32[224,128]{1,0:T(8,128)S(1)}, u32[]{:S(2)}, u32[]{:S(2)}) %collective-permute-start.11) | collective-permute-done | bytes 114720 | tf_op jit(solution)/shard_map/ppermute | solution.py:47
  61.3 4.0 %collective-permute-done.14.refs_3_ = f32[224,128]{1,0:T(8,128)S(1)} collective-permute-done((f32[224,128]{1,0:T(8,128)S(1)}, f32[224,128]{1,0:T(8,128)S(1)}, u32[]{:S(2)}, u32[]{:S(2)}) %collective-permute-start.14) | collective-permute-done | bytes 114720 | tf_op jit(solution)/shard_map/ppermute | solution.py:47
  66.1 2.8 %shard_map.41 = (f32[1936,128]{1,0:T(8,128)S(1)}, f32[16,128]{1,0:T(8,128)S(1)}, f32[128,128]{1,0:T(8,128)S(1)}, f32[8,256,128]{2,1,0:T(8,128)S(1)}) custom-call(s32[1]{0:T(128)} %bitcast.where_ref.core_ref, f32[648,128]{1,0:T(8,128)S(1)} %add.117.refs_0_, f32[320,128]{1,0:T(8,128)S(1)} %add.121.refs_1_, f32[648,128]{1,0:T(8,128)S(1)} %collective-permute-done.26.refs_2_, ...), custom_call_target="tpu_custom_call" | custom-call | flops 3000000000 | bytes 4000000 | tf_op jit(solution)/shard_map/pallas_call | solution.py:495
  69.0 4.0 %shard_map.42 = (bf16[768,1536]{1,0:T(8,128)(2,1)S(1)}, bf16[768,1536]{1,0:T(8,128)(2,1)S(1)}, f32[6,256,128]{2,1,0:T(8,128)S(1)}, f32[2,256,128]{2,1,0:T(8,128)S(1)}) custom-call(f32[1936,128]{1,0:T(8,128)S(1)} %get-tuple-element.38.flat, f32[128,128]{1,0:T(8,128)S(1)} %get-tuple-element.39.inv0, f32[8,256,128]{2,1,0:T(8,128)S(1)} %get-tuple-element.40.x), custom_call_target="tpu_custom_call" | custom-call | flops 3000000000 | bytes 4000000 | tf_op jit(solution)/shard_map/pallas_call | solution.py:495
  73.0 19.2 %shard_map.43 = (f32[64,1024]{1,0:T(8,128)S(1)}, f32[64,1024]{1,0:T(8,128)S(1)}, f32[64,1024]{1,0:T(8,128)S(1)}, f32[64,1024]{1,0:T(8,128)S(1)}) custom-call(s32[1]{0:T(128)} %bitcast.where_ref.core_ref, f32[448,128]{1,0:T(8,128)S(1)} %add.108.refs_0_, f32[224,128]{1,0:T(8,128)S(1)} %add.113.refs_1_, f32[448,128]{1,0:T(8,128)S(1)} %collective-permute-done.13.refs_2_, ...), custom_call_target="tpu_custom_call" | custom-call | flops 20000000000 | bytes 4000000 | tf_op jit(solution)/shard_map/pallas_call | solution.py:495
  92.3 3.0 %collective-permute-start.28 = (f32[64,1024]{1,0:T(8,128)S(1)}, f32[64,1024]{1,0:T(8,128)S(1)}, u32[]{:S(2)}, u32[]{:S(2)}) collective-permute-start(f32[64,1024]{1,0:T(8,128)S(1)} %get-tuple-element.45), channel_id=1, source_target_pairs={{0,111},{1,110},{2,109},{3,108},{4,107},{5,106},{6,105},{7,104},{8... | collective-permute-start | bytes 786440 | tf_op jit(solution)/shard_map/ppermute | solution.py:47
  95.2 6.2 %collective-permute-start.29 = (f32[64,1024]{1,0:T(8,128)S(1)}, f32[64,1024]{1,0:T(8,128)S(1)}, u32[]{:S(2)}, u32[]{:S(2)}) collective-permute-start(f32[64,1024]{1,0:T(8,128)S(1)} %get-tuple-element.46), channel_id=1, source_target_pairs={{0,0},{1,1},{2,2},{3,3},{4,4},{5,5},{6,6},{7,7},{8,8},{9,9},{10,10... | collective-permute-start | bytes 786440 | tf_op jit(solution)/shard_map/ppermute | solution.py:47
  102.7 2.4 %collective-permute-start.32 = (f32[64,1024]{1,0:T(8,128)S(1)}, f32[64,1024]{1,0:T(8,128)S(1)}, u32[]{:S(2)}, u32[]{:S(2)}) collective-permute-start(f32[64,1024]{1,0:T(8,128)S(1)} %collective-permute-done.28.refs_0_), channel_id=1, source_target_pairs={{0,16},{1,17},{2,18},{3,19},{4,20},{5,21},{6,22},{7,23},{8,24},{9,... | collective-permute-start | bytes 786440 | tf_op jit(solution)/shard_map/ppermute | solution.py:47
  105.1 3.4 %collective-permute-done.29.refs_1_ = f32[64,1024]{1,0:T(8,128)S(1)} collective-permute-done((f32[64,1024]{1,0:T(8,128)S(1)}, f32[64,1024]{1,0:T(8,128)S(1)}, u32[]{:S(2)}, u32[]{:S(2)}) %collective-permute-start.29) | collective-permute-done | bytes 262176 | tf_op jit(solution)/shard_map/ppermute | solution.py:47
  108.5 2.3 %collective-permute-done.30.refs_2_ = f32[64,1024]{1,0:T(8,128)S(1)} collective-permute-done((f32[64,1024]{1,0:T(8,128)S(1)}, f32[64,1024]{1,0:T(8,128)S(1)}, u32[]{:S(2)}, u32[]{:S(2)}) %collective-permute-start.30) | collective-permute-done | bytes 262176 | tf_op jit(solution)/shard_map/ppermute | solution.py:47
  (75 shorter events, 22.7 us)
Async XLA Ops:
  4.0 13.3 %collective-permute-start.2 = (f32[64,1024]{1,0:T(8,128)S(1)}, f32[64,1024]{1,0:T(8,128)S(1)}, u32[]{:S(2)}, u32[]{:S(2)}) collective-permute-start(f32[64,1024]{1,0:T(8,128)S(1)} %get-tuple-element.29), channel_id=1, source_target_pairs={{0,111},{1,110},{2,109},{3,108},{4,107},{5,106},{6,105},{7,104},{8... | collective-permute-start | bytes 786440 | tf_op jit(solution)/shard_map/ppermute | solution.py:47
  10.4 12.2 %collective-permute-start.3 = (f32[64,1024]{1,0:T(8,128)S(1)}, f32[64,1024]{1,0:T(8,128)S(1)}, u32[]{:S(2)}, u32[]{:S(2)}) collective-permute-start(f32[64,1024]{1,0:T(8,128)S(1)} %get-tuple-element.30), channel_id=1, source_target_pairs={{0,0},{1,1},{2,2},{3,3},{4,4},{5,5},{6,6},{7,7},{8,8},{9,9},{10,10... | collective-permute-start | bytes 786440 | tf_op jit(solution)/shard_map/ppermute | solution.py:47
  13.4 12.2 %collective-permute-start.4 = (f32[64,1024]{1,0:T(8,128)S(1)}, f32[64,1024]{1,0:T(8,128)S(1)}, u32[]{:S(2)}, u32[]{:S(2)}) collective-permute-start(f32[64,1024]{1,0:T(8,128)S(1)} %get-tuple-element.31), channel_id=1, source_target_pairs={{0,12},{1,13},{2,14},{3,15},{4,8},{5,9},{6,10},{7,11},{8,4},{9,5},... | collective-permute-start | bytes 786440 | tf_op jit(solution)/shard_map/ppermute | solution.py:47
  14.8 10.8 %collective-permute-start.5 = (f32[64,1024]{1,0:T(8,128)S(1)}, f32[64,1024]{1,0:T(8,128)S(1)}, u32[]{:S(2)}, u32[]{:S(2)}) collective-permute-start(f32[64,1024]{1,0:T(8,128)S(1)} %get-tuple-element.32), channel_id=1, source_target_pairs={{0,3},{1,2},{2,1},{3,0},{4,7},{5,6},{6,5},{7,4},{8,11},{9,10},{10,... | collective-permute-start | bytes 786440 | tf_op jit(solution)/shard_map/ppermute | solution.py:47
  29.5 6.3 %collective-permute-start.20 = (f32[648,128]{1,0:T(8,128)S(1)}, f32[648,128]{1,0:T(8,128)S(1)}, u32[]{:S(2)}, u32[]{:S(2)}) collective-permute-start(f32[648,128]{1,0:T(8,128)S(1)} %slice_add_fusion), channel_id=1, source_target_pairs={{0,4},{1,5},{2,6},{3,7},{4,0},{5,1},{6,2},{7,3},{8,12},{9,13},{10,... | collective-permute-start | bytes 995336 | tf_op jit(solution)/shard_map/ppermute | solution.py:47
  31.3 7.0 %collective-permute-start.7 = (f32[448,128]{1,0:T(8,128)S(1)}, f32[448,128]{1,0:T(8,128)S(1)}, u32[]{:S(2)}, u32[]{:S(2)}) collective-permute-start(f32[448,128]{1,0:T(8,128)S(1)} %slice_add_fusion.1), channel_id=1, source_target_pairs={{0,4},{1,5},{2,6},{3,7},{4,0},{5,1},{6,2},{7,3},{8,12},{9,13},{10,... | collective-permute-start | bytes 688136 | tf_op jit(solution)/shard_map/ppermute | solution.py:47
  31.5 11.3 %collective-permute-start.23 = (f32[320,128]{1,0:T(8,128)S(1)}, f32[320,128]{1,0:T(8,128)S(1)}, u32[]{:S(2)}, u32[]{:S(2)}) collective-permute-start(f32[320,128]{1,0:T(8,128)S(1)} %slice_add_fusion.3), channel_id=1, source_target_pairs={{0,32},{1,33},{2,34},{3,35},{4,36},{5,37},{6,38},{7,39},{8,40},{9,... | collective-permute-start | bytes 491528 | tf_op jit(solution)/shard_map/ppermute | solution.py:47
  38.4 7.6 %collective-permute-start.8 = (f32[448,128]{1,0:T(8,128)S(1)}, f32[448,128]{1,0:T(8,128)S(1)}, u32[]{:S(2)}, u32[]{:S(2)}) collective-permute-start(f32[448,128]{1,0:T(8,128)S(1)} %fusion), channel_id=1, source_target_pairs={{0,1},{1,0},{2,3},{3,2},{4,5},{5,4},{6,7},{7,6},{8,9},{9,8},{10,11... | collective-permute-start | bytes 688136 | tf_op jit(solution)/shard_map/ppermute | solution.py:47
  38.5 8.4 %collective-permute-start.10 = (f32[224,128]{1,0:T(8,128)S(1)}, f32[224,128]{1,0:T(8,128)S(1)}, u32[]{:S(2)}, u32[]{:S(2)}) collective-permute-start(f32[224,128]{1,0:T(8,128)S(1)} %slice_add_fusion.4), channel_id=1, source_target_pairs={{0,32},{1,33},{2,34},{3,35},{4,36},{5,37},{6,38},{7,39},{8,40},{9,... | collective-permute-start | bytes 344072 | tf_op jit(solution)/shard_map/ppermute | solution.py:47
  42.3 7.6 %collective-permute-start.22 = (f32[648,128]{1,0:T(8,128)S(1)}, f32[648,128]{1,0:T(8,128)S(1)}, u32[]{:S(2)}, u32[]{:S(2)}) collective-permute-start(f32[648,128]{1,0:T(8,128)S(1)} %add.116), channel_id=1, source_target_pairs={{0,32},{1,33},{2,34},{3,35},{4,36},{5,37},{6,38},{7,39},{8,40},{9,... | collective-permute-start | bytes 995336 | tf_op jit(solution)/shard_map/ppermute | solution.py:47
  42.8 10.5 %collective-permute-start.24 = (f32[320,128]{1,0:T(8,128)S(1)}, f32[320,128]{1,0:T(8,128)S(1)}, u32[]{:S(2)}, u32[]{:S(2)}) collective-permute-start(f32[320,128]{1,0:T(8,128)S(1)} %add.119), channel_id=1, source_target_pairs={{0,4},{1,5},{2,6},{3,7},{4,0},{5,1},{6,2},{7,3},{8,12},{9,13},{10,... | collective-permute-start | bytes 491528 | tf_op jit(solution)/shard_map/ppermute | solution.py:47
  46.0 11.4 %collective-permute-start.9 = (f32[448,128]{1,0:T(8,128)S(1)}, f32[448,128]{1,0:T(8,128)S(1)}, u32[]{:S(2)}, u32[]{:S(2)}) collective-permute-start(f32[448,128]{1,0:T(8,128)S(1)} %add.107), channel_id=1, source_target_pairs={{0,32},{1,33},{2,34},{3,35},{4,36},{5,37},{6,38},{7,39},{8,40},{9,... | collective-permute-start | bytes 688136 | tf_op jit(solution)/shard_map/ppermute | solution.py:47
  46.9 10.2 %collective-permute-start.11 = (f32[224,128]{1,0:T(8,128)S(1)}, f32[224,128]{1,0:T(8,128)S(1)}, u32[]{:S(2)}, u32[]{:S(2)}) collective-permute-start(f32[224,128]{1,0:T(8,128)S(1)} %fusion.1), channel_id=1, source_target_pairs={{0,4},{1,5},{2,6},{3,7},{4,0},{5,1},{6,2},{7,3},{8,12},{9,13},{10,... | collective-permute-start | bytes 344072 | tf_op jit(solution)/shard_map/ppermute | solution.py:47
  49.9 16.2 %collective-permute-start.26 = (f32[648,128]{1,0:T(8,128)S(1)}, f32[648,128]{1,0:T(8,128)S(1)}, u32[]{:S(2)}, u32[]{:S(2)}) collective-permute-start(f32[648,128]{1,0:T(8,128)S(1)} %add.117.refs_0_), channel_id=1, source_target_pairs={{0,16},{1,17},{2,18},{3,19},{4,20},{5,21},{6,22},{7,23},{8,24},{9,... | collective-permute-start | bytes 995336 | tf_op jit(solution)/shard_map/ppermute | solution.py:47
  57.4 8.4 %collective-permute-start.13 = (f32[448,128]{1,0:T(8,128)S(1)}, f32[448,128]{1,0:T(8,128)S(1)}, u32[]{:S(2)}, u32[]{:S(2)}) collective-permute-start(f32[448,128]{1,0:T(8,128)S(1)} %add.108.refs_0_), channel_id=1, source_target_pairs={{0,4},{1,5},{2,6},{3,7},{4,0},{5,1},{6,2},{7,3},{8,12},{9,13},{10,... | collective-permute-start | bytes 688136 | tf_op jit(solution)/shard_map/ppermute | solution.py:47
  61.3 11.7 %collective-permute-start.16 = (f32[224,128]{1,0:T(8,128)S(1)}, f32[224,128]{1,0:T(8,128)S(1)}, u32[]{:S(2)}, u32[]{:S(2)}) collective-permute-start(f32[224,128]{1,0:T(8,128)S(1)} %add.113.refs_1_), channel_id=1, source_target_pairs={{0,16},{1,17},{2,18},{3,19},{4,20},{5,21},{6,22},{7,23},{8,24},{9,... | collective-permute-start | bytes 344072 | tf_op jit(solution)/shard_map/ppermute | solution.py:47
  65.3 7.6 %collective-permute-start.18 = (f32[224,128]{1,0:T(8,128)S(1)}, f32[224,128]{1,0:T(8,128)S(1)}, u32[]{:S(2)}, u32[]{:S(2)}) collective-permute-start(f32[224,128]{1,0:T(8,128)S(1)} %collective-permute-done.14.refs_3_), channel_id=1, source_target_pairs={{0,16},{1,17},{2,18},{3,19},{4,20},{5,21},{6,22},{7,23},{8,24},{9,... | collective-permute-start | bytes 344072 | tf_op jit(solution)/shard_map/ppermute | solution.py:47
  65.6 7.4 %collective-permute-start.15 = (f32[448,128]{1,0:T(8,128)S(1)}, f32[448,128]{1,0:T(8,128)S(1)}, u32[]{:S(2)}, u32[]{:S(2)}) collective-permute-start(f32[448,128]{1,0:T(8,128)S(1)} %add.108.refs_0_), channel_id=1, source_target_pairs={{0,16},{1,17},{2,18},{3,19},{4,20},{5,21},{6,22},{7,23},{8,24},{9,... | collective-permute-start | bytes 688136 | tf_op jit(solution)/shard_map/ppermute | solution.py:47
  65.9 7.1 %collective-permute-start.17 = (f32[448,128]{1,0:T(8,128)S(1)}, f32[448,128]{1,0:T(8,128)S(1)}, u32[]{:S(2)}, u32[]{:S(2)}) collective-permute-start(f32[448,128]{1,0:T(8,128)S(1)} %collective-permute-done.13.refs_2_), channel_id=1, source_target_pairs={{0,16},{1,17},{2,18},{3,19},{4,20},{5,21},{6,22},{7,23},{8,24},{9,... | collective-permute-start | bytes 688136 | tf_op jit(solution)/shard_map/ppermute | solution.py:47
  92.3 10.4 %collective-permute-start.28 = (f32[64,1024]{1,0:T(8,128)S(1)}, f32[64,1024]{1,0:T(8,128)S(1)}, u32[]{:S(2)}, u32[]{:S(2)}) collective-permute-start(f32[64,1024]{1,0:T(8,128)S(1)} %get-tuple-element.45), channel_id=1, source_target_pairs={{0,111},{1,110},{2,109},{3,108},{4,107},{5,106},{6,105},{7,104},{8... | collective-permute-start | bytes 786440 | tf_op jit(solution)/shard_map/ppermute | solution.py:47
  95.2 13.2 %collective-permute-start.29 = (f32[64,1024]{1,0:T(8,128)S(1)}, f32[64,1024]{1,0:T(8,128)S(1)}, u32[]{:S(2)}, u32[]{:S(2)}) collective-permute-start(f32[64,1024]{1,0:T(8,128)S(1)} %get-tuple-element.46), channel_id=1, source_target_pairs={{0,0},{1,1},{2,2},{3,3},{4,4},{5,5},{6,6},{7,7},{8,8},{9,9},{10,10... | collective-permute-start | bytes 786440 | tf_op jit(solution)/shard_map/ppermute | solution.py:47
  101.4 9.4 %collective-permute-start.30 = (f32[64,1024]{1,0:T(8,128)S(1)}, f32[64,1024]{1,0:T(8,128)S(1)}, u32[]{:S(2)}, u32[]{:S(2)}) collective-permute-start(f32[64,1024]{1,0:T(8,128)S(1)} %get-tuple-element.47), channel_id=1, source_target_pairs={{0,12},{1,13},{2,14},{3,15},{4,8},{5,9},{6,10},{7,11},{8,4},{9,5},... | collective-permute-start | bytes 786440 | tf_op jit(solution)/shard_map/ppermute | solution.py:47
  101.5 9.3 %collective-permute-start.31 = (f32[64,1024]{1,0:T(8,128)S(1)}, f32[64,1024]{1,0:T(8,128)S(1)}, u32[]{:S(2)}, u32[]{:S(2)}) collective-permute-start(f32[64,1024]{1,0:T(8,128)S(1)} %get-tuple-element.48), channel_id=1, source_target_pairs={{0,3},{1,2},{2,1},{3,0},{4,7},{5,6},{6,5},{7,4},{8,11},{9,10},{10,... | collective-permute-start | bytes 786440 | tf_op jit(solution)/shard_map/ppermute | solution.py:47
  102.7 8.6 %collective-permute-start.32 = (f32[64,1024]{1,0:T(8,128)S(1)}, f32[64,1024]{1,0:T(8,128)S(1)}, u32[]{:S(2)}, u32[]{:S(2)}) collective-permute-start(f32[64,1024]{1,0:T(8,128)S(1)} %collective-permute-done.28.refs_0_), channel_id=1, source_target_pairs={{0,16},{1,17},{2,18},{3,19},{4,20},{5,21},{6,22},{7,23},{8,24},{9,... | collective-permute-start | bytes 786440 | tf_op jit(solution)/shard_map/ppermute | solution.py:47
  (13 other events, 44.6 us)

commit v6 on v5

--- a/solution.py
+++ b/solution.py
@@ -300,14 +300,17 @@
         flat[rows_of(chunk, info_ref, n // (len(refs) // 2) ^ core_of(info_ref), n % 2, n // 2 % 2), :] = ref[...]
 
 
-def make_covariance(chunk, flat, mean, scale):
+def covariance_steps(chunk, flat, mean, scale):
     mean_t = jnp.concatenate([mean, jnp.zeros((B - 8, B), jnp.float32)], axis=0).T
     eye = jnp.where(iota((B, B), 0) == iota((B, B), 1), RIDGE, 0.0)
     scale = jnp.broadcast_to(scale[0:1, :], (B, B))
-    for (i, k), n in PLACE_IN[chunk].items():
+
+    def step(n, i, k):
         block = flat[n * B : (n + 1) * B, :] * scale
         block = block - jnp.broadcast_to(mean_t[:, i : i + 1], (B, B)) * mean[k : k + 1, :]
         flat[n * B : (n + 1) * B, :] = block + eye if i == k else block
+
+    return [functools.partial(step, n, i, k) for (i, k), n in PLACE_IN[chunk].items()]
 
 
 def center_rows(rows_refs, mean, k):
@@ -337,13 +340,14 @@
     mean = flat[STAT : STAT + 8, :] * scale
     stat_ref[0:8, :] = mean
     stat_ref[8:16, :] = scale
-    make_covariance(0, flat, mean, scale)
+    first, *rest = covariance_steps(0, flat, mean, scale)
+    first()
     ones[...] = jnp.ones((8, B), jnp.float32)
 
     def center(k):
         x_ref[k] = center_rows(rows_refs, stat_ref[...], k)
 
-    leaf(flat[0:B], ones, inv, [functools.partial(center, k) for k in range(8)])
+    leaf(flat[0:B], ones, inv, rest + [functools.partial(center, k) for k in range(8)])
 
 
 def column1_kernel(flat, inv0, x, rows_l_ref, rows_r_ref, x_ref, z_ref, ones, inv, inv_r, diagonal, first_r, col0, col1, x1, z_l):
@@ -399,7 +403,8 @@
     flat, ones, inv, inv_r, diagonal, panel, x, z_l, rows_l, rows_r, white = refs[17:]
     at = PLACE_IN[1]
     gather_chunk(1, core_ref, parts_refs, flat)
-    make_covariance(1, flat, stat_ref[0:8, :], stat_ref[8:16, :])
+    for make in covariance_steps(1, flat, stat_ref[0:8, :], stat_ref[8:16, :]):
+        make()
     ones[...] = jnp.ones((8, B), jnp.float32)
     diagonal[...] = flat[0:B, :] - product(first_l[0:B, :], first_rr[0:B, :])
 

time: 114 us -> 114 us (level)
  no operation moved by 1% of the time
where the time goes in v6:
time: 114 us
  waiting for transfers between devices  41.9 us (37%)
  starting transfers between devices  38.3 us (34%)
  Pallas kernels  31.4 us (28%)
    ppermute x36, waiting for transfers between devices, permute(): return lax.ppermute(x, AXES, [(n, to(n)) for n in range(128)])  41.9 us
    ppermute x36, starting transfers between devices, permute(): return lax.ppermute(x, AXES, [(n, to(n)) for n in range(128)])  38.3 us
    pallas_call x8, Pallas kernels, call(): pl.pallas_call(kernel, out_shape=outs, in_specs=[SMEM] * scalars + [VMEM]...  31.4 us
  transfers between devices with their start and end apart: 36, of which 18 were waited for; matrix products, arithmetic and copies ran while one was open for 1% of the time, Pallas kernels for 8%

profile of v6, /device:TPU:1, one launch (start us, length us, event | category | flops | bytes accessed | tf_op | source)
XLA Modules:
  0.0 114.0 jit_solution(3354780558326320125)
XLA Ops:
  4.0 6.4 %collective-permute-start.2 = (f32[64,1024]{1,0:T(8,128)S(1)}, f32[64,1024]{1,0:T(8,128)S(1)}, u32[]{:S(2)}, u32[]{:S(2)}) collective-permute-start(f32[64,1024]{1,0:T(8,128)S(1)} %get-tuple-element.29), channel_id=1, source_target_pairs={{0,111},{1,110},{2,109},{3,108},{4,107},{5,106},{6,105},{7,104},{8... | collective-permute-start | bytes 786440 | tf_op jit(solution)/shard_map/ppermute | solution.py:47
  10.4 3.0 %collective-permute-start.3 = (f32[64,1024]{1,0:T(8,128)S(1)}, f32[64,1024]{1,0:T(8,128)S(1)}, u32[]{:S(2)}, u32[]{:S(2)}) collective-permute-start(f32[64,1024]{1,0:T(8,128)S(1)} %get-tuple-element.30), channel_id=1, source_target_pairs={{0,0},{1,1},{2,2},{3,3},{4,4},{5,5},{6,6},{7,7},{8,8},{9,9},{10,10... | collective-permute-start | bytes 786440 | tf_op jit(solution)/shard_map/ppermute | solution.py:47
  14.8 2.5 %collective-permute-start.5 = (f32[64,1024]{1,0:T(8,128)S(1)}, f32[64,1024]{1,0:T(8,128)S(1)}, u32[]{:S(2)}, u32[]{:S(2)}) collective-permute-start(f32[64,1024]{1,0:T(8,128)S(1)} %get-tuple-element.32), channel_id=1, source_target_pairs={{0,3},{1,2},{2,1},{3,0},{4,7},{5,6},{6,5},{7,4},{8,11},{9,10},{10,... | collective-permute-start | bytes 786440 | tf_op jit(solution)/shard_map/ppermute | solution.py:47
  17.4 5.2 %collective-permute-done.3.refs_1_.refs_5_ = f32[64,1024]{1,0:T(8,128)S(1)} collective-permute-done((f32[64,1024]{1,0:T(8,128)S(1)}, f32[64,1024]{1,0:T(8,128)S(1)}, u32[]{:S(2)}, u32[]{:S(2)}) %collective-permute-start.3) | collective-permute-done | bytes 262176 | tf_op jit(solution)/shard_map/ppermute | solution.py:47
  22.6 3.0 %collective-permute-done.4.refs_2_.refs_6_ = f32[64,1024]{1,0:T(8,128)S(1)} collective-permute-done((f32[64,1024]{1,0:T(8,128)S(1)}, f32[64,1024]{1,0:T(8,128)S(1)}, u32[]{:S(2)}, u32[]{:S(2)}) %collective-permute-start.4) | collective-permute-done | bytes 262176 | tf_op jit(solution)/shard_map/ppermute | solution.py:47
  27.1 1.8 %shard_map.39 = (f32[1344,128]{1,0:T(8,128)S(1)}, f32[1344,128]{1,0:T(8,128)S(1)}) custom-call(s32[1]{0:T(128)} %bitcast.where_ref.core_ref, f32[64,1024]{1,0:T(8,128)S(1)} %collective-permute-done.2.refs_0_.refs_4_, f32[64,1024]{1,0:T(8,128)S(1)} %collective-permute-done.3.refs_1_.refs_5_, f32[64,1024]{1,0:T(8,128)S(1)} %collective-permute-done.4.refs_2_.refs_6_, ...), custom_call_target="tpu_custom_call" | custom-call | flops 1000000 | bytes 4000000 | tf_op jit(solution)/shard_map/pallas_call | solution.py:500
  29.7 1.5 %collective-permute-done.6 = f32[1344,128]{1,0:T(8,128)S(1)} collective-permute-done((f32[1344,128]{1,0:T(8,128)S(1)}, f32[1344,128]{1,0:T(8,128)S(1)}, u32[]{:S(2)}, u32[]{:S(2)}) %collective-permute-start.6) | collective-permute-done | bytes 688160 | tf_op jit(solution)/shard_map/ppermute | solution.py:47
  31.6 4.3 %collective-permute-done.20 = f32[648,128]{1,0:T(8,128)S(1)} collective-permute-done((f32[648,128]{1,0:T(8,128)S(1)}, f32[648,128]{1,0:T(8,128)S(1)}, u32[]{:S(2)}, u32[]{:S(2)}) %collective-permute-start.20) | collective-permute-done | bytes 331808 | tf_op jit(solution)/shard_map/ppermute | solution.py:47
  36.0 2.3 %collective-permute-done.7 = f32[448,128]{1,0:T(8,128)S(1)} collective-permute-done((f32[448,128]{1,0:T(8,128)S(1)}, f32[448,128]{1,0:T(8,128)S(1)}, u32[]{:S(2)}, u32[]{:S(2)}) %collective-permute-start.7) | collective-permute-done | bytes 229408 | tf_op jit(solution)/shard_map/ppermute | solution.py:47
  38.5 1.5 %collective-permute-start.10 = (f32[224,128]{1,0:T(8,128)S(1)}, f32[224,128]{1,0:T(8,128)S(1)}, u32[]{:S(2)}, u32[]{:S(2)}) collective-permute-start(f32[224,128]{1,0:T(8,128)S(1)} %slice_add_fusion.4), channel_id=1, source_target_pairs={{0,32},{1,33},{2,34},{3,35},{4,36},{5,37},{6,38},{7,39},{8,40},{9,... | collective-permute-start | bytes 344072 | tf_op jit(solution)/shard_map/ppermute | solution.py:47
  40.0 2.2 %collective-permute-done.21 = f32[648,128]{1,0:T(8,128)S(1)} collective-permute-done((f32[648,128]{1,0:T(8,128)S(1)}, f32[648,128]{1,0:T(8,128)S(1)}, u32[]{:S(2)}, u32[]{:S(2)}) %collective-permute-start.21) | collective-permute-done | bytes 331808 | tf_op jit(solution)/shard_map/ppermute | solution.py:47
  44.0 2.0 %collective-permute-done.8 = f32[448,128]{1,0:T(8,128)S(1)} collective-permute-done((f32[448,128]{1,0:T(8,128)S(1)}, f32[448,128]{1,0:T(8,128)S(1)}, u32[]{:S(2)}, u32[]{:S(2)}) %collective-permute-start.8) | collective-permute-done | bytes 229408 | tf_op jit(solution)/shard_map/ppermute | solution.py:47
  47.6 2.2 %collective-permute-done.22 = f32[648,128]{1,0:T(8,128)S(1)} collective-permute-done((f32[648,128]{1,0:T(8,128)S(1)}, f32[648,128]{1,0:T(8,128)S(1)}, u32[]{:S(2)}, u32[]{:S(2)}) %collective-permute-start.22) | collective-permute-done | bytes 331808 | tf_op jit(solution)/shard_map/ppermute | solution.py:47
  51.4 2.0 %collective-permute-done.24 = f32[320,128]{1,0:T(8,128)S(1)} collective-permute-done((f32[320,128]{1,0:T(8,128)S(1)}, f32[320,128]{1,0:T(8,128)S(1)}, u32[]{:S(2)}, u32[]{:S(2)}) %collective-permute-start.24) | collective-permute-done | bytes 163872 | tf_op jit(solution)/shard_map/ppermute | solution.py:47
  53.6 3.5 %collective-permute-done.11 = f32[224,128]{1,0:T(8,128)S(1)} collective-permute-done((f32[224,128]{1,0:T(8,128)S(1)}, f32[224,128]{1,0:T(8,128)S(1)}, u32[]{:S(2)}, u32[]{:S(2)}) %collective-permute-start.11) | collective-permute-done | bytes 114720 | tf_op jit(solution)/shard_map/ppermute | solution.py:47
  61.3 4.0 %collective-permute-done.14.refs_3_ = f32[224,128]{1,0:T(8,128)S(1)} collective-permute-done((f32[224,128]{1,0:T(8,128)S(1)}, f32[224,128]{1,0:T(8,128)S(1)}, u32[]{:S(2)}, u32[]{:S(2)}) %collective-permute-start.14) | collective-permute-done | bytes 114720 | tf_op jit(solution)/shard_map/ppermute | solution.py:47
  66.1 2.9 %shard_map.41 = (f32[1936,128]{1,0:T(8,128)S(1)}, f32[16,128]{1,0:T(8,128)S(1)}, f32[128,128]{1,0:T(8,128)S(1)}, f32[8,256,128]{2,1,0:T(8,128)S(1)}) custom-call(s32[1]{0:T(128)} %bitcast.where_ref.core_ref, f32[648,128]{1,0:T(8,128)S(1)} %add.117.refs_0_, f32[320,128]{1,0:T(8,128)S(1)} %add.121.refs_1_, f32[648,128]{1,0:T(8,128)S(1)} %collective-permute-done.26.refs_2_, ...), custom_call_target="tpu_custom_call" | custom-call | flops 3000000000 | bytes 4000000 | tf_op jit(solution)/shard_map/pallas_call | solution.py:500
  69.0 4.0 %shard_map.42 = (bf16[768,1536]{1,0:T(8,128)(2,1)S(1)}, bf16[768,1536]{1,0:T(8,128)(2,1)S(1)}, f32[6,256,128]{2,1,0:T(8,128)S(1)}, f32[2,256,128]{2,1,0:T(8,128)S(1)}) custom-call(f32[1936,128]{1,0:T(8,128)S(1)} %get-tuple-element.38.flat, f32[128,128]{1,0:T(8,128)S(1)} %get-tuple-element.39.inv0, f32[8,256,128]{2,1,0:T(8,128)S(1)} %get-tuple-element.40.x), custom_call_target="tpu_custom_call" | custom-call | flops 3000000000 | bytes 4000000 | tf_op jit(solution)/shard_map/pallas_call | solution.py:500
  73.1 19.2 %shard_map.43 = (f32[64,1024]{1,0:T(8,128)S(1)}, f32[64,1024]{1,0:T(8,128)S(1)}, f32[64,1024]{1,0:T(8,128)S(1)}, f32[64,1024]{1,0:T(8,128)S(1)}) custom-call(s32[1]{0:T(128)} %bitcast.where_ref.core_ref, f32[448,128]{1,0:T(8,128)S(1)} %add.108.refs_0_, f32[224,128]{1,0:T(8,128)S(1)} %add.113.refs_1_, f32[448,128]{1,0:T(8,128)S(1)} %collective-permute-done.13.refs_2_, ...), custom_call_target="tpu_custom_call" | custom-call | flops 20000000000 | bytes 4000000 | tf_op jit(solution)/shard_map/pallas_call | solution.py:500
  92.3 3.0 %collective-permute-start.28 = (f32[64,1024]{1,0:T(8,128)S(1)}, f32[64,1024]{1,0:T(8,128)S(1)}, u32[]{:S(2)}, u32[]{:S(2)}) collective-permute-start(f32[64,1024]{1,0:T(8,128)S(1)} %get-tuple-element.45), channel_id=1, source_target_pairs={{0,111},{1,110},{2,109},{3,108},{4,107},{5,106},{6,105},{7,104},{8... | collective-permute-start | bytes 786440 | tf_op jit(solution)/shard_map/ppermute | solution.py:47
  95.3 6.2 %collective-permute-start.29 = (f32[64,1024]{1,0:T(8,128)S(1)}, f32[64,1024]{1,0:T(8,128)S(1)}, u32[]{:S(2)}, u32[]{:S(2)}) collective-permute-start(f32[64,1024]{1,0:T(8,128)S(1)} %get-tuple-element.46), channel_id=1, source_target_pairs={{0,0},{1,1},{2,2},{3,3},{4,4},{5,5},{6,6},{7,7},{8,8},{9,9},{10,10... | collective-permute-start | bytes 786440 | tf_op jit(solution)/shard_map/ppermute | solution.py:47
  102.7 2.4 %collective-permute-start.32 = (f32[64,1024]{1,0:T(8,128)S(1)}, f32[64,1024]{1,0:T(8,128)S(1)}, u32[]{:S(2)}, u32[]{:S(2)}) collective-permute-start(f32[64,1024]{1,0:T(8,128)S(1)} %collective-permute-done.28.refs_0_), channel_id=1, source_target_pairs={{0,16},{1,17},{2,18},{3,19},{4,20},{5,21},{6,22},{7,23},{8,24},{9,... | collective-permute-start | bytes 786440 | tf_op jit(solution)/shard_map/ppermute | solution.py:47
  105.1 3.4 %collective-permute-done.29.refs_1_ = f32[64,1024]{1,0:T(8,128)S(1)} collective-permute-done((f32[64,1024]{1,0:T(8,128)S(1)}, f32[64,1024]{1,0:T(8,128)S(1)}, u32[]{:S(2)}, u32[]{:S(2)}) %collective-permute-start.29) | collective-permute-done | bytes 262176 | tf_op jit(solution)/shard_map/ppermute | solution.py:47
  108.5 2.3 %collective-permute-done.30.refs_2_ = f32[64,1024]{1,0:T(8,128)S(1)} collective-permute-done((f32[64,1024]{1,0:T(8,128)S(1)}, f32[64,1024]{1,0:T(8,128)S(1)}, u32[]{:S(2)}, u32[]{:S(2)}) %collective-permute-start.30) | collective-permute-done | bytes 262176 | tf_op jit(solution)/shard_map/ppermute | solution.py:47
  (75 shorter events, 22.7 us)
Async XLA Ops:
  4.0 13.3 %collective-permute-start.2 = (f32[64,1024]{1,0:T(8,128)S(1)}, f32[64,1024]{1,0:T(8,128)S(1)}, u32[]{:S(2)}, u32[]{:S(2)}) collective-permute-start(f32[64,1024]{1,0:T(8,128)S(1)} %get-tuple-element.29), channel_id=1, source_target_pairs={{0,111},{1,110},{2,109},{3,108},{4,107},{5,106},{6,105},{7,104},{8... | collective-permute-start | bytes 786440 | tf_op jit(solution)/shard_map/ppermute | solution.py:47
  10.4 12.2 %collective-permute-start.3 = (f32[64,1024]{1,0:T(8,128)S(1)}, f32[64,1024]{1,0:T(8,128)S(1)}, u32[]{:S(2)}, u32[]{:S(2)}) collective-permute-start(f32[64,1024]{1,0:T(8,128)S(1)} %get-tuple-element.30), channel_id=1, source_target_pairs={{0,0},{1,1},{2,2},{3,3},{4,4},{5,5},{6,6},{7,7},{8,8},{9,9},{10,10... | collective-permute-start | bytes 786440 | tf_op jit(solution)/shard_map/ppermute | solution.py:47
  13.4 12.2 %collective-permute-start.4 = (f32[64,1024]{1,0:T(8,128)S(1)}, f32[64,1024]{1,0:T(8,128)S(1)}, u32[]{:S(2)}, u32[]{:S(2)}) collective-permute-start(f32[64,1024]{1,0:T(8,128)S(1)} %get-tuple-element.31), channel_id=1, source_target_pairs={{0,12},{1,13},{2,14},{3,15},{4,8},{5,9},{6,10},{7,11},{8,4},{9,5},... | collective-permute-start | bytes 786440 | tf_op jit(solution)/shard_map/ppermute | solution.py:47
  14.8 10.8 %collective-permute-start.5 = (f32[64,1024]{1,0:T(8,128)S(1)}, f32[64,1024]{1,0:T(8,128)S(1)}, u32[]{:S(2)}, u32[]{:S(2)}) collective-permute-start(f32[64,1024]{1,0:T(8,128)S(1)} %get-tuple-element.32), channel_id=1, source_target_pairs={{0,3},{1,2},{2,1},{3,0},{4,7},{5,6},{6,5},{7,4},{8,11},{9,10},{10,... | collective-permute-start | bytes 786440 | tf_op jit(solution)/shard_map/ppermute | solution.py:47
  29.5 6.3 %collective-permute-start.20 = (f32[648,128]{1,0:T(8,128)S(1)}, f32[648,128]{1,0:T(8,128)S(1)}, u32[]{:S(2)}, u32[]{:S(2)}) collective-permute-start(f32[648,128]{1,0:T(8,128)S(1)} %slice_add_fusion), channel_id=1, source_target_pairs={{0,4},{1,5},{2,6},{3,7},{4,0},{5,1},{6,2},{7,3},{8,12},{9,13},{10,... | collective-permute-start | bytes 995336 | tf_op jit(solution)/shard_map/ppermute | solution.py:47
  31.3 7.0 %collective-permute-start.7 = (f32[448,128]{1,0:T(8,128)S(1)}, f32[448,128]{1,0:T(8,128)S(1)}, u32[]{:S(2)}, u32[]{:S(2)}) collective-permute-start(f32[448,128]{1,0:T(8,128)S(1)} %slice_add_fusion.1), channel_id=1, source_target_pairs={{0,4},{1,5},{2,6},{3,7},{4,0},{5,1},{6,2},{7,3},{8,12},{9,13},{10,... | collective-permute-start | bytes 688136 | tf_op jit(solution)/shard_map/ppermute | solution.py:47
  31.5 11.3 %collective-permute-start.23 = (f32[320,128]{1,0:T(8,128)S(1)}, f32[320,128]{1,0:T(8,128)S(1)}, u32[]{:S(2)}, u32[]{:S(2)}) collective-permute-start(f32[320,128]{1,0:T(8,128)S(1)} %slice_add_fusion.3), channel_id=1, source_target_pairs={{0,32},{1,33},{2,34},{3,35},{4,36},{5,37},{6,38},{7,39},{8,40},{9,... | collective-permute-start | bytes 491528 | tf_op jit(solution)/shard_map/ppermute | solution.py:47
  38.4 7.6 %collective-permute-start.8 = (f32[448,128]{1,0:T(8,128)S(1)}, f32[448,128]{1,0:T(8,128)S(1)}, u32[]{:S(2)}, u32[]{:S(2)}) collective-permute-start(f32[448,128]{1,0:T(8,128)S(1)} %fusion), channel_id=1, source_target_pairs={{0,1},{1,0},{2,3},{3,2},{4,5},{5,4},{6,7},{7,6},{8,9},{9,8},{10,11... | collective-permute-start | bytes 688136 | tf_op jit(solution)/shard_map/ppermute | solution.py:47
  38.5 8.4 %collective-permute-start.10 = (f32[224,128]{1,0:T(8,128)S(1)}, f32[224,128]{1,0:T(8,128)S(1)}, u32[]{:S(2)}, u32[]{:S(2)}) collective-permute-start(f32[224,128]{1,0:T(8,128)S(1)} %slice_add_fusion.4), channel_id=1, source_target_pairs={{0,32},{1,33},{2,34},{3,35},{4,36},{5,37},{6,38},{7,39},{8,40},{9,... | collective-permute-start | bytes 344072 | tf_op jit(solution)/shard_map/ppermute | solution.py:47
  42.3 7.6 %collective-permute-start.22 = (f32[648,128]{1,0:T(8,128)S(1)}, f32[648,128]{1,0:T(8,128)S(1)}, u32[]{:S(2)}, u32[]{:S(2)}) collective-permute-start(f32[648,128]{1,0:T(8,128)S(1)} %add.116), channel_id=1, source_target_pairs={{0,32},{1,33},{2,34},{3,35},{4,36},{5,37},{6,38},{7,39},{8,40},{9,... | collective-permute-start | bytes 995336 | tf_op jit(solution)/shard_map/ppermute | solution.py:47
  42.8 10.5 %collective-permute-start.24 = (f32[320,128]{1,0:T(8,128)S(1)}, f32[320,128]{1,0:T(8,128)S(1)}, u32[]{:S(2)}, u32[]{:S(2)}) collective-permute-start(f32[320,128]{1,0:T(8,128)S(1)} %add.119), channel_id=1, source_target_pairs={{0,4},{1,5},{2,6},{3,7},{4,0},{5,1},{6,2},{7,3},{8,12},{9,13},{10,... | collective-permute-start | bytes 491528 | tf_op jit(solution)/shard_map/ppermute | solution.py:47
  46.0 11.4 %collective-permute-start.9 = (f32[448,128]{1,0:T(8,128)S(1)}, f32[448,128]{1,0:T(8,128)S(1)}, u32[]{:S(2)}, u32[]{:S(2)}) collective-permute-start(f32[448,128]{1,0:T(8,128)S(1)} %add.107), channel_id=1, source_target_pairs={{0,32},{1,33},{2,34},{3,35},{4,36},{5,37},{6,38},{7,39},{8,40},{9,... | collective-permute-start | bytes 688136 | tf_op jit(solution)/shard_map/ppermute | solution.py:47
  46.9 10.2 %collective-permute-start.11 = (f32[224,128]{1,0:T(8,128)S(1)}, f32[224,128]{1,0:T(8,128)S(1)}, u32[]{:S(2)}, u32[]{:S(2)}) collective-permute-start(f32[224,128]{1,0:T(8,128)S(1)} %fusion.1), channel_id=1, source_target_pairs={{0,4},{1,5},{2,6},{3,7},{4,0},{5,1},{6,2},{7,3},{8,12},{9,13},{10,... | collective-permute-start | bytes 344072 | tf_op jit(solution)/shard_map/ppermute | solution.py:47
  49.9 16.2 %collective-permute-start.26 = (f32[648,128]{1,0:T(8,128)S(1)}, f32[648,128]{1,0:T(8,128)S(1)}, u32[]{:S(2)}, u32[]{:S(2)}) collective-permute-start(f32[648,128]{1,0:T(8,128)S(1)} %add.117.refs_0_), channel_id=1, source_target_pairs={{0,16},{1,17},{2,18},{3,19},{4,20},{5,21},{6,22},{7,23},{8,24},{9,... | collective-permute-start | bytes 995336 | tf_op jit(solution)/shard_map/ppermute | solution.py:47
  57.4 8.4 %collective-permute-start.13 = (f32[448,128]{1,0:T(8,128)S(1)}, f32[448,128]{1,0:T(8,128)S(1)}, u32[]{:S(2)}, u32[]{:S(2)}) collective-permute-start(f32[448,128]{1,0:T(8,128)S(1)} %add.108.refs_0_), channel_id=1, source_target_pairs={{0,4},{1,5},{2,6},{3,7},{4,0},{5,1},{6,2},{7,3},{8,12},{9,13},{10,... | collective-permute-start | bytes 688136 | tf_op jit(solution)/shard_map/ppermute | solution.py:47
  61.3 11.7 %collective-permute-start.16 = (f32[224,128]{1,0:T(8,128)S(1)}, f32[224,128]{1,0:T(8,128)S(1)}, u32[]{:S(2)}, u32[]{:S(2)}) collective-permute-start(f32[224,128]{1,0:T(8,128)S(1)} %add.113.refs_1_), channel_id=1, source_target_pairs={{0,16},{1,17},{2,18},{3,19},{4,20},{5,21},{6,22},{7,23},{8,24},{9,... | collective-permute-start | bytes 344072 | tf_op jit(solution)/shard_map/ppermute | solution.py:47
  65.3 7.7 %collective-permute-start.18 = (f32[224,128]{1,0:T(8,128)S(1)}, f32[224,128]{1,0:T(8,128)S(1)}, u32[]{:S(2)}, u32[]{:S(2)}) collective-permute-start(f32[224,128]{1,0:T(8,128)S(1)} %collective-permute-done.14.refs_3_), channel_id=1, source_target_pairs={{0,16},{1,17},{2,18},{3,19},{4,20},{5,21},{6,22},{7,23},{8,24},{9,... | collective-permute-start | bytes 344072 | tf_op jit(solution)/shard_map/ppermute | solution.py:47
  65.6 7.5 %collective-permute-start.15 = (f32[448,128]{1,0:T(8,128)S(1)}, f32[448,128]{1,0:T(8,128)S(1)}, u32[]{:S(2)}, u32[]{:S(2)}) collective-permute-start(f32[448,128]{1,0:T(8,128)S(1)} %add.108.refs_0_), channel_id=1, source_target_pairs={{0,16},{1,17},{2,18},{3,19},{4,20},{5,21},{6,22},{7,23},{8,24},{9,... | collective-permute-start | bytes 688136 | tf_op jit(solution)/shard_map/ppermute | solution.py:47
  65.9 7.2 %collective-permute-start.17 = (f32[448,128]{1,0:T(8,128)S(1)}, f32[448,128]{1,0:T(8,128)S(1)}, u32[]{:S(2)}, u32[]{:S(2)}) collective-permute-start(f32[448,128]{1,0:T(8,128)S(1)} %collective-permute-done.13.refs_2_), channel_id=1, source_target_pairs={{0,16},{1,17},{2,18},{3,19},{4,20},{5,21},{6,22},{7,23},{8,24},{9,... | collective-permute-start | bytes 688136 | tf_op jit(solution)/shard_map/ppermute | solution.py:47
  92.3 10.4 %collective-permute-start.28 = (f32[64,1024]{1,0:T(8,128)S(1)}, f32[64,1024]{1,0:T(8,128)S(1)}, u32[]{:S(2)}, u32[]{:S(2)}) collective-permute-start(f32[64,1024]{1,0:T(8,128)S(1)} %get-tuple-element.45), channel_id=1, source_target_pairs={{0,111},{1,110},{2,109},{3,108},{4,107},{5,106},{6,105},{7,104},{8... | collective-permute-start | bytes 786440 | tf_op jit(solution)/shard_map/ppermute | solution.py:47
  95.3 13.2 %collective-permute-start.29 = (f32[64,1024]{1,0:T(8,128)S(1)}, f32[64,1024]{1,0:T(8,128)S(1)}, u32[]{:S(2)}, u32[]{:S(2)}) collective-permute-start(f32[64,1024]{1,0:T(8,128)S(1)} %get-tuple-element.46), channel_id=1, source_target_pairs={{0,0},{1,1},{2,2},{3,3},{4,4},{5,5},{6,6},{7,7},{8,8},{9,9},{10,10... | collective-permute-start | bytes 786440 | tf_op jit(solution)/shard_map/ppermute | solution.py:47
  101.5 9.4 %collective-permute-start.30 = (f32[64,1024]{1,0:T(8,128)S(1)}, f32[64,1024]{1,0:T(8,128)S(1)}, u32[]{:S(2)}, u32[]{:S(2)}) collective-permute-start(f32[64,1024]{1,0:T(8,128)S(1)} %get-tuple-element.47), channel_id=1, source_target_pairs={{0,12},{1,13},{2,14},{3,15},{4,8},{5,9},{6,10},{7,11},{8,4},{9,5},... | collective-permute-start | bytes 786440 | tf_op jit(solution)/shard_map/ppermute | solution.py:47
  101.6 9.3 %collective-permute-start.31 = (f32[64,1024]{1,0:T(8,128)S(1)}, f32[64,1024]{1,0:T(8,128)S(1)}, u32[]{:S(2)}, u32[]{:S(2)}) collective-permute-start(f32[64,1024]{1,0:T(8,128)S(1)} %get-tuple-element.48), channel_id=1, source_target_pairs={{0,3},{1,2},{2,1},{3,0},{4,7},{5,6},{6,5},{7,4},{8,11},{9,10},{10,... | collective-permute-start | bytes 786440 | tf_op jit(solution)/shard_map/ppermute | solution.py:47
  102.7 8.6 %collective-permute-start.32 = (f32[64,1024]{1,0:T(8,128)S(1)}, f32[64,1024]{1,0:T(8,128)S(1)}, u32[]{:S(2)}, u32[]{:S(2)}) collective-permute-start(f32[64,1024]{1,0:T(8,128)S(1)} %collective-permute-done.28.refs_0_), channel_id=1, source_target_pairs={{0,16},{1,17},{2,18},{3,19},{4,20},{5,21},{6,22},{7,23},{8,24},{9,... | collective-permute-start | bytes 786440 | tf_op jit(solution)/shard_map/ppermute | solution.py:47
  (13 other events, 44.6 us)
